TPU v7x, 128 devices: a whole 4x4x4 slice. The times are simulated.
128 devices in a mesh: rows: 32 (over x, z, core), lev: 4 (over y).
Axes of the slice: x: 4, y: 4, z: 4, core: 2. Of those that a mesh axis runs over, the one named last changes fastest.
Arguments:
- source: float32 [2048, 16, 2048], P('rows', 'lev'), may hold values from -40 to 40
- solid: int32 [256, 16, 32], P('rows', 'lev'), may hold values 0 or 1
- couplings: float32 [17], replicated, may hold values from 2 to 8
Outputs:
- pressure: float32 [2048, 16, 2048], P('rows', 'lev')
Inputs may be any that keep to these rules, and one draw needn't show every extreme that they name: Each entry is 0 or 1; 1 marks a block of 8 x 64 cells of one level inside a solid.
All inputs are finite; a program needn't handle non-finite values.
Results may differ from a plain program's by a relative error of at most 0.0001.
Values sent between devices are 32-bit elements; how exact they have to be, the bound alone decides.
No kernel may reach another device: no remote copies, remote signals or barrier semaphores. Data moves between devices by JAX's collectives and lax.ppermute only.
A program may use at most 128 MiB of HBM per device.

v0:
```python
import math

import jax
import jax.numpy as jnp
from jax import lax
from jax.sharding import PartitionSpec as P

BY = 8
BX = 64


full_turn = 2.0 * math.pi
highest = lax.Precision.HIGHEST


def shifted(value, axis, steps):
    count = lax.axis_size(axis)
    first, last = (max(0, -steps), min(count, count - steps))
    return lax.ppermute(value, axis, [(source, source + steps) for source in range(first, last)])


def product(form, left, right):
    return jnp.einsum(form, left, right, precision=highest, preferred_element_type=jnp.float32)


def tables(length):
    fine_size = 32
    coarse_size = length // fine_size
    coarse = jnp.arange(coarse_size, dtype=jnp.int32)
    fine = jnp.arange(fine_size, dtype=jnp.int32)
    angle_first = jnp.mod(coarse[:, None] * coarse[None, :], coarse_size).astype(jnp.float32) * (
        full_turn / coarse_size
    )
    first_table = jnp.concatenate([jnp.cos(angle_first), jnp.sin(angle_first)], 0)
    upper_rows = jnp.arange(fine_size // 2, dtype=jnp.int32)
    angle_last = jnp.mod(upper_rows[:, None] * fine[None, :], fine_size).astype(jnp.float32) * (
        full_turn / fine_size
    )
    cos_table = jnp.cos(angle_last)
    sin_table = jnp.sin(angle_last)
    angle_twist = jnp.mod(coarse[:, None] * fine[None, :], length).astype(jnp.float32) * (
        full_turn / length
    )
    twist_cos = jnp.cos(angle_twist)[:, :, None]
    twist_sin = jnp.sin(angle_twist)[:, :, None]
    alternating = (1 - 2 * jnp.mod(fine, 2)).astype(jnp.float32)
    nyquist_row = jnp.where(coarse[:, None] == 0, alternating[None, :], 0.0)[:, :, None]
    slots = jnp.arange(length, dtype=jnp.int32)
    edge = (slots == 0) | (slots == length // 2)
    weights = jnp.where(edge, math.sqrt(1.0 / length), math.sqrt(2.0 / length)).astype(jnp.float32)
    return (
        fine_size,
        coarse_size,
        first_table,
        cos_table,
        sin_table,
        twist_cos,
        twist_sin,
        alternating,
        nyquist_row,
        weights,
    )


def finish(segment_one, lookup):
    (
        fine_size,
        coarse_size,
        first_table,
        cos_table,
        sin_table,
        twist_cos,
        twist_sin,
        alternating,
        nyquist_row,
        weights,
    ) = lookup
    batch_size = segment_one.shape[2]
    real_first = segment_one[:coarse_size]
    imag_first = -segment_one[coarse_size:]
    nyquist = jnp.sum(real_first[0] * alternating[:, None], axis=0)
    real_twisted = real_first * twist_cos + imag_first * twist_sin
    imag_twisted = imag_first * twist_cos - real_first * twist_sin
    real_final = (
        product("fjb,gj->bgf", real_twisted, cos_table)
        + product("fjb,gj->bgf", imag_twisted, sin_table)
    ).reshape(batch_size, -1)
    imag_final = (
        product("fjb,gj->bgf", imag_twisted, cos_table)
        - product("fjb,gj->bgf", real_twisted, sin_table)
    ).reshape(batch_size, -1)
    leading = jnp.arange(real_final.shape[1]) == 0
    sine_half = jnp.where(leading[None, :], nyquist[:, None], -imag_final)
    return jnp.concatenate([real_final, sine_half], 1) * weights


def unfinish(packed, lookup):
    (
        fine_size,
        coarse_size,
        first_table,
        cos_table,
        sin_table,
        twist_cos,
        twist_sin,
        alternating,
        nyquist_row,
        weights,
    ) = lookup
    batch_size, length = packed.shape
    half_len = length // 2
    half_fine = fine_size // 2
    scaled = packed * weights
    cosine_half = scaled[:, :half_len]
    sine_half = scaled[:, half_len:]
    leading = jnp.arange(half_len) == 0
    back_real = cosine_half.reshape(batch_size, half_fine, coarse_size)
    back_imag = jnp.where(leading[None, :], 0.0, -sine_half).reshape(
        batch_size, half_fine, coarse_size
    )
    back_nyquist = sine_half[:, 0]
    twisted_real = product("bgf,gj->fjb", back_real, cos_table) - product(
        "bgf,gj->fjb", back_imag, sin_table
    )
    twisted_imag = product("bgf,gj->fjb", back_imag, cos_table) + product(
        "bgf,gj->fjb", back_real, sin_table
    )
    real_first = (
        twisted_real * twist_cos
        - twisted_imag * twist_sin
        + back_nyquist[None, None, :] * nyquist_row
    )
    imag_first = twisted_real * twist_sin + twisted_imag * twist_cos
    return jnp.concatenate([real_first, -imag_first], 0)


def forward_last(values, lookup):
    batch_size = values.shape[0]
    segment_one = product(
        "bkj,fk->fjb", values.reshape(batch_size, lookup[1], lookup[0]), lookup[2]
    )
    return finish(segment_one, lookup)


def inverse_last(packed, lookup):
    return product("fjb,fk->bkj", unfinish(packed, lookup), lookup[2]).reshape(packed.shape)


def forward_lead(pencil, lookup):
    length, levels, slab_width = pencil.shape
    segment_one = product(
        "kjr,fk->fjr", pencil.reshape(lookup[1], lookup[0], levels * slab_width), lookup[2]
    )
    return finish(segment_one, lookup).reshape(levels, slab_width, length)


def inverse_lead(packed, lookup):
    levels, slab_width, length = packed.shape
    segments = unfinish(packed.reshape(levels * slab_width, length), lookup)
    return product("fjr,fk->kjr", segments, lookup[2]).reshape(length, levels, slab_width)


def eigenvalue(slots, length):
    frequency = jnp.where(slots <= length // 2, slots, slots - length // 2)
    return 2.0 - 2.0 * jnp.cos(frequency.astype(jnp.float32) * (full_turn / length))


def section_solve(horizontal, part_couplings, spectrum):
    level_count = part_couplings.shape[0] - 1
    level_index = jnp.arange(level_count, dtype=jnp.int32)
    at_bottom = (level_index == 0).astype(jnp.float32)
    at_top = (level_index == level_count - 1).astype(jnp.float32)
    zero_plane = jnp.zeros(horizontal.shape, jnp.float32)
    has_source = spectrum is not None
    system_count = int(has_source) + 2 * int(True)

    def forward(carry, slices):
        pivot_ratio, partial_value = carry
        lower_w, upper_w, bottom_flag, top_flag, source_level = slices
        inverse = 1.0 / (horizontal + lower_w + upper_w - lower_w * pivot_ratio)
        updated = []
        updated.append((source_level + lower_w * partial_value[0]) * inverse)
        shift_pos = len(updated)
        updated.append(lower_w * (bottom_flag + partial_value[shift_pos]) * inverse)
        updated.append((upper_w * top_flag + lower_w * partial_value[shift_pos + 1]) * inverse)
        ratio = upper_w * inverse
        return ((ratio, tuple(updated)), (ratio, tuple(updated)))

    sweep_in = (part_couplings[:-1], part_couplings[1:], at_bottom, at_top, spectrum)
    unused, (ratios, partials) = lax.scan(
        forward, (zero_plane, (zero_plane,) * system_count), sweep_in
    )

    def backward(upper_values, slices):
        ratio, partial_value = slices
        current = tuple(
            (value + ratio * above for value, above in zip(partial_value, upper_values))
        )
        return (current, current)

    unused, solutions = lax.scan(
        backward, (zero_plane,) * system_count, (ratios, partials), reverse=True
    )
    return solutions


def chain_ends(particular, lower_part, upper_part, lev_devices):
    first_u = particular[0]
    top_u = particular[-1]
    first_a = lower_part[0]
    top_a = lower_part[-1]
    first_b = upper_part[0]
    top_b = upper_part[-1]

    def relation(incoming):
        offset_in = incoming[0]
        factor_in = incoming[1]
        scale_inv = 1.0 / (1.0 - first_a * factor_in)
        first_offset = (first_u + first_a * offset_in) * scale_inv
        first_factor = first_b * scale_inv
        offset_out = top_u + top_a * (offset_in + factor_in * first_offset)
        factor_out = top_a * factor_in * first_factor + top_b
        return (first_offset, first_factor, jnp.stack([offset_out, factor_out]))

    incoming = jnp.zeros((2,) + first_u.shape, jnp.float32)
    for round_index in range(lev_devices - 1):
        outgoing = relation(incoming)[2]
        incoming = shifted(outgoing, "lev", 1)
    first_offset, first_factor, unused = relation(incoming)
    above_value = jnp.zeros_like(first_u)
    for round_index in range(lev_devices - 1):
        above_value = shifted(first_offset + first_factor * above_value, "lev", -1)
    first_value = first_offset + first_factor * above_value
    below_value = incoming[0] + incoming[1] * first_value
    return (below_value, above_value)


def body(source, solid, couplings):
    row_count, level_count, cell_count = source.shape
    keep_cells = (1 - solid).astype(jnp.float32)
    masked_cells = (
        source.reshape(row_count // BY, BY, level_count, cell_count // BX, BX)
        * keep_cells[:, None, :, :, None]
    ).reshape(row_count * level_count, cell_count)
    lookup_x = tables(cell_count)
    spectral = forward_last(masked_cells, lookup_x).reshape(row_count, level_count, cell_count)
    row_devices = lax.axis_size("rows")
    lev_devices = lax.axis_size("lev")
    total_rows = row_count * row_devices
    lookup_y = tables(total_rows)
    row_eigen = eigenvalue(jnp.arange(total_rows, dtype=jnp.int32), total_rows)
    spectrum = forward_lead(
        lax.all_to_all(spectral, "rows", split_axis=2, concat_axis=0, tiled=True), lookup_y
    )
    slab_width = cell_count // row_devices
    slots = lax.axis_index("rows") * slab_width + jnp.arange(slab_width, dtype=jnp.int32)
    horizontal = eigenvalue(slots, cell_count)[:, None] + row_eigen[None, :]
    own_section = lax.axis_index("lev")
    local_couplings = lax.dynamic_slice_in_dim(
        couplings, own_section * level_count, level_count + 1
    )
    particular, lower_part, upper_part = section_solve(horizontal, local_couplings, spectrum)
    below_value, above_value = chain_ends(particular, lower_part, upper_part, lev_devices)
    pressure_spectrum = particular + lower_part * below_value + upper_part * above_value
    physical = inverse_lead(pressure_spectrum, lookup_y)
    pencil = lax.all_to_all(physical, "rows", split_axis=0, concat_axis=2, tiled=True)
    rows_here, levels_here, cells_here = pencil.shape
    return inverse_last(pencil.reshape(rows_here * levels_here, cells_here), lookup_x).reshape(
        pencil.shape
    )


def solution(mesh):
    return jax.shard_map(
        body,
        mesh=mesh,
        in_specs=(P("rows", "lev", None), P("rows", "lev", None), P()),
        out_specs=P("rows", "lev", None),
        check_vma=False,
    )
```

profile of v0, /device:TPU:1, one launch (start us, length us, event | category | flops | bytes accessed | tf_op | source)
XLA Modules:
  0.0 468.6 jit_solution(3819985442750889139)
XLA Ops:
  0.3 6.7 %reshape.209 = f32[256,64,32]{2,1,0:T(8,128)} reshape(f32[64,4,2048]{2,1,0:T(4,128)} %param.7) | data formatting | bytes 4194304 | tf_op jit(solution)/shard_map/reshape | solution.py:242
  9.2 7.9 %broadcast_multiply_fusion.1 = f32[256,64,32]{2,1,0:T(8,128)} fusion(f32[256,64,32]{2,1,0:T(8,128)} %reshape.209, f32[256,64]{1,0:T(8,128)S(1)} %copy.191), kind=kLoop, calls=%fused_computation.38 | loop fusion | flops 524288 | bytes 4259840 | tf_op jit(solution)/shard_map/mul | solution.py:242
  17.1 7.0 %copy.192 = f32[256,64,32]{0,1,2:T(8,128)S(1)} copy(f32[256,64,32]{2,1,0:T(8,128)} %broadcast_multiply_fusion.1) | data formatting | bytes 4194304 | tf_op jit(solution)/shard_map/mul | solution.py:242
  42.4 4.5 fusion.51
  57.2 6.3 %reshape.223 = f32[32,1,16384]{2,1,0:T(1,128)} reshape(f32[2048,4,64]{2,1,0:T(4,128)} %bitcast.219) | data formatting | bytes 4194304
  63.5 9.8 %all-to-all-start = ((f32[32,1,16384]{2,1,0:T(1,128)}), f32[32,1,16384]{2,1,0:T(1,128)S(1)}, u32[]{:S(2)}, u32[]{:S(2)}) async-start(f32[32,1,16384]{2,1,0:T(1,128)} %reshape.223), calls=%async_computation | async-start | bytes 4194304 | tf_op jit(solution)/shard_map/all_to_all | solution.py:253
  73.7 27.8 %all-to-all-done = f32[32,1,16384]{2,1,0:T(1,128)S(1)} async-done(((f32[32,1,16384]{2,1,0:T(1,128)}), f32[32,1,16384]{2,1,0:T(1,128)S(1)}, u32[]{:S(2)}, u32[]{:S(2)}) %all-to-all-start) | async-done | bytes 2097184 | tf_op jit(solution)/shard_map/all_to_all | solution.py:253
  103.4 7.4 %reduce.4 = f32[32,16384]{1,0:T(8,128)S(1)} reduce(f32[32,1,16384]{2,1,0:T(1,128)} %copy-done.10, f32[]{:T(128)} %broadcast.598), dimensions={1}, to_apply=%all_to_all.22.reduce_sub_computation | reduce | bytes 4194308 | tf_op jit(solution)/shard_map/all_to_all | solution.py:253
  115.0 6.4 %copy.203 = f32[64,4,32,64]{3,1,0,2:T(4,128)} copy(f32[64,4,32,64]{0,1,3,2:T(4,128)} %bitcast.220) | data formatting | bytes 4194304 | tf_op jit(solution)/shard_map/all_to_all | solution.py:253
  125.6 4.7 fusion.27
  147.3 4.5 fusion.66
  165.5 33.2 %while.50 = (s32[]{:T(128)}, f32[64,2048]{1,0:T(8,128)S(1)}, f32[64,2048]{1,0:T(8,128)S(1)}, f32[64,2048]{1,0:T(8,128)S(1)}, f32[64,2048]{1,0:T(8,128)S(1)}, /*i...) while((s32[]{:T(128)}, f32[64,2048]{1,0:T(8,128)S(1)}, ...), condition=%wide.region_3.4_spmd.clone, body=%wide.region_2.3_spmd.clone.sunk | while | flops 2621444 | bytes 6826479 | solution.py:190
  169.0 4.7 %bitcast_dynamic-update-slice_fusion.9 = (f32[4,64,2048]{2,1,0:T(8,128)}, f32[64,2048]{1,0:T(8,128)S(1)}, f32[4,64,2048]{2,1,0:T(8,128)}, f32[64,2048]{1,0:T(8,1...) fusion(f32[4,64,2048]{2,1,0:T(8,128)} %get-tuple-element.727, ...), kind=kLoop, calls=%fused_computation.1.clone.1 | loop fusion | flops 2621440 | bytes 6826245 | tf_op jit(solution)/shard_map/while/body/jit(dynamic_update_index_in_dim)/dynamic_update_slice | solution.py:190
  177.3 4.7 %bitcast_dynamic-update-slice_fusion.9 = (f32[4,64,2048]{2,1,0:T(8,128)}, f32[64,2048]{1,0:T(8,128)S(1)}, f32[4,64,2048]{2,1,0:T(8,128)}, f32[64,2048]{1,0:T(8,1...) fusion(f32[4,64,2048]{2,1,0:T(8,128)} %get-tuple-element.727, ...), kind=kLoop, calls=%fused_computation.1.clone.1 | loop fusion | flops 2621440 | bytes 6826245 | tf_op jit(solution)/shard_map/while/body/jit(dynamic_update_index_in_dim)/dynamic_update_slice | solution.py:190
  185.6 4.7 %bitcast_dynamic-update-slice_fusion.9 = (f32[4,64,2048]{2,1,0:T(8,128)}, f32[64,2048]{1,0:T(8,128)S(1)}, f32[4,64,2048]{2,1,0:T(8,128)}, f32[64,2048]{1,0:T(8,1...) fusion(f32[4,64,2048]{2,1,0:T(8,128)} %get-tuple-element.727, ...), kind=kLoop, calls=%fused_computation.1.clone.1 | loop fusion | flops 2621440 | bytes 6826245 | tf_op jit(solution)/shard_map/while/body/jit(dynamic_update_index_in_dim)/dynamic_update_slice | solution.py:190
  193.8 4.8 %bitcast_dynamic-update-slice_fusion.9 = (f32[4,64,2048]{2,1,0:T(8,128)}, f32[64,2048]{1,0:T(8,128)S(1)}, f32[4,64,2048]{2,1,0:T(8,128)}, f32[64,2048]{1,0:T(8,1...) fusion(f32[4,64,2048]{2,1,0:T(8,128)} %get-tuple-element.727, ...), kind=kLoop, calls=%fused_computation.1.clone.1 | loop fusion | flops 2621440 | bytes 6826245 | tf_op jit(solution)/shard_map/while/body/jit(dynamic_update_index_in_dim)/dynamic_update_slice | solution.py:190
  202.1 11.8 %while.51 = (s32[]{:T(128)}, f32[64,2048]{1,0:T(8,128)S(1)}, f32[64,2048]{1,0:T(8,128)S(1)}, f32[64,2048]{1,0:T(8,128)}, f32[4,64,2048]{2,1,0:T(8,128)S(1)}, /*i...) while((s32[]{:T(128)}, f32[64,2048]{1,0:T(8,128)S(1)}, ...), condition=%wide.region_5.6_spmd.clone, body=%wide.region_4.5_spmd.clone.sunk | while | flops 1179652 | bytes 6815903 | solution.py:201
  219.3 21.6 %collective-permute-done = f32[2,64,2048]{2,1,0:T(8,128)S(1)} collective-permute-done((f32[2,64,2048]{2,1,0:T(8,128)S(1)}, f32[2,64,2048]{2,1,0:T(8,128)S(1)}, u32[]{:S(2)}, u32[]{:S(2)}) %collective-permute-start) | collective-permute-done | bytes 1048608 | tf_op jit(solution)/shard_map/ppermute | solution.py:19
  245.6 20.7 %collective-permute-done.1 = f32[2,64,2048]{2,1,0:T(8,128)S(1)} collective-permute-done((f32[2,64,2048]{2,1,0:T(8,128)S(1)}, f32[2,64,2048]{2,1,0:T(8,128)S(1)}, u32[]{:S(2)}, u32[]{:S(2)}) %collective-permute-start.1) | collective-permute-done | bytes 1048608 | tf_op jit(solution)/shard_map/ppermute | solution.py:19
  271.0 19.9 %collective-permute-done.2 = f32[2,64,2048]{2,1,0:T(8,128)S(1)} collective-permute-done((f32[2,64,2048]{2,1,0:T(8,128)S(1)}, f32[2,64,2048]{2,1,0:T(8,128)S(1)}, u32[]{:S(2)}, u32[]{:S(2)}) %collective-permute-start.2) | collective-permute-done | bytes 1048608 | tf_op jit(solution)/shard_map/ppermute | solution.py:19
  292.4 11.7 %collective-permute-done.3 = f32[64,2048]{1,0:T(8,128)S(1)} collective-permute-done((f32[64,2048]{1,0:T(8,128)S(1)}, f32[64,2048]{1,0:T(8,128)S(1)}, u32[]{:S(2)}, u32[]{:S(2)}) %collective-permute-start.3) | collective-permute-done | bytes 524320 | tf_op jit(solution)/shard_map/ppermute | solution.py:19
  305.5 10.1 %collective-permute-done.4 = f32[64,2048]{1,0:T(8,128)S(1)} collective-permute-done((f32[64,2048]{1,0:T(8,128)S(1)}, f32[64,2048]{1,0:T(8,128)S(1)}, u32[]{:S(2)}, u32[]{:S(2)}) %collective-permute-start.4) | collective-permute-done | bytes 524320 | tf_op jit(solution)/shard_map/ppermute | solution.py:19
  317.3 9.0 %collective-permute-done.5 = f32[64,2048]{1,0:T(8,128)S(1)} collective-permute-done((f32[64,2048]{1,0:T(8,128)S(1)}, f32[64,2048]{1,0:T(8,128)S(1)}, u32[]{:S(2)}, u32[]{:S(2)}) %collective-permute-start.5) | collective-permute-done | bytes 524320 | tf_op jit(solution)/shard_map/ppermute | solution.py:19
  343.8 5.1 %fusion.24 = (f32[64,32,256]{2,0,1:T(8,128)S(1)}, f32[64,32,256]{2,0,1:T(8,128)S(1)}) fusion(f32[64,32]{0,1:T(8,128)S(1)} %broadcast_select_fusion.1, f32[256]{0:T(256)S(1)} %slice_reduce_fusion.1, f32[64,32]{0,1:T(8,128)S(1)} %get-tuple-element.505, f32[64,32]{0,1:T(8,128)S(1)} %get-tuple-element.506, f32[32,256,64]{1,0,2:T(8,128)S(1)} %copy-done.9, ...), kind=kLoop, calls=%fused_computation.55 | loop fusion | flops 5767168 | bytes 12608512 | tf_op jit(solution)/shard_map/add | solution.py:129
  355.5 5.3 %reshape.225 = f32[32,1,16384]{2,1,0:T(1,128)S(1)} reshape(f32[2048,4,64]{2,1,0:T(4,128)} %reshape.214) | data formatting | bytes 4194304
  360.9 43.3 %all_to_all.30 = f32[32,1,16384]{2,1,0:T(1,128)} all-to-all(f32[32,1,16384]{2,1,0:T(1,128)S(1)} %reshape.225), channel_id=1, replica_groups=mesh['rows'=32,'lev'=4] {'rows'}, dimensions={0} | all-to-all | bytes 4194304 | tf_op jit(solution)/shard_map/all_to_all | solution.py:266
  404.1 7.4 %reduce.5 = f32[32,16384]{1,0:T(8,128)S(1)} reduce(f32[32,1,16384]{2,1,0:T(1,128)} %all_to_all.30, f32[]{:T(128)} %broadcast.598), dimensions={1}, to_apply=%all_to_all.25.reduce_sub_computation | reduce | bytes 4194308 | tf_op jit(solution)/shard_map/all_to_all | solution.py:266
  415.8 6.6 %copy.342 = f32[32,64,4,64]{3,0,2,1:T(8,128)} copy(f32[32,64,4,64]{3,2,1,0:T(4,128)} %bitcast.222) | data formatting | bytes 4194304 | tf_op jit(solution)/shard_map/all_to_all | solution.py:266
  422.4 5.1 %reshape.215 = f32[256,2048]{1,0:T(8,128)} reshape(f32[64,4,32,64]{3,2,1,0:T(8,128)} %bitcast.223) | data formatting | bytes 4194304 | tf_op jit(solution)/shard_map/reshape | solution.py:268
  445.7 5.1 %fusion.20 = (f32[64,32,256]{2,0,1:T(8,128)S(1)}, f32[64,32,256]{2,0,1:T(8,128)S(1)}) fusion(f32[256]{0:T(256)S(1)} %slice_reduce_fusion, f32[64,32]{0,1:T(8,128)S(1)} %broadcast_select_fusion.1, f32[64,32]{0,1:T(8,128)S(1)} %get-tuple-element.505, f32[64,32]{0,1:T(8,128)S(1)} %get-tuple-element.506, f32[32,256,64]{1,0,2:T(8,128)S(1)} %copy-done.7, ...), kind=kLoop, calls=%fused_computation.47 | loop fusion | flops 5767168 | bytes 12608512 | tf_op jit(solution)/shard_map/add | solution.py:129
  453.0 7.6 %copy.235 = f32[256,64,32]{2,1,0:T(8,128)} copy(f32[256,64,32]{0,1,2:T(8,128)S(1)} %fusion.45) | data formatting | bytes 4194304 | tf_op jit(solution)/shard_map/fjb,fk->bkj/transpose | solution.py:23
  460.6 7.8 %reshape_reshape.4 = f32[64,4,2048]{2,1,0:T(4,128)} reshape(f32[256,64,32]{2,1,0:T(8,128)} %copy.235) | data formatting | bytes 4194304 | tf_op jit(solution)/shard_map/reshape;reshape | solution.py:268
  (153 shorter events, 164.7 us)
Async XLA Ops:
  0.3 6.7 %copy-start.12 = (s32[8,4,32]{2,1,0:T(4,128)S(1)}, s32[8,4,32]{2,1,0:T(4,128)}, u32[]{:S(2)}) copy-start(s32[8,4,32]{2,1,0:T(4,128)} %param.8) | copy-start | bytes 12292
  63.5 9.9 %copy-start.13 = (f32[17]{0:T(128)S(1)}, f32[17]{0:T(128)}, u32[]{:S(2)}) copy-start(f32[17]{0:T(128)} %param.9) | copy-start | bytes 208
  63.5 38.0 %all-to-all-start = ((f32[32,1,16384]{2,1,0:T(1,128)}), f32[32,1,16384]{2,1,0:T(1,128)S(1)}, u32[]{:S(2)}, u32[]{:S(2)}) async-start(f32[32,1,16384]{2,1,0:T(1,128)} %reshape.223), calls=%async_computation | async-start | bytes 4194304 | tf_op jit(solution)/shard_map/all_to_all | solution.py:253
  101.6 1.3 copy-start.10
  156.0 1.5 copy-start.11
  162.2 3.2 copy-start.2
  162.2 3.2 copy-start.3
  162.2 3.2 copy-start.4
  162.2 3.2 copy-start.5
  213.9 27.0 %copy-start.1 = (f32[4,64,2048]{2,1,0:T(8,128)S(1)}, f32[4,64,2048]{2,1,0:T(8,128)}, u32[]{:S(2)}) copy-start(f32[4,64,2048]{2,1,0:T(8,128)} %get-tuple-element.310) | copy-start | bytes 6291460
  215.8 25.1 %copy-start = (f32[4,64,2048]{2,1,0:T(8,128)S(1)}, f32[4,64,2048]{2,1,0:T(8,128)}, u32[]{:S(2)}) copy-start(f32[4,64,2048]{2,1,0:T(8,128)} %get-tuple-element.309) | copy-start | bytes 6291460
  215.9 25.0 %collective-permute-start = (f32[2,64,2048]{2,1,0:T(8,128)S(1)}, f32[2,64,2048]{2,1,0:T(8,128)S(1)}, u32[]{:S(2)}, u32[]{:S(2)}) collective-permute-start(f32[2,64,2048]{2,1,0:T(8,128)S(1)} %pad_maximum_fusion), channel_id=1, source_target_pairs={{0,1},{1,2},{2,3},{4,5},{5,6},{6,7},{8,9},{9,10},{10,11},{12,13},{... | collective-permute-start | bytes 3145736 | tf_op jit(solution)/shard_map/ppermute | solution.py:19
  241.4 24.9 %collective-permute-start.1 = (f32[2,64,2048]{2,1,0:T(8,128)S(1)}, f32[2,64,2048]{2,1,0:T(8,128)S(1)}, u32[]{:S(2)}, u32[]{:S(2)}) collective-permute-start(f32[2,64,2048]{2,1,0:T(8,128)S(1)} %pad_maximum_fusion.1), channel_id=1, source_target_pairs={{0,1},{1,2},{2,3},{4,5},{5,6},{6,7},{8,9},{9,10},{10,11},{12,13},{... | collective-permute-start | bytes 3145736 | tf_op jit(solution)/shard_map/ppermute | solution.py:19
  266.8 24.1 %collective-permute-start.2 = (f32[2,64,2048]{2,1,0:T(8,128)S(1)}, f32[2,64,2048]{2,1,0:T(8,128)S(1)}, u32[]{:S(2)}, u32[]{:S(2)}) collective-permute-start(f32[2,64,2048]{2,1,0:T(8,128)S(1)} %pad_maximum_fusion.2), channel_id=1, source_target_pairs={{0,1},{1,2},{2,3},{4,5},{5,6},{6,7},{8,9},{9,10},{10,11},{12,13},{... | collective-permute-start | bytes 3145736 | tf_op jit(solution)/shard_map/ppermute | solution.py:19
  291.1 13.0 %collective-permute-start.3 = (f32[64,2048]{1,0:T(8,128)S(1)}, f32[64,2048]{1,0:T(8,128)S(1)}, u32[]{:S(2)}, u32[]{:S(2)}) collective-permute-start(f32[64,2048]{1,0:T(8,128)S(1)} %get-tuple-element.470), channel_id=1, source_target_pairs={{1,0},{2,1},{3,2},{5,4},{6,5},{7,6},{9,8},{10,9},{11,10},{13,12},{... | collective-permute-start | bytes 1572872 | tf_op jit(solution)/shard_map/ppermute | solution.py:19
  304.2 11.4 %collective-permute-start.4 = (f32[64,2048]{1,0:T(8,128)S(1)}, f32[64,2048]{1,0:T(8,128)S(1)}, u32[]{:S(2)}, u32[]{:S(2)}) collective-permute-start(f32[64,2048]{1,0:T(8,128)S(1)} %multiply_add_fusion.5), channel_id=1, source_target_pairs={{1,0},{2,1},{3,2},{5,4},{6,5},{7,6},{9,8},{10,9},{11,10},{13,12},{... | collective-permute-start | bytes 1572872 | tf_op jit(solution)/shard_map/ppermute | solution.py:19
  315.7 10.5 %collective-permute-start.5 = (f32[64,2048]{1,0:T(8,128)S(1)}, f32[64,2048]{1,0:T(8,128)S(1)}, u32[]{:S(2)}, u32[]{:S(2)}) collective-permute-start(f32[64,2048]{1,0:T(8,128)S(1)} %multiply_add_fusion.4), channel_id=1, source_target_pairs={{1,0},{2,1},{3,2},{5,4},{6,5},{7,6},{9,8},{10,9},{11,10},{13,12},{... | collective-permute-start | bytes 1572872 | tf_op jit(solution)/shard_map/ppermute | solution.py:19
  339.2 4.6 copy-start.9
  341.5 2.4 copy-start.8
  441.0 4.6 copy-start.7
  443.3 2.4 copy-start.6
where the time goes:
time: 477 us; the launch traced here: 469 us
  local copies, waits for them, and re-layouts  132 us (28%)
  waiting for transfers between devices  121 us (25%)
  other arithmetic  79.6 us (17%)
  matrix products  61.5 us (13%)
  blocking collectives  43.3 us (9%)
  starting transfers between devices  25.6 us (5%)
  loops' own time  4.8 us (1%)
    ppermute x6, waiting for transfers between devices, shifted(): lax.ppermute(value, axis, [(source, source + steps) for source in range(f...  93 us
    dot_general x20, matrix products, product(): jnp.einsum(form, left, right, precision=highest, preferred_element_type=j...  61.5 us
    all_to_all x1, blocking collectives, body(): lax.all_to_all(physical, 'rows', split_axis=0, concat_axis=2, tiled=True)  43.3 us
    dynamic_update_slice x8, other arithmetic, section_solve(): lax.scan(forward, (zero_plane, (zero_plane,) * system_count), sweep_in)  30.7 us
    all_to_all x1, waiting for transfers between devices, body(): lax.all_to_all(spectral, 'rows', split_axis=2, concat_axis=0, tiled=True)  27.8 us
    unnamed x32, local copies, waits for them, and re-layouts  21.4 us
    ppermute x6, starting transfers between devices, shifted(): lax.ppermute(value, axis, [(source, source + steps) for source in range(f...  15.8 us
    neg x4, local copies, waits for them, and re-layouts, finish(): sine_half = jnp.where(leading[None, :], nyquist[:, None], -imag_final)  12.5 us
  transfers between devices with their start and end apart: 7, of which 7 were waited for; matrix products, arithmetic and copies ran while one was open for 0% of the time, Pallas kernels for 0%

commit v1 on v0

v1 whole, which is shorter than its diff:
```python
import math

import jax
import jax.numpy as jnp
import ml_dtypes
import numpy as np
from jax import lax
from jax.experimental import pallas as pl
from jax.experimental.pallas import tpu as pltpu
from jax.sharding import PartitionSpec as P

F32 = jnp.float32
BF16 = jnp.bfloat16
BY = 8
BX = 64
N = 2048
LANES = 128
NZ = 16
TURN = 2.0 * math.pi
RESIDUES = (1, 5, 9, 13, 2, 10, 4)
SWEEPS = 7


def split_host(table):
    table = np.asarray(table, np.float32)
    high = table.astype(ml_dtypes.bfloat16)
    low = (table - high.astype(np.float32)).astype(ml_dtypes.bfloat16)
    return high, low


def host_tables():
    b = np.arange(LANES)
    m = np.arange(LANES)
    angle = TURN * np.mod(np.outer(b, m), LANES) / LANES
    scale = math.sqrt(2.0 / N)
    cos, sin = scale * np.cos(angle), scale * np.sin(angle)
    full = np.block([[cos, -sin], [sin, cos]])
    edge = np.zeros((2 * LANES, 2 * LANES))
    freq0 = np.concatenate([np.arange(65), np.arange(1, 64)])
    angle0 = TURN * np.mod(np.outer(b, freq0), LANES) / LANES
    part = np.where(np.arange(LANES)[None, :] < 65, np.cos(angle0), -np.sin(angle0)) * scale
    part[:, 0] *= math.sqrt(0.5)
    part[:, 64] *= math.sqrt(0.5)
    edge[:LANES, :LANES] = part
    freq8 = 16 * np.arange(64) + 8
    angle8 = TURN * np.mod(np.outer(b, freq8), N) / N
    edge[LANES:, LANES:] = scale * np.concatenate([np.cos(angle8), -np.sin(angle8)], 1)
    q = np.array(RESIDUES)
    twist = TURN * np.outer(q, b) / N
    twiddle = np.zeros((16, LANES), np.float32)
    twiddle[:7] = np.cos(twist)
    twiddle[8:15] = np.sin(twist)
    freqs = [np.concatenate([16 * freq0, freq8, freq8])]
    for residue in RESIDUES:
        freqs.append(np.tile(16 * m + residue, 2))
    freqs = np.concatenate(freqs)
    eigen = (4.0 * np.sin(np.pi * freqs / N) ** 2).astype(np.float32).reshape(8, 256)
    spread = (np.arange(32)[:, None] == np.arange(N)[None, :] // BX).astype(ml_dtypes.bfloat16)
    return full, edge, twiddle, eigen, spread


def halves(value):
    high = value.astype(BF16)
    return high, (value - high.astype(F32)).astype(BF16)


def mm(left, right):
    return jnp.dot(left, right, preferred_element_type=F32)


def mm3(left, right):
    return mm(left[0], right[0]) + (mm(left[1], right[0]) + mm(left[0], right[1]))


def cmul(value, cos, sin):
    re, im = value
    return re * cos + im * sin, im * cos - re * sin


def cadd(left, right):
    return left[0] + right[0], left[1] + right[1]


def csub(left, right):
    return left[0] - right[0], left[1] - right[1]


def phase(steps):
    return math.cos(TURN * steps / 16), math.sin(TURN * steps / 16)


def real16(v):
    s = [v[a] + v[a + 8] for a in range(8)]
    d = [v[a] - v[a + 8] for a in range(8)]
    u = [(d[0], -d[4])]
    for a in range(1, 4):
        u.append(cmul((d[a], -d[a + 4]), *phase(a)))
    p02, m02 = cadd(u[0], u[2]), csub(u[0], u[2])
    p13, m13 = cadd(u[1], u[3]), csub(u[1], u[3])
    y1, y9 = cadd(p02, p13), csub(p02, p13)
    y5 = (m02[0] + m13[1], m02[1] - m13[0])
    y13 = (m02[0] - m13[1], m02[1] + m13[0])
    t = [s[a] + s[a + 4] for a in range(4)]
    e = [s[a] - s[a + 4] for a in range(4)]
    z1 = cmul((e[1], -e[3]), *phase(2))
    z0 = (e[0], -e[2])
    y2, y10 = cadd(z0, z1), csub(z0, z1)
    a0, a1 = t[0] + t[2], t[1] + t[3]
    y4 = (t[0] - t[2], t[3] - t[1])
    return (a0 + a1, a0 - a1), (y1, y5, y9, y13, y2, y10, y4)


def real16_back(real, comps):
    g1, g5, g9, g13, g2, g10, g4 = comps
    a0, a1 = real[0] + real[1], real[0] - real[1]
    t = [a0 + g4[0], a1 - g4[1], a0 - g4[0], a1 + g4[1]]
    z0 = cadd(g2, g10)
    cos, sin = phase(2)
    z1 = cmul(csub(g2, g10), cos, -sin)
    e = [z0[0], z1[0], -z0[1], -z1[1]]
    s = [t[a] + e[a] for a in range(4)] + [t[a] - e[a] for a in range(4)]
    p19, m19 = cadd(g1, g9), csub(g1, g9)
    p513, m513 = cadd(g5, g13), csub(g5, g13)
    u = [cadd(p19, p513), None, csub(p19, p513), None]
    u[1] = (m19[0] - m513[1], m19[1] + m513[0])
    u[3] = (m19[0] + m513[1], m19[1] - m513[0])
    d = [None] * 8
    for a in range(4):
        cos, sin = phase(a)
        z = u[a] if a == 0 else cmul(u[a], cos, -sin)
        d[a], d[a + 4] = z[0], -z[1]
    return [s[a] + d[a] for a in range(8)] + [s[a] - d[a] for a in range(8)]


YB = 16


def forward_x_kernel(src, keep, spread, twiddle, fh, fl, eh, el, out, hi, lo):
    masks = mm(keep[...].reshape(keep.shape[0] * keep.shape[1], keep.shape[2]).astype(BF16), spread[...])
    levels = src.shape[1]
    for z in range(levels):
        rows = []
        for a in range(16):
            piece = src[:, z, a * LANES : (a + 1) * LANES]
            mask = masks[:, a * LANES : (a + 1) * LANES]
            pieces = [
                piece[8 * i : 8 * i + 8] * mask[i * levels + z : i * levels + z + 1]
                for i in range(YB // 8)
            ]
            rows.append(jnp.concatenate(pieces, 0))
        real, comps = real16(rows)
        blocks = [real]
        for i in range(7):
            blocks.append(cmul(comps[i], twiddle[i : i + 1, :], twiddle[8 + i : 9 + i, :]))
        for i in range(8):
            for part in range(2):
                high, low = halves(blocks[i][part])
                at = pl.ds((i * levels + z) * YB, YB)
                cols = pl.ds(part * LANES, LANES)
                hi[at, cols] = high
                lo[at, cols] = low
    rows = levels * YB
    first = mm3((hi[:rows, :], lo[:rows, :]), (eh[...], el[...]))
    rest = mm3((hi[rows:, :], lo[rows:, :]), (fh[...], fl[...]))
    for i in range(8):
        value = first if i == 0 else rest[(i - 1) * rows : i * rows]
        out[i // 2, :, :, (i % 2) * 256 : (i % 2) * 256 + 256] = value.reshape(levels, YB, 256)


def forward_x(source, keep, consts):
    rows, levels, cells = source.shape
    spread, twiddle, fh, fl, eh, el = consts
    full2 = lambda shape: pl.BlockSpec(shape, lambda i: (0, 0))
    return pl.pallas_call(
        forward_x_kernel,
        grid=(rows // YB,),
        in_specs=[
            pl.BlockSpec((YB, levels, cells), lambda i: (i, 0, 0)),
            pl.BlockSpec((YB // BY, levels, cells // BX), lambda i: (i, 0, 0)),
            full2(spread.shape),
            full2(twiddle.shape),
        ]
        + [full2((256, 256))] * 4,
        out_specs=pl.BlockSpec((4, levels, YB, 512), lambda i: (0, 0, i, 0)),
        out_shape=jax.ShapeDtypeStruct((4, levels, rows, 512), F32),
        scratch_shapes=[pltpu.VMEM((8 * levels * YB, 256), BF16)] * 2,
        name="forward_x",
    )(source, keep, spread, twiddle, fh, fl, eh, el)


def inverse_x_kernel(spec, twiddle, fh, fl, eh, el, out, hi, lo):
    levels = spec.shape[1]
    rows = levels * YB
    for i in range(8):
        value = spec[i // 2, :, :, (i % 2) * 256 : (i % 2) * 256 + 256].reshape(rows, 256)
        high, low = halves(value)
        hi[i * rows : (i + 1) * rows, :] = high
        lo[i * rows : (i + 1) * rows, :] = low
    first = mm3((hi[:rows, :], lo[:rows, :]), (eh[...], el[...]))
    rest = mm3((hi[rows:, :], lo[rows:, :]), (fh[...], fl[...]))
    for z in range(levels):
        real = (first[z * YB : (z + 1) * YB, :LANES], first[z * YB : (z + 1) * YB, LANES:])
        comps = []
        for i in range(7):
            at = i * rows + z * YB
            value = (rest[at : at + YB, :LANES], rest[at : at + YB, LANES:])
            comps.append(cmul(value, twiddle[i : i + 1, :], -twiddle[8 + i : 9 + i, :]))
        cells = real16_back(real, comps)
        for a in range(16):
            out[:, z, a * LANES : (a + 1) * LANES] = cells[a]


def inverse_x(spec, consts):
    sections, levels, rows, _ = spec.shape
    twiddle, fh, fl, eh, el = consts
    full2 = lambda shape: pl.BlockSpec(shape, lambda i: (0, 0))
    return pl.pallas_call(
        inverse_x_kernel,
        grid=(rows // YB,),
        in_specs=[
            pl.BlockSpec((4, levels, YB, 512), lambda i: (0, 0, i, 0)),
            full2(twiddle.shape),
        ]
        + [full2((256, 256))] * 4,
        out_specs=pl.BlockSpec((YB, levels, N), lambda i: (i, 0, 0)),
        out_shape=jax.ShapeDtypeStruct((rows, levels, N), F32),
        scratch_shapes=[pltpu.VMEM((8 * levels * YB, 256), BF16)] * 2,
        name="inverse_x",
    )(spec, twiddle, fh, fl, eh, el)


def eigen_kernel(coup, lam, w2h, w2l, w4h, w4l):
    sub = lax.broadcasted_iota(jnp.int32, (8, LANES), 0)
    lane = lax.broadcasted_iota(jnp.int32, (8, LANES), 1)
    top = jnp.zeros((8, LANES), F32)
    bottom = jnp.zeros((8, LANES), F32)
    for i in range(NZ):
        row = jnp.where(lane == i, coup[i] + coup[i + 1], 0.0)
        if i > 0:
            row = row - jnp.where(lane == i - 1, coup[i], 0.0)
        if i < NZ - 1:
            row = row - jnp.where(lane == i + 1, coup[i + 1], 0.0)
        row = row + jnp.where(lane == NZ + i, 1.0, 0.0)
        if i < 8:
            top = jnp.where(sub == i, row, top)
        else:
            bottom = jnp.where(sub == i - 8, row, bottom)
    near, far = lane == sub, lane == sub + 8
    both = jnp.logical_or(near, far)
    low_half = lane < 8
    square = lane < NZ

    def pick(mask, value):
        return jnp.where(mask, value, 0.0)

    def angle(p, q, a):
        d = q - p
        root = jnp.sqrt(d * d + 4.0 * a * a)
        t = 2.0 * a / (jnp.abs(d) + root + 1e-30)
        t = jnp.where(d >= 0.0, t, -t)
        w = 1.0 + t * t
        c = lax.rsqrt(w)
        c = c * (1.5 - 0.5 * w * c * c)
        return c, t * c

    def partner(value):
        return jnp.where(low_half, pltpu.roll(value, LANES - 8, 1), pltpu.roll(value, 8, 1))

    def shuffle(value):
        right = pltpu.roll(value, 1, 1)
        left = pltpu.roll(value, LANES - 1, 1)
        out = jnp.where(lane < 8, right, left)
        out = jnp.where(lane == 1, pltpu.roll(value, LANES - 7, 1), out)
        out = jnp.where(lane == 15, pltpu.roll(value, 8, 1), out)
        return jnp.where(jnp.logical_or(lane == 0, lane >= NZ), value, out)

    def step(_, carry):
        top, bottom = carry
        c_s, s_s = angle(
            jnp.sum(pick(near, top), 1, keepdims=True),
            jnp.sum(pick(far, bottom), 1, keepdims=True),
            jnp.sum(pick(far, top), 1, keepdims=True),
        )
        one = jnp.broadcast_to(jnp.sum(pick(both, top), 0, keepdims=True), (8, LANES))
        two = jnp.broadcast_to(jnp.sum(pick(both, bottom), 0, keepdims=True), (8, LANES))
        p = jnp.where(low_half, one, pltpu.roll(one, 8, 1))
        q = jnp.where(low_half, pltpu.roll(two, LANES - 8, 1), two)
        a = jnp.where(low_half, pltpu.roll(one, LANES - 8, 1), one)
        c_l, s_l = angle(p, q, a)
        c_l = jnp.where(square, c_l, 1.0)
        s_l = jnp.where(low_half, -s_l, jnp.where(square, s_l, 0.0))
        t1 = top * c_l + partner(top) * s_l
        b1 = bottom * c_l + partner(bottom) * s_l
        t1, b1 = shuffle(t1), shuffle(b1)
        t2 = c_s * t1 - s_s * b1
        b2 = s_s * t1 + c_s * b1
        new_top = jnp.where(
            sub == 0, t2, jnp.where(sub == 1, pltpu.roll(b2, 1, 0), pltpu.roll(t2, 1, 0))
        )
        new_bottom = jnp.where(sub == 7, t2, pltpu.roll(b2, 7, 0))
        return new_top, new_bottom

    top, bottom = lax.fori_loop(0, 15 * SWEEPS, step, (top, bottom))
    lam[...] = jnp.concatenate(
        [
            jnp.broadcast_to(jnp.sum(pick(near, top), 1, keepdims=True), (8, LANES)),
            jnp.broadcast_to(jnp.sum(pick(far, bottom), 1, keepdims=True), (8, LANES)),
        ],
        0,
    )
    rows = jnp.concatenate([top, bottom], 0)
    rows = jnp.concatenate([rows] * 8, 0)
    src = lax.broadcasted_iota(jnp.int32, (LANES, LANES), 0)
    dst = lax.broadcasted_iota(jnp.int32, (LANES, LANES), 1)
    expand = (src == dst // 8 + NZ).astype(F32)
    wide = jnp.dot(rows, expand, precision=lax.Precision.HIGHEST, preferred_element_type=F32)
    w2 = jnp.where(src // NZ == dst % 8, wide, 0.0)
    w2h[...], w2l[...] = halves(w2)
    w4h[...], w4l[...] = halves(w2.T)


def eigen(couplings):
    matrix = jax.ShapeDtypeStruct((LANES, LANES), BF16)
    return pl.pallas_call(
        eigen_kernel,
        in_specs=[pl.BlockSpec(memory_space=pltpu.SMEM)],
        out_shape=[jax.ShapeDtypeStruct((NZ, LANES), F32), matrix, matrix, matrix, matrix],
        name="level_modes",
    )(couplings)


def decay(lam, e):
    half = 0.5 * (lam + e)
    root = jnp.sqrt(half * (2.0 + half))
    return 1.0 / (1.0 + half + root), 0.5 / root


def level_kernel(at, x, wh, wl, lam, eig, f, ends):
    h = pl.program_id(0)
    rows = x.shape[1]
    w = (wh[...], wl[...])
    e = eig[pl.ds(at[0] * 2 + h, 1), :]
    r, _ = decay(lam[:, 0:1], e)
    for o in range(rows // 8):
        block = x[:, 8 * o : 8 * o + 8, :].reshape(LANES, 256)
        value = mm3(w, halves(block))
        f[8 * o : 8 * o + 8, :, :] = value.reshape(8, NZ, 256)
    up = jnp.zeros((NZ, 256), F32)
    down = jnp.zeros((NZ, 256), F32)
    for y in range(rows):
        up = f[y] + r * up
        down = f[rows - 1 - y] + r * down
    ends[:, 0, :] = up[:, :LANES]
    ends[:, 1, :] = up[:, LANES:]
    ends[:, 2, :] = down[:, :LANES]
    ends[:, 3, :] = down[:, LANES:]


def level_transform(at, x, wh, wl, lam, eig):
    _, rows, width = x.shape
    whole = lambda shape: pl.BlockSpec(shape, lambda h, at: (0,) * len(shape))
    return pl.pallas_call(
        level_kernel,
        grid_spec=pltpu.PrefetchScalarGridSpec(
            num_scalar_prefetch=1,
            grid=(width // 256,),
            in_specs=[
                pl.BlockSpec((NZ, rows, 256), lambda h, at: (0, 0, h)),
                whole((LANES, LANES)),
                whole((LANES, LANES)),
                whole((NZ, LANES)),
                whole((8, 256)),
            ],
            out_specs=[
                pl.BlockSpec((rows, NZ, 256), lambda h, at: (0, 0, h)),
                pl.BlockSpec((NZ, 4, LANES), lambda h, at: (h, 0, 0)),
            ],
        ),
        out_shape=[
            jax.ShapeDtypeStruct((rows, NZ, width), F32),
            jax.ShapeDtypeStruct((2 * NZ, 4, LANES), F32),
        ],
        name="level_transform",
    )(at, x, wh, wl, lam, eig)


def carry_kernel(at, ends, lam, eig, out):
    sections = ends.shape[0]
    j = at[1]
    k = lax.rem(j, NZ)
    h = lax.div(j, NZ)
    e = eig[pl.ds(at[0] * 2 + h, 1), :]
    r, _ = decay(lam[pl.ds(k, 1), 0:1], e)
    for _ in range(6):
        r = r * r
    row = lax.broadcasted_iota(jnp.int32, (4, LANES), 0)
    ratio = jnp.where(lax.rem(row, 2) == 0, r[:, :LANES], r[:, LANES:])
    whole = ratio
    for _ in range(5):
        whole = whole * whole
    scale = 1.0 / (1.0 - whole)
    up = jnp.zeros((4, LANES), F32)
    down = jnp.zeros((4, LANES), F32)
    for s in range(sections):
        up = ends[s] + ratio * up
        down = ends[sections - 1 - s] + ratio * down
    up = up * scale
    down = down * scale
    first = row < 2
    ups = []
    for s in range(sections):
        ups.append(up)
        up = ends[s] + ratio * up
    for s in reversed(range(sections)):
        out[s] = jnp.where(first, ups[s], down)
        down = ends[s] + ratio * down


def carries(at, ends, lam, eig):
    return pl.pallas_call(
        carry_kernel,
        in_specs=[pl.BlockSpec(memory_space=pltpu.SMEM)] + [pl.BlockSpec(memory_space=pltpu.VMEM)] * 3,
        out_shape=jax.ShapeDtypeStruct(ends.shape, F32),
        name="section_carries",
    )(at, ends, lam, eig)


def solve_kernel(at, f, ends, wh, wl, lam, eig, out, work):
    h = pl.program_id(0)
    rows = f.shape[0]
    w = (wh[...], wl[...])
    e = eig[pl.ds(at[0] * 2 + h, 1), :]
    r, gain = decay(lam[:, 0:1], e)
    up = jnp.concatenate([ends[:, 0, :], ends[:, 1, :]], 1)
    down = jnp.concatenate([ends[:, 2, :], ends[:, 3, :]], 1)
    for y in range(rows):
        up = r * up
        work[y] = up
        up = up + f[y]
    for y in reversed(range(rows)):
        down = f[y] + r * down
        work[y] = (work[y] + down) * gain
    for o in range(rows // 8):
        block = work[8 * o : 8 * o + 8].reshape(LANES, 256)
        value = mm3(w, halves(block))
        out[:, 8 * o : 8 * o + 8, :] = value.reshape(NZ, 8, 256)


def solve(at, f, ends, wh, wl, lam, eig):
    rows, _, width = f.shape
    whole = lambda shape: pl.BlockSpec(shape, lambda h, at: (0,) * len(shape))
    return pl.pallas_call(
        solve_kernel,
        grid_spec=pltpu.PrefetchScalarGridSpec(
            num_scalar_prefetch=1,
            grid=(width // 256,),
            in_specs=[
                pl.BlockSpec((rows, NZ, 256), lambda h, at: (0, 0, h)),
                pl.BlockSpec((NZ, 4, LANES), lambda h, at: (h, 0, 0)),
                whole((LANES, LANES)),
                whole((LANES, LANES)),
                whole((NZ, LANES)),
                whole((8, 256)),
            ],
            out_specs=pl.BlockSpec((NZ, rows, 256), lambda h, at: (0, 0, h)),
            scratch_shapes=[pltpu.VMEM((rows, NZ, 256), F32)],
        ),
        out_shape=jax.ShapeDtypeStruct((NZ, rows, width), F32),
        name="solve_columns",
    )(at, f, ends, wh, wl, lam, eig)


def body(source, solid, couplings):
    rows, levels, _ = source.shape
    full, edge, twiddle, eig, spread = host_tables()
    fh, fl = split_host(full)
    eh, el = split_host(edge)
    fth, ftl = split_host(full.T)
    eth, etl = split_host(edge.T)
    keep = (1 - solid).astype(F32)
    at = jnp.stack([lax.axis_index("lev"), lax.axis_index("rows")]).astype(jnp.int32)
    lam, w2h, w2l, w4h, w4l = eigen(couplings)
    spectral = forward_x(source, keep, (spread, twiddle, fh, fl, eh, el))
    gathered = lax.all_to_all(spectral, "lev", 0, 0, tiled=True)
    f, ends = level_transform(at, gathered.reshape(NZ, rows, 512), w2h, w2l, lam, eig)
    ends = lax.all_to_all(ends, "rows", 0, 0, tiled=True)
    ends = carries(at, ends, lam, eig)
    ends = lax.all_to_all(ends, "rows", 0, 0, tiled=True)
    pressure = solve(at, f, ends, w4h, w4l, lam, eig)
    back = lax.all_to_all(pressure.reshape(4, levels, rows, 512), "lev", 0, 0, tiled=True)
    return inverse_x(back, (twiddle, fth, ftl, eth, etl))


def solution(mesh):
    return jax.shard_map(
        body,
        mesh=mesh,
        in_specs=(P("rows", "lev", None), P("rows", "lev", None), P()),
        out_specs=P("rows", "lev", None),
        check_vma=False,
    )
```

time: 477 us -> 116 us (0.24); the launches traced: 469 us -> 115 us
  local copies, waits for them, and re-layouts: 132 us -> 1.32 us
  waiting for transfers between devices: 121 us -> 2.48 us
  other arithmetic: 79.6 us -> 1.98 us
  matrix products: 61.5 us -> 0 us
  Pallas kernels: 0 us -> 44.8 us
  starting transfers between devices: 25.6 us -> 5 us
  blocking collectives: 43.3 us -> 59.7 us
  loops' own time: 4.8 us -> 0 us
    ppermute x6 -> x0, waiting for transfers between devices: 93 us -> none  [shifted(): lax.ppermute(value, axis, [(source, source + steps) for source in range(f...]
    dot_general x20 -> x0, matrix products: 61.5 us -> none  [product(): jnp.einsum(form, left, right, precision=highest, preferred_element_type=j...]
    pallas_call x0 -> x6, Pallas kernels: none -> 44.8 us  [the longest x1 22.3 us: eigen(): pl.pallas_call(eigen_kernel, in_specs=[pl.BlockSpec(memory_space=pltpu.SM...]
    dynamic_update_slice x8 -> x0, other arithmetic: 30.7 us -> none  [section_solve(): lax.scan(forward, (zero_plane, (zero_plane,) * system_count), sweep_in)]
    all_to_all x1, waiting for transfers between devices: 27.8 us -> 2.48 us  [body(): gathered = lax.all_to_all(spectral, 'lev', 0, 0, tiled=True)]
    unnamed x32 -> x2, local copies, waits for them, and re-layouts: 21.4 us -> 1.32 us
    reshape x4 -> x0, local copies, waits for them, and re-layouts: 19.1 us -> none  [the longest x1 6.7 us: body(): source.reshape(row_count // BY, BY, level_count, cell_count // BX, BX)]
    another operation x8 -> x0, local copies, waits for them, and re-layouts: 17.5 us -> none
  transfers between devices with their start and end apart: 7 -> 1, of which waited for: 7 -> 1; matrix products, arithmetic and copies ran while one was open for 0% -> 1% of each run, Pallas kernels for 0% -> 19%
where the time goes in v1:
time: 116 us; the launch traced here: 115 us
  blocking collectives  59.7 us (51%)
  Pallas kernels  44.8 us (39%)
  starting transfers between devices  5 us (4%)
  waiting for transfers between devices  2.48 us (2%)
  other arithmetic  1.98 us (2%)
  local copies, waits for them, and re-layouts  1.32 us (1%)
    all_to_all x1, blocking collectives, body(): lax.all_to_all(pressure.reshape(4, levels, rows, 512), 'lev', 0, 0, tiled...  30.5 us
    all_to_all x2, blocking collectives, body(): ends = lax.all_to_all(ends, 'rows', 0, 0, tiled=True)  29.3 us
    pallas_call x1, Pallas kernels, eigen(): pl.pallas_call(eigen_kernel, in_specs=[pl.BlockSpec(memory_space=pltpu.SM...  22.3 us
    pallas_call x1, Pallas kernels, forward_x(): pl.pallas_call(forward_x_kernel, grid=(rows // YB,), in_specs=[pl.BlockSp...  6.31 us
    pallas_call x1, Pallas kernels, inverse_x(): pl.pallas_call(inverse_x_kernel, grid=(rows // YB,), in_specs=[pl.BlockSp...  5.6 us
    all_to_all x1, starting transfers between devices, body(): gathered = lax.all_to_all(spectral, 'lev', 0, 0, tiled=True)  5 us
    pallas_call x1, Pallas kernels, solve(): pl.pallas_call(solve_kernel, grid_spec=pltpu.PrefetchScalarGridSpec(num_s...  4.55 us
    pallas_call x1, Pallas kernels, level_transform(): pl.pallas_call(level_kernel, grid_spec=pltpu.PrefetchScalarGridSpec(num_s...  4.29 us
  transfers between devices with their start and end apart: 1, of which 1 were waited for; matrix products, arithmetic and copies ran while one was open for 1% of the time, Pallas kernels for 19%

profile of v1, /device:TPU:1, one launch (start us, length us, event | category | flops | bytes accessed | tf_op | source)
XLA Modules:
  0.0 115.3 jit_solution(7458337841659840824)
XLA Ops:
  0.0 1.3 %subtract_convert_fusion.keep = f32[8,4,32]{2,1,0:T(4,128)} fusion(s32[8,4,32]{2,1,0:T(4,128)} %param.15), kind=kLoop, calls=%fused_computation | loop fusion | flops 2048 | bytes 8192 | tf_op jit(solution)/shard_map/convert_element_type | solution.py:480
  1.3 6.3 %forward_x.1 = f32[4,4,64,512]{3,2,1,0:T(8,128)} custom-call(f32[64,4,2048]{2,1,0:T(4,128)} %src.1, f32[8,4,32]{2,1,0:T(4,128)} %subtract_convert_fusion.keep, bf16[32,2048]{1,0:T(8,128)(2,1)} %constant.33.clone.spread, f32[16,128]{1,0:T(8,128)} %constant.34.clone.twiddle, bf16[256,256]{1,0:T(8,128)(2,1)} %constant.35.clone.fh, ...), custom_call_target="tpu_custom_call" | custom-call | tf_op jit(solution)/shard_map/forward_x/pallas_call | solution.py:174
  7.6 5.0 %all-to-all-start = ((f32[4,4,64,512]{3,2,1,0:T(8,128)}), f32[4,4,64,512]{3,2,1,0:T(8,128)S(1)}, u32[]{:S(2)}, u32[]{:S(2)}) async-start(f32[4,4,64,512]{3,2,1,0:T(8,128)} %forward_x.1), calls=%async_computation | async-start | bytes 4194304 | tf_op jit(solution)/shard_map/all_to_all | solution.py:484
  12.6 22.3 %level_modes.1 = (f32[16,128]{1,0:T(8,128)}, bf16[128,128]{1,0:T(8,128)(2,1)}, bf16[128,128]{1,0:T(8,128)(2,1)}, bf16[128,128]{1,0:T(8,128)(2,1)}, bf16[128,128]{1,0:T(8,128)(2,1)}) custom-call(f32[17]{0:T(128)} %coup.1), custom_call_target="tpu_custom_call" | custom-call | tf_op jit(solution)/shard_map/level_modes/pallas_call | solution.py:324
  35.0 0.7 pad_add_fusion.at
  35.6 2.5 %all-to-all-done = f32[4,4,64,512]{3,2,1,0:T(8,128)S(1)} async-done(((f32[4,4,64,512]{3,2,1,0:T(8,128)}), f32[4,4,64,512]{3,2,1,0:T(8,128)S(1)}, u32[]{:S(2)}, u32[]{:S(2)}) %all-to-all-start) | async-done | bytes 2097184 | tf_op jit(solution)/shard_map/all_to_all | solution.py:484
  38.1 0.0 copy-start
  38.1 1.3 %copy-done = f32[4,4,64,512]{3,2,1,0:T(8,128)} copy-done((f32[4,4,64,512]{3,2,1,0:T(8,128)}, f32[4,4,64,512]{3,2,1,0:T(8,128)S(1)}, u32[]{:S(2)}) %copy-start) | copy-done | bytes 2097176
  39.4 4.3 %level_transform.1 = (f32[64,16,512]{2,1,0:T(8,128)}, f32[32,4,128]{2,1,0:T(4,128)}) custom-call(s32[2]{0:T(128)} %pad_add_fusion.at, f32[16,64,512]{2,1,0:T(8,128)} %bitcast.4, bf16[128,128]{1,0:T(8,128)(2,1)} %get-tuple-element.12.wh, bf16[128,128]{1,0:T(8,128)(2,1)} %get-tuple-element.13.wl, f32[16,128]{1,0:T(8,128)} %get-tuple-element.14.lam, ...), custom_call_target="tpu_custom_call" | custom-call | tf_op jit(solution)/shard_map/level_transform/pallas_call | solution.py:362
  43.7 17.2 %all_to_all.20.ends = f32[32,4,128]{2,1,0:T(4,128)} all-to-all(f32[32,4,128]{2,1,0:T(4,128)} %get-tuple-element.16), channel_id=1, replica_groups=mesh['rows'=32,'lev'=4] {'rows'}, dimensions={0} | all-to-all | bytes 131072 | tf_op jit(solution)/shard_map/all_to_all | solution.py:486
  60.9 1.7 %section_carries.1 = f32[32,4,128]{2,1,0:T(4,128)} custom-call(s32[2]{0:T(128)} %pad_add_fusion.at, f32[32,4,128]{2,1,0:T(4,128)} %all_to_all.20.ends, f32[16,128]{1,0:T(8,128)} %get-tuple-element.14.lam, f32[8,256]{1,0:T(8,128)} %constant.39.clone.eig), custom_call_target="tpu_custom_call" | custom-call | tf_op jit(solution)/shard_map/section_carries/pallas_call | solution.py:420
  62.7 12.0 %all_to_all.21.ends = f32[32,4,128]{2,1,0:T(4,128)} all-to-all(f32[32,4,128]{2,1,0:T(4,128)} %section_carries.1), channel_id=1, replica_groups=mesh['rows'=32,'lev'=4] {'rows'}, dimensions={0} | all-to-all | bytes 131072 | tf_op jit(solution)/shard_map/all_to_all | solution.py:488
  74.7 4.5 %solve_columns.1 = f32[16,64,512]{2,1,0:T(8,128)} custom-call(s32[2]{0:T(128)} %pad_add_fusion.at, f32[64,16,512]{2,1,0:T(8,128)} %get-tuple-element.15.f, f32[32,4,128]{2,1,0:T(4,128)} %all_to_all.21.ends, bf16[128,128]{1,0:T(8,128)(2,1)} %get-tuple-element.17.wh, bf16[128,128]{1,0:T(8,128)(2,1)} %get-tuple-element.18.wl, f32[16,128]{1,0:T(8,128)} %get-tuple-element.14.lam, ...), custom_call_target="tpu_custom_call" | custom-call | tf_op jit(solution)/shard_map/solve_columns/pallas_call | solution.py:452
  79.3 30.5 %all_to_all.22.spec = f32[4,4,64,512]{3,2,1,0:T(8,128)} all-to-all(f32[4,4,64,512]{3,2,1,0:T(8,128)} %bitcast.5), channel_id=1, replica_groups=mesh['rows'=32,'lev'=4] {'lev'}, dimensions={0} | all-to-all | bytes 4194304 | tf_op jit(solution)/shard_map/all_to_all | solution.py:490
  109.7 5.6 %inverse_x.1 = f32[64,4,2048]{2,1,0:T(4,128)} custom-call(f32[4,4,64,512]{3,2,1,0:T(8,128)} %all_to_all.22.spec, f32[16,128]{1,0:T(8,128)} %constant.34.clone.twiddle, bf16[256,256]{1,0:T(8,128)(2,1)} %constant.40.clone.fh, bf16[256,256]{1,0:T(8,128)(2,1)} %constant.41.clone.fl, bf16[256,256]{1,0:T(8,128)(2,1)} %constant.42.clone.eh, ...), custom_call_target="tpu_custom_call" | custom-call | tf_op jit(solution)/shard_map/inverse_x/pallas_call | solution.py:217
Async XLA Ops:
  7.6 30.5 %all-to-all-start = ((f32[4,4,64,512]{3,2,1,0:T(8,128)}), f32[4,4,64,512]{3,2,1,0:T(8,128)S(1)}, u32[]{:S(2)}, u32[]{:S(2)}) async-start(f32[4,4,64,512]{3,2,1,0:T(8,128)} %forward_x.1), calls=%async_computation | async-start | bytes 4194304 | tf_op jit(solution)/shard_map/all_to_all | solution.py:484
  38.1 1.3 %copy-start = (f32[4,4,64,512]{3,2,1,0:T(8,128)}, f32[4,4,64,512]{3,2,1,0:T(8,128)S(1)}, u32[]{:S(2)}) copy-start(f32[4,4,64,512]{3,2,1,0:T(8,128)S(1)} %all-to-all-done) | copy-start | bytes 6291460

commit v2 on v1

--- a/solution.py
+++ b/solution.py
@@ -136,7 +136,8 @@
 
 
 def forward_x_kernel(src, keep, spread, twiddle, fh, fl, eh, el, out, hi, lo):
-    masks = mm(keep[...].reshape(keep.shape[0] * keep.shape[1], keep.shape[2]).astype(BF16), spread[...])
+    open_cells = (1 - keep[...]).astype(F32).astype(BF16)
+    masks = mm(open_cells.reshape(keep.shape[0] * keep.shape[1], keep.shape[2]), spread[...])
     levels = src.shape[1]
     for z in range(levels):
         rows = []
@@ -188,48 +189,7 @@
     )(source, keep, spread, twiddle, fh, fl, eh, el)
 
 
-def inverse_x_kernel(spec, twiddle, fh, fl, eh, el, out, hi, lo):
-    levels = spec.shape[1]
-    rows = levels * YB
-    for i in range(8):
-        value = spec[i // 2, :, :, (i % 2) * 256 : (i % 2) * 256 + 256].reshape(rows, 256)
-        high, low = halves(value)
-        hi[i * rows : (i + 1) * rows, :] = high
-        lo[i * rows : (i + 1) * rows, :] = low
-    first = mm3((hi[:rows, :], lo[:rows, :]), (eh[...], el[...]))
-    rest = mm3((hi[rows:, :], lo[rows:, :]), (fh[...], fl[...]))
-    for z in range(levels):
-        real = (first[z * YB : (z + 1) * YB, :LANES], first[z * YB : (z + 1) * YB, LANES:])
-        comps = []
-        for i in range(7):
-            at = i * rows + z * YB
-            value = (rest[at : at + YB, :LANES], rest[at : at + YB, LANES:])
-            comps.append(cmul(value, twiddle[i : i + 1, :], -twiddle[8 + i : 9 + i, :]))
-        cells = real16_back(real, comps)
-        for a in range(16):
-            out[:, z, a * LANES : (a + 1) * LANES] = cells[a]
-
-
-def inverse_x(spec, consts):
-    sections, levels, rows, _ = spec.shape
-    twiddle, fh, fl, eh, el = consts
-    full2 = lambda shape: pl.BlockSpec(shape, lambda i: (0, 0))
-    return pl.pallas_call(
-        inverse_x_kernel,
-        grid=(rows // YB,),
-        in_specs=[
-            pl.BlockSpec((4, levels, YB, 512), lambda i: (0, 0, i, 0)),
-            full2(twiddle.shape),
-        ]
-        + [full2((256, 256))] * 4,
-        out_specs=pl.BlockSpec((YB, levels, N), lambda i: (i, 0, 0)),
-        out_shape=jax.ShapeDtypeStruct((rows, levels, N), F32),
-        scratch_shapes=[pltpu.VMEM((8 * levels * YB, 256), BF16)] * 2,
-        name="inverse_x",
-    )(spec, twiddle, fh, fl, eh, el)
-
-
-def eigen_kernel(coup, lam, w2h, w2l, w4h, w4l):
+def eigen_kernel(coup, lam, modes, w2h, w2l, w4h, w4l):
     sub = lax.broadcasted_iota(jnp.int32, (8, LANES), 0)
     lane = lax.broadcasted_iota(jnp.int32, (8, LANES), 1)
     top = jnp.zeros((8, LANES), F32)
@@ -309,6 +269,7 @@
         0,
     )
     rows = jnp.concatenate([top, bottom], 0)
+    modes[...] = pltpu.roll(rows, LANES - NZ, 1)
     rows = jnp.concatenate([rows] * 8, 0)
     src = lax.broadcasted_iota(jnp.int32, (LANES, LANES), 0)
     dst = lax.broadcasted_iota(jnp.int32, (LANES, LANES), 1)
@@ -316,7 +277,8 @@
     wide = jnp.dot(rows, expand, precision=lax.Precision.HIGHEST, preferred_element_type=F32)
     w2 = jnp.where(src // NZ == dst % 8, wide, 0.0)
     w2h[...], w2l[...] = halves(w2)
-    w4h[...], w4l[...] = halves(w2.T)
+    w4 = w2.T
+    w4h[...], w4l[...] = halves(jnp.concatenate([w4, w4], 0))
 
 
 def eigen(couplings):
@@ -324,7 +286,9 @@
     return pl.pallas_call(
         eigen_kernel,
         in_specs=[pl.BlockSpec(memory_space=pltpu.SMEM)],
-        out_shape=[jax.ShapeDtypeStruct((NZ, LANES), F32), matrix, matrix, matrix, matrix],
+        out_shape=[jax.ShapeDtypeStruct((NZ, LANES), F32)] * 2
+        + [matrix] * 2
+        + [jax.ShapeDtypeStruct((2 * LANES, LANES), BF16)] * 2,
         name="level_modes",
     )(couplings)
 
@@ -335,53 +299,159 @@
     return 1.0 / (1.0 + half + root), 0.5 / root
 
 
-def level_kernel(at, x, wh, wl, lam, eig, f, ends):
+def powers(base, count):
+    square = base * base
+    value = jnp.where((count & 1) != 0, base, 1.0)
+    value = value * jnp.where((count & 2) != 0, square, 1.0)
+    return value * jnp.where((count & 4) != 0, square * square, 1.0)
+
+
+def inverse_x_kernel(
+    at, spec0, spec1, spec2, spec3, ends, modes, lam, eig, twiddle, fh, fl, eh, el,
+    out, hi, lo, above, below, eighth, steps,
+):
+    levels = spec0.shape[0]
+    rows = levels * YB
+    i = pl.program_id(0)
+    blocks = 2 * pl.num_programs(0)
+
+    @pl.when(i == 0)
+    def _():
+        b = lax.broadcasted_iota(jnp.int32, (8, LANES), 0)
+        for t in range(16):
+            l, h, p = t // 4, (t // 2) % 2, t % 2
+            e = eig[t // 2 : t // 2 + 1, p * LANES : (p + 1) * LANES]
+            r, gain = decay(lam[:, 0:1], e)
+            gain = gain * r
+            up = ends[h, :, l, p, :] * gain
+            down = ends[h, :, l, 2 + p, :] * gain
+            r2 = r * r
+            r4 = r2 * r2
+            eighth[t] = r4 * r4
+            for k in range(NZ):
+                base = jnp.broadcast_to(r[k : k + 1], (8, LANES))
+                above[t, k] = powers(base, b) * up[k : k + 1]
+                below[t, k] = powers(base, 7 - b) * down[k : k + 1]
+
+    r8 = eighth[...]
+    for o in range(2):
+        steps[o] = powers(r8, 2 * i + o)
+        steps[2 + o] = powers(r8, blocks - 1 - 2 * i - o)
+    first_level = at[0] * levels
+    for step, spec in enumerate((spec0, spec1, spec2, spec3)):
+        l = (at[0] - step) & 3
+        for part in range(4):
+            t = 4 * l + part
+            acc = [[None, None] for _ in range(levels)]
+            for k in range(NZ):
+                u, d = above[t, k], below[t, k]
+                for o in range(2):
+                    value = u * steps[o, t, k : k + 1, :] + d * steps[2 + o, t, k : k + 1, :]
+                    for z in range(levels):
+                        term = value * modes[k, first_level + z]
+                        acc[z][o] = term if k == 0 else acc[z][o] + term
+            for z in range(levels):
+                value = spec[z, :, part * LANES : (part + 1) * LANES] + jnp.concatenate(acc[z], 0)
+                high, low = halves(value)
+                place = pl.multiple_of((2 * l + part // 2) * rows + z * YB, YB)
+                half = pl.ds((part % 2) * LANES, LANES)
+                hi[pl.ds(place, YB), half] = high
+                lo[pl.ds(place, YB), half] = low
+    first = mm3((hi[:rows, :], lo[:rows, :]), (eh[...], el[...]))
+    rest = mm3((hi[rows:, :], lo[rows:, :]), (fh[...], fl[...]))
+    for z in range(levels):
+        real = (first[z * YB : (z + 1) * YB, :LANES], first[z * YB : (z + 1) * YB, LANES:])
+        comps = []
+        for i in range(7):
+            place = i * rows + z * YB
+            value = (rest[place : place + YB, :LANES], rest[place : place + YB, LANES:])
+            comps.append(cmul(value, twiddle[i : i + 1, :], -twiddle[8 + i : 9 + i, :]))
+        cells = real16_back(real, comps)
+        for a in range(16):
+            out[:, z, a * LANES : (a + 1) * LANES] = cells[a]
+
+
+def inverse_x(at, specs, ends, modes, lam, eig, consts):
+    levels, rows, _ = specs[0].shape
+    twiddle, fh, fl, eh, el = consts
+    whole = lambda value: pl.BlockSpec(value.shape, lambda i, at: (0,) * value.ndim)
+    return pl.pallas_call(
+        inverse_x_kernel,
+        grid_spec=pltpu.PrefetchScalarGridSpec(
+            num_scalar_prefetch=1,
+            grid=(rows // YB,),
+            in_specs=[pl.BlockSpec((levels, YB, 512), lambda i, at: (0, i, 0))] * 4
+            + [
+                whole(ends),
+                pl.BlockSpec(memory_space=pltpu.SMEM),
+                whole(lam),
+                whole(eig),
+                whole(twiddle),
+            ]
+            + [whole(fh)] * 4,
+            out_specs=pl.BlockSpec((YB, levels, N), lambda i, at: (i, 0, 0)),
+            scratch_shapes=[pltpu.VMEM((8 * levels * YB, 256), BF16)] * 2
+            + [pltpu.VMEM((16, NZ, 8, LANES), F32)] * 2
+            + [pltpu.VMEM((16, NZ, LANES), F32), pltpu.VMEM((4, 16, NZ, LANES), F32)],
+        ),
+        out_shape=jax.ShapeDtypeStruct((rows, levels, N), F32),
+        name="inverse_x",
+    )(at, *specs, ends, modes, lam, eig, twiddle, fh, fl, eh, el)
+
+
+def level_kernel(at, x, w2h, w2l, w4h, w4l, lam, eig, out0, out1, out2, out3, ends, f, work):
     h = pl.program_id(0)
     rows = x.shape[1]
-    w = (wh[...], wl[...])
+    w2 = (w2h[...], w2l[...])
+    turned = pl.ds(pl.multiple_of(at[0] * 32, 32), LANES)
+    w4 = (w4h[turned, :], w4l[turned, :])
     e = eig[pl.ds(at[0] * 2 + h, 1), :]
-    r, _ = decay(lam[:, 0:1], e)
+    r, gain = decay(lam[:, 0:1], e)
     for o in range(rows // 8):
         block = x[:, 8 * o : 8 * o + 8, :].reshape(LANES, 256)
-        value = mm3(w, halves(block))
+        value = mm3(w2, halves(block))
         f[8 * o : 8 * o + 8, :, :] = value.reshape(8, NZ, 256)
     up = jnp.zeros((NZ, 256), F32)
     down = jnp.zeros((NZ, 256), F32)
     for y in range(rows):
-        up = f[y] + r * up
-        down = f[rows - 1 - y] + r * down
+        up = r * up
+        work[y] = up
+        up = up + f[y]
+    for y in reversed(range(rows)):
+        down = f[y] + r * down
+        work[y] = (work[y] + down) * gain
     ends[:, 0, :] = up[:, :LANES]
     ends[:, 1, :] = up[:, LANES:]
     ends[:, 2, :] = down[:, :LANES]
     ends[:, 3, :] = down[:, LANES:]
-
-
-def level_transform(at, x, wh, wl, lam, eig):
+    for o in range(rows // 8):
+        block = work[8 * o : 8 * o + 8].reshape(LANES, 256)
+        value = mm3(w4, halves(block))
+        for step, out in enumerate((out0, out1, out2, out3)):
+            out[:, 8 * o : 8 * o + 8, :] = value[32 * step : 32 * step + 32].reshape(4, 8, 256)
+
+
+def level_solve(at, x, weights, lam, eig):
     _, rows, width = x.shape
     whole = lambda shape: pl.BlockSpec(shape, lambda h, at: (0,) * len(shape))
+    field = pl.BlockSpec((NZ, rows, 256), lambda h, at: (0, 0, h))
     return pl.pallas_call(
         level_kernel,
         grid_spec=pltpu.PrefetchScalarGridSpec(
             num_scalar_prefetch=1,
             grid=(width // 256,),
-            in_specs=[
-                pl.BlockSpec((NZ, rows, 256), lambda h, at: (0, 0, h)),
-                whole((LANES, LANES)),
-                whole((LANES, LANES)),
-                whole((NZ, LANES)),
-                whole((8, 256)),
-            ],
-            out_specs=[
-                pl.BlockSpec((rows, NZ, 256), lambda h, at: (0, 0, h)),
-                pl.BlockSpec((NZ, 4, LANES), lambda h, at: (h, 0, 0)),
-            ],
+            in_specs=[field]
+            + [whole((LANES, LANES))] * 2
+            + [whole((2 * LANES, LANES))] * 2
+            + [whole((NZ, LANES)), whole((8, 256))],
+            out_specs=[pl.BlockSpec((4, rows, 256), lambda h, at: (0, 0, h))] * 4
+            + [pl.BlockSpec((NZ, 4, LANES), lambda h, at: (h, 0, 0))],
+            scratch_shapes=[pltpu.VMEM((rows, NZ, 256), F32)] * 2,
         ),
-        out_shape=[
-            jax.ShapeDtypeStruct((rows, NZ, width), F32),
-            jax.ShapeDtypeStruct((2 * NZ, 4, LANES), F32),
-        ],
-        name="level_transform",
-    )(at, x, wh, wl, lam, eig)
+        out_shape=[jax.ShapeDtypeStruct((4, rows, width), F32)] * 4
+        + [jax.ShapeDtypeStruct((2 * NZ, 4, LANES), F32)],
+        name="level_solve",
+    )(at, x, *weights, lam, eig)
 
 
 def carry_kernel(at, ends, lam, eig, out):
@@ -412,7 +482,9 @@
         ups.append(up)
         up = ends[s] + ratio * up
     for s in reversed(range(sections)):
-        out[s] = jnp.where(first, ups[s], down)
+        value = jnp.where(first, ups[s], down)
+        for section in range(4):
+            out[s, section] = value
         down = ends[s] + ratio * down
 
 
@@ -420,54 +492,9 @@
     return pl.pallas_call(
         carry_kernel,
         in_specs=[pl.BlockSpec(memory_space=pltpu.SMEM)] + [pl.BlockSpec(memory_space=pltpu.VMEM)] * 3,
-        out_shape=jax.ShapeDtypeStruct(ends.shape, F32),
+        out_shape=jax.ShapeDtypeStruct((ends.shape[0], 4) + ends.shape[1:], F32),
         name="section_carries",
     )(at, ends, lam, eig)
-
-
-def solve_kernel(at, f, ends, wh, wl, lam, eig, out, work):
-    h = pl.program_id(0)
-    rows = f.shape[0]
-    w = (wh[...], wl[...])
-    e = eig[pl.ds(at[0] * 2 + h, 1), :]
-    r, gain = decay(lam[:, 0:1], e)
-    up = jnp.concatenate([ends[:, 0, :], ends[:, 1, :]], 1)
-    down = jnp.concatenate([ends[:, 2, :], ends[:, 3, :]], 1)
-    for y in range(rows):
-        up = r * up
-        work[y] = up
-        up = up + f[y]
-    for y in reversed(range(rows)):
-        down = f[y] + r * down
-        work[y] = (work[y] + down) * gain
-    for o in range(rows // 8):
-        block = work[8 * o : 8 * o + 8].reshape(LANES, 256)
-        value = mm3(w, halves(block))
-        out[:, 8 * o : 8 * o + 8, :] = value.reshape(NZ, 8, 256)
-
-
-def solve(at, f, ends, wh, wl, lam, eig):
-    rows, _, width = f.shape
-    whole = lambda shape: pl.BlockSpec(shape, lambda h, at: (0,) * len(shape))
-    return pl.pallas_call(
-        solve_kernel,
-        grid_spec=pltpu.PrefetchScalarGridSpec(
-            num_scalar_prefetch=1,
-            grid=(width // 256,),
-            in_specs=[
-                pl.BlockSpec((rows, NZ, 256), lambda h, at: (0, 0, h)),
-                pl.BlockSpec((NZ, 4, LANES), lambda h, at: (h, 0, 0)),
-                whole((LANES, LANES)),
-                whole((LANES, LANES)),
-                whole((NZ, LANES)),
-                whole((8, 256)),
-            ],
-            out_specs=pl.BlockSpec((NZ, rows, 256), lambda h, at: (0, 0, h)),
-            scratch_shapes=[pltpu.VMEM((rows, NZ, 256), F32)],
-        ),
-        out_shape=jax.ShapeDtypeStruct((NZ, rows, width), F32),
-        name="solve_columns",
-    )(at, f, ends, wh, wl, lam, eig)
 
 
 def body(source, solid, couplings):
@@ -477,18 +504,18 @@
     eh, el = split_host(edge)
     fth, ftl = split_host(full.T)
     eth, etl = split_host(edge.T)
-    keep = (1 - solid).astype(F32)
     at = jnp.stack([lax.axis_index("lev"), lax.axis_index("rows")]).astype(jnp.int32)
-    lam, w2h, w2l, w4h, w4l = eigen(couplings)
-    spectral = forward_x(source, keep, (spread, twiddle, fh, fl, eh, el))
+    lam, modes, w2h, w2l, w4h, w4l = eigen(couplings)
+    spectral = forward_x(source, solid, (spread, twiddle, fh, fl, eh, el))
     gathered = lax.all_to_all(spectral, "lev", 0, 0, tiled=True)
-    f, ends = level_transform(at, gathered.reshape(NZ, rows, 512), w2h, w2l, lam, eig)
+    *parts, ends = level_solve(at, gathered.reshape(NZ, rows, 512), (w2h, w2l, w4h, w4l), lam, eig)
+    specs = [parts[0]]
+    for step in range(1, 4):
+        specs.append(lax.ppermute(parts[step], "lev", [(i, (i + step) % 4) for i in range(4)]))
     ends = lax.all_to_all(ends, "rows", 0, 0, tiled=True)
-    ends = carries(at, ends, lam, eig)
-    ends = lax.all_to_all(ends, "rows", 0, 0, tiled=True)
-    pressure = solve(at, f, ends, w4h, w4l, lam, eig)
-    back = lax.all_to_all(pressure.reshape(4, levels, rows, 512), "lev", 0, 0, tiled=True)
-    return inverse_x(back, (twiddle, fth, ftl, eth, etl))
+    ends = carries(at, ends, lam, eig).reshape(128, 4, LANES)
+    ends = lax.all_to_all(ends, ("rows", "lev"), 0, 0, tiled=True).reshape(2, NZ, 4, 4, LANES)
+    return inverse_x(at, specs, ends, modes, lam, eig, (twiddle, fth, ftl, eth, etl))
 
 
 def solution(mesh):

time: 116 us -> 95.8 us (0.83)
  blocking collectives: 59.7 us -> 34.6 us
  starting transfers between devices: 5 us -> 7.78 us
  Pallas kernels: 44.8 us -> 47.4 us
  other arithmetic: 1.98 us -> 0.59 us
    all_to_all x1, blocking collectives: 30.5 us -> 16.8 us  [body(): lax.all_to_all(ends, ('rows', 'lev'), 0, 0, tiled=True)]
    all_to_all x2 -> x1, blocking collectives: 29.3 us -> 17.8 us  [body(): ends = lax.all_to_all(ends, 'rows', 0, 0, tiled=True)]
    ppermute x0 -> x3, starting transfers between devices: none -> 2.78 us  [body(): lax.ppermute(parts[step], 'lev', [(i, (i + step) % 4) for i in range(4)])]
    pallas_call x3 -> x2, Pallas kernels: 14.4 us -> 16.9 us  [the longest x1 11.3 us: inverse_x(): pl.pallas_call(inverse_x_kernel, grid_spec=pltpu.PrefetchScalarGridSpec(n...]
    convert_element_type x1 -> x0, other arithmetic: 1.32 us -> none  [body(): keep = (1 - solid).astype(F32)]
    unnamed x2 -> x8, local copies, waits for them, and re-layouts: 1.32 us -> 2.43 us
  transfers between devices with their start and end apart: 1 -> 4, of which waited for: 1 -> 1; matrix products, arithmetic and copies ran while one was open for 1% -> 1% of each run, Pallas kernels for 19% -> 25%
where the time goes in v2:
time: 95.8 us; the launch traced here: 95.3 us
  Pallas kernels  47.4 us (49%)
  blocking collectives  34.6 us (36%)
  starting transfers between devices  7.78 us (8%)
  waiting for transfers between devices  2.54 us (3%)
  local copies, waits for them, and re-layouts  2.43 us (3%)
    pallas_call x1, Pallas kernels, eigen(): pl.pallas_call(eigen_kernel, in_specs=[pl.BlockSpec(memory_space=pltpu.SM...  22.4 us
    all_to_all x1, blocking collectives, body(): ends = lax.all_to_all(ends, 'rows', 0, 0, tiled=True)  17.8 us
    all_to_all x1, blocking collectives, body(): lax.all_to_all(ends, ('rows', 'lev'), 0, 0, tiled=True)  16.8 us
    pallas_call x1, Pallas kernels, inverse_x(): pl.pallas_call(inverse_x_kernel, grid_spec=pltpu.PrefetchScalarGridSpec(n...  11.3 us
    pallas_call x1, Pallas kernels, forward_x(): pl.pallas_call(forward_x_kernel, grid=(rows // YB,), in_specs=[pl.BlockSp...  6.36 us
    pallas_call x1, Pallas kernels, level_solve(): pl.pallas_call(level_kernel, grid_spec=pltpu.PrefetchScalarGridSpec(num_s...  5.6 us
    all_to_all x1, starting transfers between devices, body(): gathered = lax.all_to_all(spectral, 'lev', 0, 0, tiled=True)  5 us
    ppermute x3, starting transfers between devices, body(): lax.ppermute(parts[step], 'lev', [(i, (i + step) % 4) for i in range(4)])  2.78 us
  transfers between devices with their start and end apart: 4, of which 1 were waited for; matrix products, arithmetic and copies ran while one was open for 1% of the time, Pallas kernels for 25%

profile of v2, /device:TPU:1, one launch (start us, length us, event | category | flops | bytes accessed | tf_op | source)
XLA Modules:
  0.0 95.3 jit_solution(3006000103102936988)
XLA Ops:
  0.0 6.4 %forward_x.1 = f32[4,4,64,512]{3,2,1,0:T(8,128)} custom-call(f32[64,4,2048]{2,1,0:T(4,128)} %src.1, s32[8,4,32]{2,1,0:T(4,128)} %keep.1, bf16[32,2048]{1,0:T(8,128)(2,1)} %constant.31.clone.spread, f32[16,128]{1,0:T(8,128)} %constant.32.clone.twiddle, bf16[256,256]{1,0:T(8,128)(2,1)} %constant.33.clone.fh, bf16[256,256]{1,0:T(8,128)(2,1)} %constant.34.clone.fl, ...), custom_call_target="tpu_custom_call" | custom-call | tf_op jit(solution)/shard_map/forward_x/pallas_call | solution.py:175
  6.4 5.0 %all-to-all-start = ((f32[4,4,64,512]{3,2,1,0:T(8,128)}), f32[4,4,64,512]{3,2,1,0:T(8,128)S(1)}, u32[]{:S(2)}, u32[]{:S(2)}) async-start(f32[4,4,64,512]{3,2,1,0:T(8,128)} %forward_x.1), calls=%async_computation | async-start | bytes 4194304 | tf_op jit(solution)/shard_map/all_to_all | solution.py:510
  11.4 22.4 %level_modes.1 = (f32[16,128]{1,0:T(8,128)}, f32[16,128]{1,0:T(8,128)}, bf16[128,128]{1,0:T(8,128)(2,1)}, bf16[128,128]{1,0:T(8,128)(2,1)}, bf16[256,128]{1,0:T(8,128)(2,1)}, /*index=5*/bf16[256,128]{1,0:T(8,128)(2,1)}) custom-call(f32[17]{0:T(128)} %coup.1), custom_call_target="tpu_custom_call" | custom-call | tf_op jit(solution)/shard_map/level_modes/pallas_call | solution.py:286
  33.7 0.6 pad_add_fusion.at
  34.3 2.5 %all-to-all-done = f32[4,4,64,512]{3,2,1,0:T(8,128)S(1)} async-done(((f32[4,4,64,512]{3,2,1,0:T(8,128)}), f32[4,4,64,512]{3,2,1,0:T(8,128)S(1)}, u32[]{:S(2)}, u32[]{:S(2)}) %all-to-all-start) | async-done | bytes 2097184 | tf_op jit(solution)/shard_map/all_to_all | solution.py:510
  36.8 0.0 copy-start
  36.8 1.3 %copy-done = f32[4,4,64,512]{3,2,1,0:T(8,128)} copy-done((f32[4,4,64,512]{3,2,1,0:T(8,128)}, f32[4,4,64,512]{3,2,1,0:T(8,128)S(1)}, u32[]{:S(2)}) %copy-start) | copy-done | bytes 2097176
  38.2 5.6 %level_solve.1 = (f32[4,64,512]{2,1,0:T(8,128)}, f32[4,64,512]{2,1,0:T(8,128)}, f32[4,64,512]{2,1,0:T(8,128)}, f32[4,64,512]{2,1,0:T(8,128)}, f32[32,4,128]{2,1,0:T(4,128)}) custom-call(s32[2]{0:T(128)} %pad_add_fusion.at, f32[16,64,512]{2,1,0:T(8,128)} %bitcast.5, bf16[128,128]{1,0:T(8,128)(2,1)} %get-tuple-element.16.w2h, ...), custom_call_target="tpu_custom_call" | custom-call | tf_op jit(solution)/shard_map/level_solve/pallas_call | solution.py:438
  43.8 0.3 collective-permute-start
  44.1 1.8 %collective-permute-start.1 = (f32[4,64,512]{2,1,0:T(8,128)}, f32[4,64,512]{2,1,0:T(8,128)S(1)}, u32[]{:S(2)}, u32[]{:S(2)}) collective-permute-start(f32[4,64,512]{2,1,0:T(8,128)} %get-tuple-element.23), channel_id=1, source_target_pairs={{0,2},{1,3},{2,0},{3,1},{4,6},{5,7},{6,4},{7,5},{8,10},{9,11},{10,... | collective-permute-start | bytes 1572872 | tf_op jit(solution)/shard_map/ppermute | solution.py:514
  45.8 0.7 collective-permute-start.2
  46.5 17.8 %all_to_all.15.ends = f32[32,4,128]{2,1,0:T(4,128)} all-to-all(f32[32,4,128]{2,1,0:T(4,128)} %get-tuple-element.25), channel_id=1, replica_groups=mesh['rows'=32,'lev'=4] {'rows'}, dimensions={0} | all-to-all | bytes 131072 | tf_op jit(solution)/shard_map/all_to_all | solution.py:515
  64.3 1.8 %section_carries.1 = f32[32,4,4,128]{3,2,1,0:T(4,128)} custom-call(s32[2]{0:T(128)} %pad_add_fusion.at, f32[32,4,128]{2,1,0:T(4,128)} %all_to_all.15.ends, f32[16,128]{1,0:T(8,128)} %get-tuple-element.20.lam, f32[8,256]{1,0:T(8,128)} %constant.37.clone.eig), custom_call_target="tpu_custom_call" | custom-call | tf_op jit(solution)/shard_map/section_carries/pallas_call | solution.py:492
  66.1 16.8 %all_to_all.16 = f32[128,4,128]{2,1,0:T(4,128)} all-to-all(f32[128,4,128]{2,1,0:T(4,128)} %bitcast.6), channel_id=1, replica_groups=mesh['rows'=32,'lev'=4] {'rows','lev'}, dimensions={0} | all-to-all | bytes 524288 | tf_op jit(solution)/shard_map/all_to_all | solution.py:517
  82.9 0.0 collective-permute-done.spec1
  82.9 0.0 copy-start.1
  82.9 0.0 collective-permute-done.1.spec2
  82.9 0.0 copy-start.2
  82.9 0.0 collective-permute-done.2.spec3
  83.0 0.0 copy-start.3
  83.0 0.8 copy-done.1
  83.7 0.2 copy-done.2
  83.9 0.1 copy-done.3
  84.1 11.3 %inverse_x.1 = f32[64,4,2048]{2,1,0:T(4,128)} custom-call(s32[2]{0:T(128)} %pad_add_fusion.at, f32[4,64,512]{2,1,0:T(8,128)} %get-tuple-element.21.spec0, f32[4,64,512]{2,1,0:T(8,128)} %copy-done.1, f32[4,64,512]{2,1,0:T(8,128)} %copy-done.2, f32[4,64,512]{2,1,0:T(8,128)} %copy-done.3, f32[2,16,4,4,128]{4,3,2,1,0:T(4,128)} %bitcast.7, ...), custom_call_target="tpu_custom_call" | custom-call | tf_op jit(solution)/shard_map/inverse_x/pallas_call | solution.py:378
Async XLA Ops:
  6.4 30.5 %all-to-all-start = ((f32[4,4,64,512]{3,2,1,0:T(8,128)}), f32[4,4,64,512]{3,2,1,0:T(8,128)S(1)}, u32[]{:S(2)}, u32[]{:S(2)}) async-start(f32[4,4,64,512]{3,2,1,0:T(8,128)} %forward_x.1), calls=%async_computation | async-start | bytes 4194304 | tf_op jit(solution)/shard_map/all_to_all | solution.py:510
  36.8 1.3 %copy-start = (f32[4,4,64,512]{3,2,1,0:T(8,128)}, f32[4,4,64,512]{3,2,1,0:T(8,128)S(1)}, u32[]{:S(2)}) copy-start(f32[4,4,64,512]{3,2,1,0:T(8,128)S(1)} %all-to-all-done) | copy-start | bytes 6291460
  43.8 39.2 %collective-permute-start = (f32[4,64,512]{2,1,0:T(8,128)}, f32[4,64,512]{2,1,0:T(8,128)S(1)}, u32[]{:S(2)}, u32[]{:S(2)}) collective-permute-start(f32[4,64,512]{2,1,0:T(8,128)} %get-tuple-element.22), channel_id=1, source_target_pairs={{0,1},{1,2},{2,3},{3,0},{4,5},{5,6},{6,7},{7,4},{8,9},{9,10},{10,1... | collective-permute-start | bytes 1572872 | tf_op jit(solution)/shard_map/ppermute | solution.py:514
  44.1 38.9 %collective-permute-start.1 = (f32[4,64,512]{2,1,0:T(8,128)}, f32[4,64,512]{2,1,0:T(8,128)S(1)}, u32[]{:S(2)}, u32[]{:S(2)}) collective-permute-start(f32[4,64,512]{2,1,0:T(8,128)} %get-tuple-element.23), channel_id=1, source_target_pairs={{0,2},{1,3},{2,0},{3,1},{4,6},{5,7},{6,4},{7,5},{8,10},{9,11},{10,... | collective-permute-start | bytes 1572872 | tf_op jit(solution)/shard_map/ppermute | solution.py:514
  45.8 37.1 %collective-permute-start.2 = (f32[4,64,512]{2,1,0:T(8,128)}, f32[4,64,512]{2,1,0:T(8,128)S(1)}, u32[]{:S(2)}, u32[]{:S(2)}) collective-permute-start(f32[4,64,512]{2,1,0:T(8,128)} %get-tuple-element.24), channel_id=1, source_target_pairs={{0,3},{1,0},{2,1},{3,2},{4,7},{5,4},{6,5},{7,6},{8,11},{9,8},{10,9... | collective-permute-start | bytes 1572872 | tf_op jit(solution)/shard_map/ppermute | solution.py:514
  82.9 0.8 copy-start.1
  82.9 1.0 %copy-start.2 = (f32[4,64,512]{2,1,0:T(8,128)}, f32[4,64,512]{2,1,0:T(8,128)S(1)}, u32[]{:S(2)}) copy-start(f32[4,64,512]{2,1,0:T(8,128)S(1)} %collective-permute-done.1.spec2) | copy-start | bytes 1572868
  83.0 1.1 %copy-start.3 = (f32[4,64,512]{2,1,0:T(8,128)}, f32[4,64,512]{2,1,0:T(8,128)S(1)}, u32[]{:S(2)}) copy-start(f32[4,64,512]{2,1,0:T(8,128)S(1)} %collective-permute-done.2.spec3) | copy-start | bytes 1572868

commit v3 on v2

--- a/solution.py
+++ b/solution.py
@@ -8,6 +8,7 @@
 from jax.experimental import pallas as pl
 from jax.experimental.pallas import tpu as pltpu
 from jax.sharding import PartitionSpec as P
+
 
 F32 = jnp.float32
 BF16 = jnp.bfloat16
@@ -18,7 +19,7 @@
 NZ = 16
 TURN = 2.0 * math.pi
 RESIDUES = (1, 5, 9, 13, 2, 10, 4)
-SWEEPS = 7
+SWEEPS = 12
 
 
 def split_host(table):
@@ -135,12 +136,15 @@
 YB = 16
 
 
-def forward_x_kernel(src, keep, spread, twiddle, fh, fl, eh, el, out, hi, lo):
-    open_cells = (1 - keep[...]).astype(F32).astype(BF16)
-    masks = mm(open_cells.reshape(keep.shape[0] * keep.shape[1], keep.shape[2]), spread[...])
+def forward_x_kernel(
+    at, src, solid, spread, twiddle, fh, fl, eh, el, out0, out1, out2, out3, hi, lo, hi0, lo0
+):
     levels = src.shape[1]
+    rows = levels * YB
+    open_cells = (1 - solid[...]).astype(F32).astype(BF16)
+    masks = mm(open_cells.reshape(solid.shape[0] * levels, solid.shape[2]), spread[...])
     for z in range(levels):
-        rows = []
+        cells = []
         for a in range(16):
             piece = src[:, z, a * LANES : (a + 1) * LANES]
             mask = masks[:, a * LANES : (a + 1) * LANES]
@@ -148,147 +152,152 @@
                 piece[8 * i : 8 * i + 8] * mask[i * levels + z : i * levels + z + 1]
                 for i in range(YB // 8)
             ]
-            rows.append(jnp.concatenate(pieces, 0))
-        real, comps = real16(rows)
-        blocks = [real]
-        for i in range(7):
-            blocks.append(cmul(comps[i], twiddle[i : i + 1, :], twiddle[8 + i : 9 + i, :]))
-        for i in range(8):
+            cells.append(jnp.concatenate(pieces, 0))
+        real, comps = real16(cells)
+        for part in range(2):
+            high, low = halves(real[part])
+            hi0[z * YB : (z + 1) * YB, part * LANES : (part + 1) * LANES] = high
+            lo0[z * YB : (z + 1) * YB, part * LANES : (part + 1) * LANES] = low
+        for i in range(1, 8):
+            block = cmul(comps[i - 1], twiddle[i - 1 : i, :], twiddle[7 + i : 8 + i, :])
+            slot = 2 * ((at[0] - i // 2) & 3) + i % 2
+            place = pl.multiple_of(slot * rows + z * YB, YB)
             for part in range(2):
-                high, low = halves(blocks[i][part])
-                at = pl.ds((i * levels + z) * YB, YB)
-                cols = pl.ds(part * LANES, LANES)
-                hi[at, cols] = high
-                lo[at, cols] = low
-    rows = levels * YB
-    first = mm3((hi[:rows, :], lo[:rows, :]), (eh[...], el[...]))
-    rest = mm3((hi[rows:, :], lo[rows:, :]), (fh[...], fl[...]))
-    for i in range(8):
-        value = first if i == 0 else rest[(i - 1) * rows : i * rows]
-        out[i // 2, :, :, (i % 2) * 256 : (i % 2) * 256 + 256] = value.reshape(levels, YB, 256)
-
-
-def forward_x(source, keep, consts):
+                high, low = halves(block[part])
+                hi[pl.ds(place, YB), part * LANES : (part + 1) * LANES] = high
+                lo[pl.ds(place, YB), part * LANES : (part + 1) * LANES] = low
+    outs = (out0, out1, out2, out3)
+    rest = mm3((hi[...], lo[...]), (fh[...], fl[...]))
+    for step in range(4):
+        for h in range(2):
+            value = rest[(2 * step + h) * rows : (2 * step + h + 1) * rows]
+            outs[step][:, :, h * 256 : h * 256 + 256] = value.reshape(levels, YB, 256)
+    first = mm3((hi0[...], lo0[...]), (eh[...], el[...])).reshape(levels, YB, 256)
+    for step in range(4):
+
+        @pl.when(at[0] == step)
+        def _(step=step):
+            outs[step][:, :, 0:256] = first
+
+
+def forward_x(at, source, solid, consts):
     rows, levels, cells = source.shape
     spread, twiddle, fh, fl, eh, el = consts
-    full2 = lambda shape: pl.BlockSpec(shape, lambda i: (0, 0))
+    whole = lambda value: pl.BlockSpec(value.shape, lambda i, at: (0,) * value.ndim)
     return pl.pallas_call(
         forward_x_kernel,
-        grid=(rows // YB,),
-        in_specs=[
-            pl.BlockSpec((YB, levels, cells), lambda i: (i, 0, 0)),
-            pl.BlockSpec((YB // BY, levels, cells // BX), lambda i: (i, 0, 0)),
-            full2(spread.shape),
-            full2(twiddle.shape),
-        ]
-        + [full2((256, 256))] * 4,
-        out_specs=pl.BlockSpec((4, levels, YB, 512), lambda i: (0, 0, i, 0)),
-        out_shape=jax.ShapeDtypeStruct((4, levels, rows, 512), F32),
-        scratch_shapes=[pltpu.VMEM((8 * levels * YB, 256), BF16)] * 2,
+        grid_spec=pltpu.PrefetchScalarGridSpec(
+            num_scalar_prefetch=1,
+            grid=(rows // YB,),
+            in_specs=[
+                pl.BlockSpec((YB, levels, cells), lambda i, at: (i, 0, 0)),
+                pl.BlockSpec((YB // BY, levels, cells // BX), lambda i, at: (i, 0, 0)),
+            ]
+            + [whole(value) for value in (spread, twiddle, fh, fl, eh, el)],
+            out_specs=[pl.BlockSpec((levels, YB, 512), lambda i, at: (0, i, 0))] * 4,
+            scratch_shapes=[pltpu.VMEM((8 * levels * YB, 256), BF16)] * 2
+            + [pltpu.VMEM((levels * YB, 256), BF16)] * 2,
+        ),
+        out_shape=[jax.ShapeDtypeStruct((levels, rows, 512), F32)] * 4,
         name="forward_x",
-    )(source, keep, spread, twiddle, fh, fl, eh, el)
+    )(at, source, solid, spread, twiddle, fh, fl, eh, el)
+
+
+def rsqrt(value):
+    root = lax.rsqrt(value)
+    return root * (1.5 - 0.5 * value * root * root)
 
 
 def eigen_kernel(coup, lam, modes, w2h, w2l, w4h, w4l):
     sub = lax.broadcasted_iota(jnp.int32, (8, LANES), 0)
-    lane = lax.broadcasted_iota(jnp.int32, (8, LANES), 1)
-    top = jnp.zeros((8, LANES), F32)
-    bottom = jnp.zeros((8, LANES), F32)
-    for i in range(NZ):
-        row = jnp.where(lane == i, coup[i] + coup[i + 1], 0.0)
-        if i > 0:
-            row = row - jnp.where(lane == i - 1, coup[i], 0.0)
-        if i < NZ - 1:
-            row = row - jnp.where(lane == i + 1, coup[i + 1], 0.0)
-        row = row + jnp.where(lane == NZ + i, 1.0, 0.0)
-        if i < 8:
-            top = jnp.where(sub == i, row, top)
-        else:
-            bottom = jnp.where(sub == i - 8, row, bottom)
-    near, far = lane == sub, lane == sub + 8
-    both = jnp.logical_or(near, far)
-    low_half = lane < 8
-    square = lane < NZ
-
-    def pick(mask, value):
-        return jnp.where(mask, value, 0.0)
-
-    def angle(p, q, a):
-        d = q - p
-        root = jnp.sqrt(d * d + 4.0 * a * a)
-        t = 2.0 * a / (jnp.abs(d) + root + 1e-30)
-        t = jnp.where(d >= 0.0, t, -t)
-        w = 1.0 + t * t
-        c = lax.rsqrt(w)
-        c = c * (1.5 - 0.5 * w * c * c)
-        return c, t * c
-
-    def partner(value):
-        return jnp.where(low_half, pltpu.roll(value, LANES - 8, 1), pltpu.roll(value, 8, 1))
-
-    def shuffle(value):
-        right = pltpu.roll(value, 1, 1)
-        left = pltpu.roll(value, LANES - 1, 1)
-        out = jnp.where(lane < 8, right, left)
-        out = jnp.where(lane == 1, pltpu.roll(value, LANES - 7, 1), out)
-        out = jnp.where(lane == 15, pltpu.roll(value, 8, 1), out)
-        return jnp.where(jnp.logical_or(lane == 0, lane >= NZ), value, out)
+    lane = lax.broadcasted_iota(jnp.int32, (8, LANES), 1) & (NZ - 1)
+    low = lane < 8
+    g = [jnp.zeros((8, LANES), F32), jnp.zeros((8, LANES), F32)]
+    link = jnp.zeros((8, LANES), F32)
+    for k in range(NZ):
+        pivot = coup[k] + coup[k + 1] - link * link
+        inverse = rsqrt(pivot)
+        here = lane == (k // 2 + 8 * (k % 2))
+        g[k // 8] = jnp.where(here & (sub == k % 8), pivot * inverse, g[k // 8])
+        link = -coup[k + 1] * inverse
+        if k < NZ - 1:
+            below = (k + 1) // 8
+            g[below] = jnp.where(here & (sub == (k + 1) % 8), link, g[below])
+    partners = [pltpu.roll(value, 8, 1) for value in g]
+
+    def total(first, second):
+        value = first + second
+        for shift in (4, 2, 1):
+            value = value + pltpu.roll(value, shift, 0)
+        return value
+
+    def right(value):
+        return pltpu.roll(value, 1, 1)
+
+    def left(value):
+        return pltpu.roll(value, LANES - 1, 1)
 
     def step(_, carry):
-        top, bottom = carry
-        c_s, s_s = angle(
-            jnp.sum(pick(near, top), 1, keepdims=True),
-            jnp.sum(pick(far, bottom), 1, keepdims=True),
-            jnp.sum(pick(far, top), 1, keepdims=True),
-        )
-        one = jnp.broadcast_to(jnp.sum(pick(both, top), 0, keepdims=True), (8, LANES))
-        two = jnp.broadcast_to(jnp.sum(pick(both, bottom), 0, keepdims=True), (8, LANES))
-        p = jnp.where(low_half, one, pltpu.roll(one, 8, 1))
-        q = jnp.where(low_half, pltpu.roll(two, LANES - 8, 1), two)
-        a = jnp.where(low_half, pltpu.roll(one, LANES - 8, 1), one)
-        c_l, s_l = angle(p, q, a)
-        c_l = jnp.where(square, c_l, 1.0)
-        s_l = jnp.where(low_half, -s_l, jnp.where(square, s_l, 0.0))
-        t1 = top * c_l + partner(top) * s_l
-        b1 = bottom * c_l + partner(bottom) * s_l
-        t1, b1 = shuffle(t1), shuffle(b1)
-        t2 = c_s * t1 - s_s * b1
-        b2 = s_s * t1 + c_s * b1
-        new_top = jnp.where(
-            sub == 0, t2, jnp.where(sub == 1, pltpu.roll(b2, 1, 0), pltpu.roll(t2, 1, 0))
-        )
-        new_bottom = jnp.where(sub == 7, t2, pltpu.roll(b2, 7, 0))
-        return new_top, new_bottom
-
-    top, bottom = lax.fori_loop(0, 15 * SWEEPS, step, (top, bottom))
-    lam[...] = jnp.concatenate(
-        [
-            jnp.broadcast_to(jnp.sum(pick(near, top), 1, keepdims=True), (8, LANES)),
-            jnp.broadcast_to(jnp.sum(pick(far, bottom), 1, keepdims=True), (8, LANES)),
-        ],
-        0,
-    )
-    rows = jnp.concatenate([top, bottom], 0)
-    modes[...] = pltpu.roll(rows, LANES - NZ, 1)
-    rows = jnp.concatenate([rows] * 8, 0)
-    src = lax.broadcasted_iota(jnp.int32, (LANES, LANES), 0)
-    dst = lax.broadcasted_iota(jnp.int32, (LANES, LANES), 1)
-    expand = (src == dst // 8 + NZ).astype(F32)
-    wide = jnp.dot(rows, expand, precision=lax.Precision.HIGHEST, preferred_element_type=F32)
-    w2 = jnp.where(src // NZ == dst % 8, wide, 0.0)
-    w2h[...], w2l[...] = halves(w2)
-    w4 = w2.T
-    w4h[...], w4l[...] = halves(jnp.concatenate([w4, w4], 0))
+        g0, g1, p0, p1, worst = carry
+        own = total(g0 * g0, g1 * g1)
+        other = total(p0 * p0, p1 * p1)
+        a = total(g0 * p0, g1 * p1)
+        d = other - own
+        w = d * d + 4.0 * a * a
+        h = rsqrt(w)
+        x = 0.5 + 0.5 * jnp.abs(d) * h
+        y = rsqrt(x)
+        positive = (d > 0.0) | ((d == 0.0) & low)
+        turn = a * h * y
+        still = w == 0.0
+        c = jnp.where(still, 1.0, x * y)
+        turn = jnp.where(still, 0.0, jnp.where(positive, turn, -turn))
+        worst = jnp.maximum(worst, jnp.where(still, 0.0, a * a / (own * other)))
+        out = []
+        for value, partner in ((g0, p0), (g1, p1)):
+            mine = c * value - turn * partner
+            theirs = c * partner + turn * value
+            rising = right(jnp.where(lane == 0, theirs, mine))
+            new = jnp.where(low, rising, jnp.where(lane == 15, theirs, left(mine)))
+            new = jnp.where(lane == 0, mine, new)
+            falling = right(jnp.where(lane == 8, mine, theirs))
+            new_partner = jnp.where(low, jnp.where(lane == 7, mine, left(theirs)), falling)
+            new_partner = jnp.where(lane == 8, theirs, new_partner)
+            out.append((new, new_partner))
+        return out[0][0], out[1][0], out[0][1], out[1][1], worst
+
+    def sweep(carry):
+        count, _, *state = carry
+        state = lax.fori_loop(0, 15, step, (*state, jnp.zeros((8, LANES), F32)))
+        return (count + 1, jnp.max(state[4]), *state[:4])
+
+    def unfinished(carry):
+        return (carry[0] < SWEEPS) & (carry[1] > 1e-7)
+
+    state = (jnp.int32(0), jnp.float32(1.0), g[0], g[1], partners[0], partners[1])
+    _, _, g0, g1, _, _ = lax.while_loop(unfinished, sweep, state)
+    square = total(g0 * g0, g1 * g1)
+    inverse = rsqrt(square)
+    vectors = jnp.concatenate([g0 * inverse, g1 * inverse], 0)
+    lam[...] = jnp.concatenate([square] * NZ, 0).T[:NZ]
+    modes[...] = jnp.concatenate([vectors] * 8, 0).T[:NZ]
+    wide = [jnp.broadcast_to(vectors[z : z + 1], (8, LANES)) for z in range(NZ)]
+    row = lax.broadcasted_iota(jnp.int32, (LANES, LANES), 0)
+    col = lax.broadcasted_iota(jnp.int32, (LANES, LANES), 1)
+    for section in range(4):
+        order = [wide[(z + 4 * section) % NZ] for z in range(NZ)]
+        w4 = jnp.where(row % 8 == col // NZ, jnp.concatenate(order, 0), 0.0)
+        w4h[section], w4l[section] = halves(w4)
+        w2h[section], w2l[section] = halves(w4.T)
 
 
 def eigen(couplings):
-    matrix = jax.ShapeDtypeStruct((LANES, LANES), BF16)
+    table = jax.ShapeDtypeStruct((NZ, LANES), F32)
+    matrix = jax.ShapeDtypeStruct((4, LANES, LANES), BF16)
     return pl.pallas_call(
         eigen_kernel,
         in_specs=[pl.BlockSpec(memory_space=pltpu.SMEM)],
-        out_shape=[jax.ShapeDtypeStruct((NZ, LANES), F32)] * 2
-        + [matrix] * 2
-        + [jax.ShapeDtypeStruct((2 * LANES, LANES), BF16)] * 2,
+        out_shape=[table, table, matrix, matrix, matrix, matrix],
         name="level_modes",
     )(couplings)
 
@@ -399,18 +408,33 @@
     )(at, *specs, ends, modes, lam, eig, twiddle, fh, fl, eh, el)
 
 
-def level_kernel(at, x, w2h, w2l, w4h, w4l, lam, eig, out0, out1, out2, out3, ends, f, work):
+def ends_kernel(at, x0, x1, x2, x3, wh, wl, lam, eig, f, ends):
     h = pl.program_id(0)
-    rows = x.shape[1]
-    w2 = (w2h[...], w2l[...])
-    turned = pl.ds(pl.multiple_of(at[0] * 32, 32), LANES)
-    w4 = (w4h[turned, :], w4l[turned, :])
+    rows = x0.shape[1]
+    w = (wh[at[0]], wl[at[0]])
+    e = eig[pl.ds(at[0] * 2 + h, 1), :]
+    r, _ = decay(lam[:, 0:1], e)
+    for o in range(rows // 8):
+        block = [x[:, 8 * o : 8 * o + 8, :].reshape(32, 256) for x in (x0, x1, x2, x3)]
+        value = mm3(w, halves(jnp.concatenate(block, 0)))
+        f[8 * o : 8 * o + 8, :, :] = value.reshape(8, NZ, 256)
+    up = jnp.zeros((NZ, 256), F32)
+    down = jnp.zeros((NZ, 256), F32)
+    for y in range(rows):
+        up = f[y] + r * up
+        down = f[rows - 1 - y] + r * down
+    ends[:, 0, :] = up[:, :LANES]
+    ends[:, 1, :] = up[:, LANES:]
+    ends[:, 2, :] = down[:, :LANES]
+    ends[:, 3, :] = down[:, LANES:]
+
+
+def solve_kernel(at, f, wh, wl, lam, eig, out0, out1, out2, out3, work):
+    h = pl.program_id(0)
+    rows = f.shape[0]
+    w = (wh[at[0]], wl[at[0]])
     e = eig[pl.ds(at[0] * 2 + h, 1), :]
     r, gain = decay(lam[:, 0:1], e)
-    for o in range(rows // 8):
-        block = x[:, 8 * o : 8 * o + 8, :].reshape(LANES, 256)
-        value = mm3(w2, halves(block))
-        f[8 * o : 8 * o + 8, :, :] = value.reshape(8, NZ, 256)
     up = jnp.zeros((NZ, 256), F32)
     down = jnp.zeros((NZ, 256), F32)
     for y in range(rows):
@@ -420,38 +444,52 @@
     for y in reversed(range(rows)):
         down = f[y] + r * down
         work[y] = (work[y] + down) * gain
-    ends[:, 0, :] = up[:, :LANES]
-    ends[:, 1, :] = up[:, LANES:]
-    ends[:, 2, :] = down[:, :LANES]
-    ends[:, 3, :] = down[:, LANES:]
     for o in range(rows // 8):
         block = work[8 * o : 8 * o + 8].reshape(LANES, 256)
-        value = mm3(w4, halves(block))
+        value = mm3(w, halves(block))
         for step, out in enumerate((out0, out1, out2, out3)):
             out[:, 8 * o : 8 * o + 8, :] = value[32 * step : 32 * step + 32].reshape(4, 8, 256)
 
 
-def level_solve(at, x, weights, lam, eig):
-    _, rows, width = x.shape
-    whole = lambda shape: pl.BlockSpec(shape, lambda h, at: (0,) * len(shape))
-    field = pl.BlockSpec((NZ, rows, 256), lambda h, at: (0, 0, h))
+def level_ends(at, xs, wh, wl, lam, eig):
+    _, rows, width = xs[0].shape
+    whole = lambda value: pl.BlockSpec(value.shape, lambda h, at: (0,) * value.ndim)
     return pl.pallas_call(
-        level_kernel,
+        ends_kernel,
         grid_spec=pltpu.PrefetchScalarGridSpec(
             num_scalar_prefetch=1,
             grid=(width // 256,),
-            in_specs=[field]
-            + [whole((LANES, LANES))] * 2
-            + [whole((2 * LANES, LANES))] * 2
-            + [whole((NZ, LANES)), whole((8, 256))],
-            out_specs=[pl.BlockSpec((4, rows, 256), lambda h, at: (0, 0, h))] * 4
-            + [pl.BlockSpec((NZ, 4, LANES), lambda h, at: (h, 0, 0))],
-            scratch_shapes=[pltpu.VMEM((rows, NZ, 256), F32)] * 2,
+            in_specs=[pl.BlockSpec((4, rows, 256), lambda h, at: (0, 0, h))] * 4
+            + [whole(value) for value in (wh, wl, lam, eig)],
+            out_specs=[
+                pl.BlockSpec((rows, NZ, 256), lambda h, at: (0, 0, h)),
+                pl.BlockSpec((NZ, 4, LANES), lambda h, at: (h, 0, 0)),
+            ],
         ),
-        out_shape=[jax.ShapeDtypeStruct((4, rows, width), F32)] * 4
-        + [jax.ShapeDtypeStruct((2 * NZ, 4, LANES), F32)],
+        out_shape=[
+            jax.ShapeDtypeStruct((rows, NZ, width), F32),
+            jax.ShapeDtypeStruct((2 * NZ, 4, LANES), F32),
+        ],
+        name="level_ends",
+    )(at, *xs, wh, wl, lam, eig)
+
+
+def level_solve(at, f, wh, wl, lam, eig):
+    rows, _, width = f.shape
+    whole = lambda value: pl.BlockSpec(value.shape, lambda h, at: (0,) * value.ndim)
+    return pl.pallas_call(
+        solve_kernel,
+        grid_spec=pltpu.PrefetchScalarGridSpec(
+            num_scalar_prefetch=1,
+            grid=(width // 256,),
+            in_specs=[pl.BlockSpec((rows, NZ, 256), lambda h, at: (0, 0, h))]
+            + [whole(value) for value in (wh, wl, lam, eig)],
+            out_specs=[pl.BlockSpec((4, rows, 256), lambda h, at: (0, 0, h))] * 4,
+            scratch_shapes=[pltpu.VMEM((rows, NZ, 256), F32)],
+        ),
+        out_shape=[jax.ShapeDtypeStruct((4, rows, width), F32)] * 4,
         name="level_solve",
-    )(at, x, *weights, lam, eig)
+    )(at, f, wh, wl, lam, eig)
 
 
 def carry_kernel(at, ends, lam, eig, out):
@@ -497,8 +535,11 @@
     )(at, ends, lam, eig)
 
 
+def shift(value, step):
+    return lax.ppermute(value, "lev", [(i, (i + step) % 4) for i in range(4)])
+
+
 def body(source, solid, couplings):
-    rows, levels, _ = source.shape
     full, edge, twiddle, eig, spread = host_tables()
     fh, fl = split_host(full)
     eh, el = split_host(edge)
@@ -506,13 +547,12 @@
     eth, etl = split_host(edge.T)
     at = jnp.stack([lax.axis_index("lev"), lax.axis_index("rows")]).astype(jnp.int32)
     lam, modes, w2h, w2l, w4h, w4l = eigen(couplings)
-    spectral = forward_x(source, solid, (spread, twiddle, fh, fl, eh, el))
-    gathered = lax.all_to_all(spectral, "lev", 0, 0, tiled=True)
-    *parts, ends = level_solve(at, gathered.reshape(NZ, rows, 512), (w2h, w2l, w4h, w4l), lam, eig)
-    specs = [parts[0]]
-    for step in range(1, 4):
-        specs.append(lax.ppermute(parts[step], "lev", [(i, (i + step) % 4) for i in range(4)]))
+    parts = forward_x(at, source, solid, (spread, twiddle, fh, fl, eh, el))
+    xs = [parts[0]] + [shift(parts[step], -step) for step in (1, 2, 3)]
+    f, ends = level_ends(at, xs, w2h, w2l, lam, eig)
     ends = lax.all_to_all(ends, "rows", 0, 0, tiled=True)
+    parts = level_solve(at, f, w4h, w4l, lam, eig)
+    specs = [parts[0]] + [shift(parts[step], step) for step in (1, 2, 3)]
     ends = carries(at, ends, lam, eig).reshape(128, 4, LANES)
     ends = lax.all_to_all(ends, ("rows", "lev"), 0, 0, tiled=True).reshape(2, NZ, 4, 4, LANES)
     return inverse_x(at, specs, ends, modes, lam, eig, (twiddle, fth, ftl, eth, etl))

time: 95.8 us -> 98.7 us (1.030)
  waiting for transfers between devices: 2.54 us -> 14.9 us
  Pallas kernels: 47.4 us -> 40.3 us
  blocking collectives: 34.6 us -> 33.1 us
    ppermute x3 -> x6, waiting for transfers between devices: 0.01 us -> 14.9 us  [shift(): return lax.ppermute(value, 'lev', [(i, (i + step) % 4) for i in range(4)])]
    pallas_call x1, Pallas kernels: 22.4 us -> 10.9 us  [eigen(): pl.pallas_call(eigen_kernel, in_specs=[pl.BlockSpec(memory_space=pltpu.SM...]
    all_to_all x1 -> x0, starting transfers between devices: 5 us -> none  [body(): gathered = lax.all_to_all(spectral, 'lev', 0, 0, tiled=True)]
    ppermute x3 -> x6, starting transfers between devices: 2.78 us -> 7.32 us  [shift(): return lax.ppermute(value, 'lev', [(i, (i + step) % 4) for i in range(4)])]
    pallas_call x2 -> x3, Pallas kernels: 12 us -> 16.4 us  [the longest x1 7.25 us: forward_x(): pl.pallas_call(forward_x_kernel, grid_spec=pltpu.PrefetchScalarGridSpec(n...]
    all_to_all x1 -> x0, waiting for transfers between devices: 2.53 us -> none  [body(): gathered = lax.all_to_all(spectral, 'lev', 0, 0, tiled=True)]
    all_to_all x1, blocking collectives: 17.8 us -> 16.3 us  [body(): ends = lax.all_to_all(ends, 'rows', 0, 0, tiled=True)]
    unnamed x8 -> x14, local copies, waits for them, and re-layouts: 2.43 us -> 1.96 us
  transfers between devices with their start and end apart: 4 -> 6, of which waited for: 1 -> 2; matrix products, arithmetic and copies ran while one was open for 1% -> 0% of each run, Pallas kernels for 25% -> 13%
where the time goes in v3:
time: 98.7 us; the launch traced here: 98.3 us
  Pallas kernels  40.3 us (41%)
  blocking collectives  33.1 us (34%)
  waiting for transfers between devices  14.9 us (15%)
  starting transfers between devices  7.32 us (7%)
  local copies, waits for them, and re-layouts  1.96 us (2%)
    all_to_all x1, blocking collectives, body(): lax.all_to_all(ends, ('rows', 'lev'), 0, 0, tiled=True)  16.9 us
    all_to_all x1, blocking collectives, body(): ends = lax.all_to_all(ends, 'rows', 0, 0, tiled=True)  16.3 us
    ppermute x6, waiting for transfers between devices, shift(): return lax.ppermute(value, 'lev', [(i, (i + step) % 4) for i in range(4)])  14.9 us
    pallas_call x1, Pallas kernels, inverse_x(): pl.pallas_call(inverse_x_kernel, grid_spec=pltpu.PrefetchScalarGridSpec(n...  11.3 us
    pallas_call x1, Pallas kernels, eigen(): pl.pallas_call(eigen_kernel, in_specs=[pl.BlockSpec(memory_space=pltpu.SM...  10.9 us
    ppermute x6, starting transfers between devices, shift(): return lax.ppermute(value, 'lev', [(i, (i + step) % 4) for i in range(4)])  7.32 us
    pallas_call x1, Pallas kernels, forward_x(): pl.pallas_call(forward_x_kernel, grid_spec=pltpu.PrefetchScalarGridSpec(n...  7.25 us
    pallas_call x1, Pallas kernels, level_solve(): pl.pallas_call(solve_kernel, grid_spec=pltpu.PrefetchScalarGridSpec(num_s...  4.79 us
  transfers between devices with their start and end apart: 6, of which 2 were waited for; matrix products, arithmetic and copies ran while one was open for 0% of the time, Pallas kernels for 13%

profile of v3, /device:TPU:1, one launch (start us, length us, event | category | flops | bytes accessed | tf_op | source)
XLA Modules:
  0.0 98.3 jit_solution(7285117031449543187)
XLA Ops:
  0.0 0.6 pad_add_fusion.at
  0.6 7.2 %forward_x.1 = (f32[4,64,512]{2,1,0:T(8,128)}, f32[4,64,512]{2,1,0:T(8,128)}, f32[4,64,512]{2,1,0:T(8,128)}, f32[4,64,512]{2,1,0:T(8,128)}) custom-call(s32[2]{0:T(128)} %pad_add_fusion.at, f32[64,4,2048]{2,1,0:T(4,128)} %src.1, s32[8,4,32]{2,1,0:T(4,128)} %solid.1, bf16[32,2048]{1,0:T(8,128)(2,1)} %constant.31.clone.spread, ...), custom_call_target="tpu_custom_call" | custom-call | tf_op jit(solution)/shard_map/forward_x/pallas_call | solution.py:187
  7.8 3.6 %collective-permute-start = (f32[4,64,512]{2,1,0:T(8,128)}, f32[4,64,512]{2,1,0:T(8,128)S(1)}, u32[]{:S(2)}, u32[]{:S(2)}) collective-permute-start(f32[4,64,512]{2,1,0:T(8,128)} %get-tuple-element.22), channel_id=1, source_target_pairs={{0,3},{1,0},{2,1},{3,2},{4,7},{5,4},{6,5},{7,6},{8,11},{9,8},{10,9... | collective-permute-start | bytes 1572872 | tf_op jit(solution)/shard_map/ppermute | solution.py:539
  11.4 0.3 collective-permute-start.1
  11.8 0.7 collective-permute-start.2
  12.5 10.9 %level_modes.1 = (f32[16,128]{1,0:T(8,128)}, f32[16,128]{1,0:T(8,128)}, bf16[4,128,128]{2,1,0:T(8,128)(2,1)}, bf16[4,128,128]{2,1,0:T(8,128)(2,1)}, bf16[4,128,1...) custom-call(f32[17]{0:T(128)} %coup.1), custom_call_target="tpu_custom_call" | custom-call | tf_op jit(solution)/shard_map/level_modes/pallas_call | solution.py:297
  23.4 10.1 %collective-permute-done.x1 = f32[4,64,512]{2,1,0:T(8,128)S(1)} collective-permute-done((f32[4,64,512]{2,1,0:T(8,128)}, f32[4,64,512]{2,1,0:T(8,128)S(1)}, u32[]{:S(2)}, u32[]{:S(2)}) %collective-permute-start) | collective-permute-done | bytes 524320 | tf_op jit(solution)/shard_map/ppermute | solution.py:539
  33.5 0.0 copy-start
  33.5 0.0 collective-permute-done.1.x2
  33.5 0.0 copy-start.1
  33.5 4.8 %collective-permute-done.2.x3 = f32[4,64,512]{2,1,0:T(8,128)S(1)} collective-permute-done((f32[4,64,512]{2,1,0:T(8,128)}, f32[4,64,512]{2,1,0:T(8,128)S(1)}, u32[]{:S(2)}, u32[]{:S(2)}) %collective-permute-start.2) | collective-permute-done | bytes 524320 | tf_op jit(solution)/shard_map/ppermute | solution.py:539
  38.2 0.0 copy-done
  38.2 0.0 copy-done.1
  38.2 0.8 copy-done.2
  39.0 4.3 %level_ends.1 = (f32[64,16,512]{2,1,0:T(8,128)}, f32[32,4,128]{2,1,0:T(4,128)}) custom-call(s32[2]{0:T(128)} %pad_add_fusion.at, f32[4,64,512]{2,1,0:T(8,128)} %get-tuple-element.21.x0, f32[4,64,512]{2,1,0:T(8,128)} %copy-done, f32[4,64,512]{2,1,0:T(8,128)} %copy-done.1, f32[4,64,512]{2,1,0:T(8,128)} %copy-done.2, ...), custom_call_target="tpu_custom_call" | custom-call | tf_op jit(solution)/shard_map/level_ends/pallas_call | solution.py:457
  43.4 4.8 %level_solve.1 = (f32[4,64,512]{2,1,0:T(8,128)}, f32[4,64,512]{2,1,0:T(8,128)}, f32[4,64,512]{2,1,0:T(8,128)}, f32[4,64,512]{2,1,0:T(8,128)}) custom-call(s32[2]{0:T(128)} %pad_add_fusion.at, f32[64,16,512]{2,1,0:T(8,128)} %get-tuple-element.28.f, bf16[4,128,128]{2,1,0:T(8,128)(2,1)} %get-tuple-element.29.wh, bf16[4,128,128]{2,1,0:T(8,128)(2,1)} %get-tuple-element.30.wl, ...), custom_call_target="tpu_custom_call" | custom-call | tf_op jit(solution)/shard_map/level_solve/pallas_call | solution.py:480
  48.2 0.0 collective-permute-start.3
  48.2 0.5 collective-permute-start.4
  48.7 2.1 %collective-permute-start.5 = (f32[4,64,512]{2,1,0:T(8,128)}, f32[4,64,512]{2,1,0:T(8,128)S(1)}, u32[]{:S(2)}, u32[]{:S(2)}) collective-permute-start(f32[4,64,512]{2,1,0:T(8,128)} %get-tuple-element.34), channel_id=1, source_target_pairs={{0,3},{1,0},{2,1},{3,2},{4,7},{5,4},{6,5},{7,6},{8,11},{9,8},{10,9... | collective-permute-start | bytes 1572872 | tf_op jit(solution)/shard_map/ppermute | solution.py:539
  50.9 0.0 copy-done.6
  50.9 16.3 %all_to_all.10.ends = f32[32,4,128]{2,1,0:T(4,128)} all-to-all(f32[32,4,128]{2,1,0:T(4,128)S(1)} %copy-done.6), channel_id=1, replica_groups=mesh['rows'=32,'lev'=4] {'rows'}, dimensions={0} | all-to-all | bytes 131072 | tf_op jit(solution)/shard_map/all_to_all | solution.py:553
  67.1 1.8 %section_carries.1 = f32[32,4,4,128]{3,2,1,0:T(4,128)} custom-call(s32[2]{0:T(128)} %pad_add_fusion.at, f32[32,4,128]{2,1,0:T(4,128)} %all_to_all.10.ends, f32[16,128]{1,0:T(8,128)} %get-tuple-element.27.lam, f32[8,256]{1,0:T(8,128)} %constant.37.clone.eig), custom_call_target="tpu_custom_call" | custom-call | tf_op jit(solution)/shard_map/section_carries/pallas_call | solution.py:530
  68.9 16.9 %all_to_all.11 = f32[128,4,128]{2,1,0:T(4,128)} all-to-all(f32[128,4,128]{2,1,0:T(4,128)} %bitcast.4), channel_id=1, replica_groups=mesh['rows'=32,'lev'=4] {'rows','lev'}, dimensions={0} | all-to-all | bytes 524288 | tf_op jit(solution)/shard_map/all_to_all | solution.py:557
  85.8 0.0 collective-permute-done.3.spec1
  85.8 0.0 collective-permute-done.4.spec2
  85.8 0.0 copy-start.4
  85.8 0.0 collective-permute-done.5.spec3
  85.8 0.0 copy-start.5
  85.9 0.8 copy-done.3
  86.6 0.2 copy-done.4
  86.9 0.1 copy-done.5
  87.0 11.3 %inverse_x.1 = f32[64,4,2048]{2,1,0:T(4,128)} custom-call(s32[2]{0:T(128)} %pad_add_fusion.at, f32[4,64,512]{2,1,0:T(8,128)} %get-tuple-element.31.spec0, f32[4,64,512]{2,1,0:T(8,128)} %copy-done.3, f32[4,64,512]{2,1,0:T(8,128)} %copy-done.4, f32[4,64,512]{2,1,0:T(8,128)} %copy-done.5, f32[2,16,4,4,128]{4,3,2,1,0:T(4,128)} %bitcast.5, ...), custom_call_target="tpu_custom_call" | custom-call | tf_op jit(solution)/shard_map/inverse_x/pallas_call | solution.py:387
  (3 shorter events, 0.0 us)
Async XLA Ops:
  7.8 25.6 %collective-permute-start = (f32[4,64,512]{2,1,0:T(8,128)}, f32[4,64,512]{2,1,0:T(8,128)S(1)}, u32[]{:S(2)}, u32[]{:S(2)}) collective-permute-start(f32[4,64,512]{2,1,0:T(8,128)} %get-tuple-element.22), channel_id=1, source_target_pairs={{0,3},{1,0},{2,1},{3,2},{4,7},{5,4},{6,5},{7,6},{8,11},{9,8},{10,9... | collective-permute-start | bytes 1572872 | tf_op jit(solution)/shard_map/ppermute | solution.py:539
  11.4 22.0 %collective-permute-start.1 = (f32[4,64,512]{2,1,0:T(8,128)}, f32[4,64,512]{2,1,0:T(8,128)S(1)}, u32[]{:S(2)}, u32[]{:S(2)}) collective-permute-start(f32[4,64,512]{2,1,0:T(8,128)} %get-tuple-element.23), channel_id=1, source_target_pairs={{0,2},{1,3},{2,0},{3,1},{4,6},{5,7},{6,4},{7,5},{8,10},{9,11},{10,... | collective-permute-start | bytes 1572872 | tf_op jit(solution)/shard_map/ppermute | solution.py:539
  11.8 26.4 %collective-permute-start.2 = (f32[4,64,512]{2,1,0:T(8,128)}, f32[4,64,512]{2,1,0:T(8,128)S(1)}, u32[]{:S(2)}, u32[]{:S(2)}) collective-permute-start(f32[4,64,512]{2,1,0:T(8,128)} %get-tuple-element.24), channel_id=1, source_target_pairs={{0,1},{1,2},{2,3},{3,0},{4,5},{5,6},{6,7},{7,4},{8,9},{9,10},{10,1... | collective-permute-start | bytes 1572872 | tf_op jit(solution)/shard_map/ppermute | solution.py:539
  33.5 4.8 %copy-start = (f32[4,64,512]{2,1,0:T(8,128)}, f32[4,64,512]{2,1,0:T(8,128)S(1)}, u32[]{:S(2)}) copy-start(f32[4,64,512]{2,1,0:T(8,128)S(1)} %collective-permute-done.x1) | copy-start | bytes 1572868
  33.5 4.8 %copy-start.1 = (f32[4,64,512]{2,1,0:T(8,128)}, f32[4,64,512]{2,1,0:T(8,128)S(1)}, u32[]{:S(2)}) copy-start(f32[4,64,512]{2,1,0:T(8,128)S(1)} %collective-permute-done.1.x2) | copy-start | bytes 1572868
  38.2 0.8 copy-start.2
  43.4 7.5 %copy-start.6 = (f32[32,4,128]{2,1,0:T(4,128)S(1)}, f32[32,4,128]{2,1,0:T(4,128)}, u32[]{:S(2)}) copy-start(f32[32,4,128]{2,1,0:T(4,128)} %get-tuple-element.35) | copy-start | bytes 196612
  48.2 37.6 %collective-permute-start.3 = (f32[4,64,512]{2,1,0:T(8,128)}, f32[4,64,512]{2,1,0:T(8,128)S(1)}, u32[]{:S(2)}, u32[]{:S(2)}) collective-permute-start(f32[4,64,512]{2,1,0:T(8,128)} %get-tuple-element.32), channel_id=1, source_target_pairs={{0,1},{1,2},{2,3},{3,0},{4,5},{5,6},{6,7},{7,4},{8,9},{9,10},{10,1... | collective-permute-start | bytes 1572872 | tf_op jit(solution)/shard_map/ppermute | solution.py:539
  48.2 37.6 %collective-permute-start.4 = (f32[4,64,512]{2,1,0:T(8,128)}, f32[4,64,512]{2,1,0:T(8,128)S(1)}, u32[]{:S(2)}, u32[]{:S(2)}) collective-permute-start(f32[4,64,512]{2,1,0:T(8,128)} %get-tuple-element.33), channel_id=1, source_target_pairs={{0,2},{1,3},{2,0},{3,1},{4,6},{5,7},{6,4},{7,5},{8,10},{9,11},{10,... | collective-permute-start | bytes 1572872 | tf_op jit(solution)/shard_map/ppermute | solution.py:539
  48.7 37.1 %collective-permute-start.5 = (f32[4,64,512]{2,1,0:T(8,128)}, f32[4,64,512]{2,1,0:T(8,128)S(1)}, u32[]{:S(2)}, u32[]{:S(2)}) collective-permute-start(f32[4,64,512]{2,1,0:T(8,128)} %get-tuple-element.34), channel_id=1, source_target_pairs={{0,3},{1,0},{2,1},{3,2},{4,7},{5,4},{6,5},{7,6},{8,11},{9,8},{10,9... | collective-permute-start | bytes 1572872 | tf_op jit(solution)/shard_map/ppermute | solution.py:539
  85.8 0.8 copy-start.3
  85.8 1.0 %copy-start.4 = (f32[4,64,512]{2,1,0:T(8,128)}, f32[4,64,512]{2,1,0:T(8,128)S(1)}, u32[]{:S(2)}) copy-start(f32[4,64,512]{2,1,0:T(8,128)S(1)} %collective-permute-done.4.spec2) | copy-start | bytes 1572868
  85.8 1.2 %copy-start.5 = (f32[4,64,512]{2,1,0:T(8,128)}, f32[4,64,512]{2,1,0:T(8,128)S(1)}, u32[]{:S(2)}) copy-start(f32[4,64,512]{2,1,0:T(8,128)S(1)} %collective-permute-done.5.spec3) | copy-start | bytes 1572868

commit v4 on v3

--- a/solution.py
+++ b/solution.py
@@ -8,7 +8,6 @@
 from jax.experimental import pallas as pl
 from jax.experimental.pallas import tpu as pltpu
 from jax.sharding import PartitionSpec as P
-
 
 F32 = jnp.float32
 BF16 = jnp.bfloat16
@@ -20,6 +19,13 @@
 TURN = 2.0 * math.pi
 RESIDUES = (1, 5, 9, 13, 2, 10, 4)
 SWEEPS = 12
+
+
+VMEM = pl.BlockSpec(memory_space=pltpu.VMEM)
+
+
+def grant(mebibytes):
+    return pltpu.CompilerParams(vmem_limit_bytes=mebibytes << 20)
 
 
 def split_host(table):
@@ -137,8 +143,10 @@
 
 
 def forward_x_kernel(
-    at, src, solid, spread, twiddle, fh, fl, eh, el, out0, out1, out2, out3, hi, lo, hi0, lo0
+    src, solid, spread, twiddle, fh, fl, eh, el, out0, out1, out2, out3, hi, lo, hi0, lo0
 ):
+    lev = lax.axis_index("lev")
+    band = pl.ds(pl.multiple_of(pl.program_id(0) * YB, YB), YB)
     levels = src.shape[1]
     rows = levels * YB
     open_cells = (1 - solid[...]).astype(F32).astype(BF16)
@@ -160,7 +168,7 @@
             lo0[z * YB : (z + 1) * YB, part * LANES : (part + 1) * LANES] = low
         for i in range(1, 8):
             block = cmul(comps[i - 1], twiddle[i - 1 : i, :], twiddle[7 + i : 8 + i, :])
-            slot = 2 * ((at[0] - i // 2) & 3) + i % 2
+            slot = 2 * ((lev - i // 2) & 3) + i % 2
             place = pl.multiple_of(slot * rows + z * YB, YB)
             for part in range(2):
                 high, low = halves(block[part])
@@ -171,36 +179,32 @@
     for step in range(4):
         for h in range(2):
             value = rest[(2 * step + h) * rows : (2 * step + h + 1) * rows]
-            outs[step][:, :, h * 256 : h * 256 + 256] = value.reshape(levels, YB, 256)
+            outs[step][:, band, h * 256 : h * 256 + 256] = value.reshape(levels, YB, 256)
     first = mm3((hi0[...], lo0[...]), (eh[...], el[...])).reshape(levels, YB, 256)
     for step in range(4):
 
-        @pl.when(at[0] == step)
+        @pl.when(lev == step)
         def _(step=step):
-            outs[step][:, :, 0:256] = first
-
-
-def forward_x(at, source, solid, consts):
+            outs[step][:, band, 0:256] = first
+
+
+def forward_x(source, solid, consts):
     rows, levels, cells = source.shape
-    spread, twiddle, fh, fl, eh, el = consts
-    whole = lambda value: pl.BlockSpec(value.shape, lambda i, at: (0,) * value.ndim)
     return pl.pallas_call(
         forward_x_kernel,
-        grid_spec=pltpu.PrefetchScalarGridSpec(
-            num_scalar_prefetch=1,
-            grid=(rows // YB,),
-            in_specs=[
-                pl.BlockSpec((YB, levels, cells), lambda i, at: (i, 0, 0)),
-                pl.BlockSpec((YB // BY, levels, cells // BX), lambda i, at: (i, 0, 0)),
-            ]
-            + [whole(value) for value in (spread, twiddle, fh, fl, eh, el)],
-            out_specs=[pl.BlockSpec((levels, YB, 512), lambda i, at: (0, i, 0))] * 4,
-            scratch_shapes=[pltpu.VMEM((8 * levels * YB, 256), BF16)] * 2
-            + [pltpu.VMEM((levels * YB, 256), BF16)] * 2,
-        ),
+        grid=(rows // YB,),
+        in_specs=[
+            pl.BlockSpec((YB, levels, cells), lambda i: (i, 0, 0)),
+            pl.BlockSpec((YB // BY, levels, cells // BX), lambda i: (i, 0, 0)),
+        ]
+        + [VMEM] * 6,
+        out_specs=[VMEM] * 4,
         out_shape=[jax.ShapeDtypeStruct((levels, rows, 512), F32)] * 4,
+        scratch_shapes=[pltpu.VMEM((8 * levels * YB, 256), BF16)] * 2
+        + [pltpu.VMEM((levels * YB, 256), BF16)] * 2,
+        compiler_params=grant(12),
         name="forward_x",
-    )(at, source, solid, spread, twiddle, fh, fl, eh, el)
+    )(source, solid, *consts)
 
 
 def rsqrt(value):
@@ -297,7 +301,9 @@
     return pl.pallas_call(
         eigen_kernel,
         in_specs=[pl.BlockSpec(memory_space=pltpu.SMEM)],
+        out_specs=[VMEM] * 6,
         out_shape=[table, table, matrix, matrix, matrix, matrix],
+        compiler_params=grant(4),
         name="level_modes",
     )(couplings)
 
@@ -316,12 +322,14 @@
 
 
 def inverse_x_kernel(
-    at, spec0, spec1, spec2, spec3, ends, modes, lam, eig, twiddle, fh, fl, eh, el,
+    spec0, spec1, spec2, spec3, ends, modes, lam, eig, twiddle, fh, fl, eh, el,
     out, hi, lo, above, below, eighth, steps,
 ):
     levels = spec0.shape[0]
     rows = levels * YB
+    lev = lax.axis_index("lev")
     i = pl.program_id(0)
+    band = pl.ds(pl.multiple_of(i * YB, YB), YB)
     blocks = 2 * pl.num_programs(0)
 
     @pl.when(i == 0)
@@ -346,9 +354,9 @@
     for o in range(2):
         steps[o] = powers(r8, 2 * i + o)
         steps[2 + o] = powers(r8, blocks - 1 - 2 * i - o)
-    first_level = at[0] * levels
+    first_level = lev * levels
     for step, spec in enumerate((spec0, spec1, spec2, spec3)):
-        l = (at[0] - step) & 3
+        l = (lev - step) & 3
         for part in range(4):
             t = 4 * l + part
             acc = [[None, None] for _ in range(levels)]
@@ -360,7 +368,7 @@
                         term = value * modes[k, first_level + z]
                         acc[z][o] = term if k == 0 else acc[z][o] + term
             for z in range(levels):
-                value = spec[z, :, part * LANES : (part + 1) * LANES] + jnp.concatenate(acc[z], 0)
+                value = spec[z, band, part * LANES : (part + 1) * LANES] + jnp.concatenate(acc[z], 0)
                 high, low = halves(value)
                 place = pl.multiple_of((2 * l + part // 2) * rows + z * YB, YB)
                 half = pl.ds((part % 2) * LANES, LANES)
@@ -380,124 +388,78 @@
             out[:, z, a * LANES : (a + 1) * LANES] = cells[a]
 
 
-def inverse_x(at, specs, ends, modes, lam, eig, consts):
+def inverse_x(specs, ends, modes, lam, eig, consts):
     levels, rows, _ = specs[0].shape
-    twiddle, fh, fl, eh, el = consts
-    whole = lambda value: pl.BlockSpec(value.shape, lambda i, at: (0,) * value.ndim)
     return pl.pallas_call(
         inverse_x_kernel,
-        grid_spec=pltpu.PrefetchScalarGridSpec(
-            num_scalar_prefetch=1,
-            grid=(rows // YB,),
-            in_specs=[pl.BlockSpec((levels, YB, 512), lambda i, at: (0, i, 0))] * 4
-            + [
-                whole(ends),
-                pl.BlockSpec(memory_space=pltpu.SMEM),
-                whole(lam),
-                whole(eig),
-                whole(twiddle),
-            ]
-            + [whole(fh)] * 4,
-            out_specs=pl.BlockSpec((YB, levels, N), lambda i, at: (i, 0, 0)),
-            scratch_shapes=[pltpu.VMEM((8 * levels * YB, 256), BF16)] * 2
-            + [pltpu.VMEM((16, NZ, 8, LANES), F32)] * 2
-            + [pltpu.VMEM((16, NZ, LANES), F32), pltpu.VMEM((4, 16, NZ, LANES), F32)],
-        ),
+        grid=(rows // YB,),
+        in_specs=[VMEM] * 5 + [pl.BlockSpec(memory_space=pltpu.SMEM)] + [VMEM] * 7,
+        out_specs=pl.BlockSpec((YB, levels, N), lambda i: (i, 0, 0)),
         out_shape=jax.ShapeDtypeStruct((rows, levels, N), F32),
+        scratch_shapes=[pltpu.VMEM((8 * levels * YB, 256), BF16)] * 2
+        + [pltpu.VMEM((16, NZ, 8, LANES), F32)] * 2
+        + [pltpu.VMEM((16, NZ, LANES), F32), pltpu.VMEM((4, 16, NZ, LANES), F32)],
+        compiler_params=grant(16),
         name="inverse_x",
-    )(at, *specs, ends, modes, lam, eig, twiddle, fh, fl, eh, el)
-
-
-def ends_kernel(at, x0, x1, x2, x3, wh, wl, lam, eig, f, ends):
-    h = pl.program_id(0)
+    )(*specs, ends, modes, lam, eig, *consts)
+
+
+def level_kernel(
+    x0, x1, x2, x3, w2h, w2l, w4h, w4l, lam, eig, out0, out1, out2, out3, ends, f, work
+):
+    lev = lax.axis_index("lev")
     rows = x0.shape[1]
-    w = (wh[at[0]], wl[at[0]])
-    e = eig[pl.ds(at[0] * 2 + h, 1), :]
-    r, _ = decay(lam[:, 0:1], e)
-    for o in range(rows // 8):
-        block = [x[:, 8 * o : 8 * o + 8, :].reshape(32, 256) for x in (x0, x1, x2, x3)]
-        value = mm3(w, halves(jnp.concatenate(block, 0)))
-        f[8 * o : 8 * o + 8, :, :] = value.reshape(8, NZ, 256)
-    up = jnp.zeros((NZ, 256), F32)
-    down = jnp.zeros((NZ, 256), F32)
-    for y in range(rows):
-        up = f[y] + r * up
-        down = f[rows - 1 - y] + r * down
-    ends[:, 0, :] = up[:, :LANES]
-    ends[:, 1, :] = up[:, LANES:]
-    ends[:, 2, :] = down[:, :LANES]
-    ends[:, 3, :] = down[:, LANES:]
-
-
-def solve_kernel(at, f, wh, wl, lam, eig, out0, out1, out2, out3, work):
-    h = pl.program_id(0)
-    rows = f.shape[0]
-    w = (wh[at[0]], wl[at[0]])
-    e = eig[pl.ds(at[0] * 2 + h, 1), :]
-    r, gain = decay(lam[:, 0:1], e)
-    up = jnp.zeros((NZ, 256), F32)
-    down = jnp.zeros((NZ, 256), F32)
-    for y in range(rows):
-        up = r * up
-        work[y] = up
-        up = up + f[y]
-    for y in reversed(range(rows)):
-        down = f[y] + r * down
-        work[y] = (work[y] + down) * gain
-    for o in range(rows // 8):
-        block = work[8 * o : 8 * o + 8].reshape(LANES, 256)
-        value = mm3(w, halves(block))
-        for step, out in enumerate((out0, out1, out2, out3)):
-            out[:, 8 * o : 8 * o + 8, :] = value[32 * step : 32 * step + 32].reshape(4, 8, 256)
-
-
-def level_ends(at, xs, wh, wl, lam, eig):
+    w2 = (w2h[lev], w2l[lev])
+    w4 = (w4h[lev], w4l[lev])
+    for h in range(x0.shape[2] // 256):
+        cols = pl.ds(h * 256, 256)
+        e = eig[pl.ds(lev * 2 + h, 1), :]
+        r, gain = decay(lam[:, 0:1], e)
+        for o in range(rows // 8):
+            block = [x[:, 8 * o : 8 * o + 8, cols].reshape(32, 256) for x in (x0, x1, x2, x3)]
+            value = mm3(w2, halves(jnp.concatenate(block, 0)))
+            f[8 * o : 8 * o + 8] = value.reshape(8, NZ, 256)
+        up = jnp.zeros((NZ, 256), F32)
+        down = jnp.zeros((NZ, 256), F32)
+        for y in range(rows):
+            up = r * up
+            work[y] = up
+            up = up + f[y]
+        for y in reversed(range(rows)):
+            down = f[y] + r * down
+            work[y] = (work[y] + down) * gain
+        place = pl.ds(h * NZ, NZ)
+        ends[place, 0, :] = up[:, :LANES]
+        ends[place, 1, :] = up[:, LANES:]
+        ends[place, 2, :] = down[:, :LANES]
+        ends[place, 3, :] = down[:, LANES:]
+        for o in range(rows // 8):
+            block = work[8 * o : 8 * o + 8].reshape(LANES, 256)
+            value = mm3(w4, halves(block))
+            for step, out in enumerate((out0, out1, out2, out3)):
+                out[:, 8 * o : 8 * o + 8, cols] = value[32 * step : 32 * step + 32].reshape(4, 8, 256)
+
+
+def level_solve(xs, weights, lam, eig):
     _, rows, width = xs[0].shape
-    whole = lambda value: pl.BlockSpec(value.shape, lambda h, at: (0,) * value.ndim)
     return pl.pallas_call(
-        ends_kernel,
-        grid_spec=pltpu.PrefetchScalarGridSpec(
-            num_scalar_prefetch=1,
-            grid=(width // 256,),
-            in_specs=[pl.BlockSpec((4, rows, 256), lambda h, at: (0, 0, h))] * 4
-            + [whole(value) for value in (wh, wl, lam, eig)],
-            out_specs=[
-                pl.BlockSpec((rows, NZ, 256), lambda h, at: (0, 0, h)),
-                pl.BlockSpec((NZ, 4, LANES), lambda h, at: (h, 0, 0)),
-            ],
-        ),
-        out_shape=[
-            jax.ShapeDtypeStruct((rows, NZ, width), F32),
-            jax.ShapeDtypeStruct((2 * NZ, 4, LANES), F32),
-        ],
-        name="level_ends",
-    )(at, *xs, wh, wl, lam, eig)
-
-
-def level_solve(at, f, wh, wl, lam, eig):
-    rows, _, width = f.shape
-    whole = lambda value: pl.BlockSpec(value.shape, lambda h, at: (0,) * value.ndim)
-    return pl.pallas_call(
-        solve_kernel,
-        grid_spec=pltpu.PrefetchScalarGridSpec(
-            num_scalar_prefetch=1,
-            grid=(width // 256,),
-            in_specs=[pl.BlockSpec((rows, NZ, 256), lambda h, at: (0, 0, h))]
-            + [whole(value) for value in (wh, wl, lam, eig)],
-            out_specs=[pl.BlockSpec((4, rows, 256), lambda h, at: (0, 0, h))] * 4,
-            scratch_shapes=[pltpu.VMEM((rows, NZ, 256), F32)],
-        ),
-        out_shape=[jax.ShapeDtypeStruct((4, rows, width), F32)] * 4,
+        level_kernel,
+        in_specs=[VMEM] * 10,
+        out_specs=[VMEM] * 5,
+        out_shape=[jax.ShapeDtypeStruct((4, rows, width), F32)] * 4
+        + [jax.ShapeDtypeStruct((2 * NZ, 4, LANES), F32)],
+        scratch_shapes=[pltpu.VMEM((rows, NZ, 256), F32)] * 2,
+        compiler_params=grant(12),
         name="level_solve",
-    )(at, f, wh, wl, lam, eig)
-
-
-def carry_kernel(at, ends, lam, eig, out):
+    )(*xs, *weights, lam, eig)
+
+
+def carry_kernel(ends, lam, eig, out):
     sections = ends.shape[0]
-    j = at[1]
+    j = lax.axis_index("rows")
     k = lax.rem(j, NZ)
     h = lax.div(j, NZ)
-    e = eig[pl.ds(at[0] * 2 + h, 1), :]
+    e = eig[pl.ds(lax.axis_index("lev") * 2 + h, 1), :]
     r, _ = decay(lam[pl.ds(k, 1), 0:1], e)
     for _ in range(6):
         r = r * r
@@ -526,13 +488,15 @@
         down = ends[s] + ratio * down
 
 
-def carries(at, ends, lam, eig):
+def carries(ends, lam, eig):
     return pl.pallas_call(
         carry_kernel,
-        in_specs=[pl.BlockSpec(memory_space=pltpu.SMEM)] + [pl.BlockSpec(memory_space=pltpu.VMEM)] * 3,
+        in_specs=[VMEM] * 3,
+        out_specs=VMEM,
         out_shape=jax.ShapeDtypeStruct((ends.shape[0], 4) + ends.shape[1:], F32),
+        compiler_params=grant(4),
         name="section_carries",
-    )(at, ends, lam, eig)
+    )(ends, lam, eig)
 
 
 def shift(value, step):
@@ -545,17 +509,15 @@
     eh, el = split_host(edge)
     fth, ftl = split_host(full.T)
     eth, etl = split_host(edge.T)
-    at = jnp.stack([lax.axis_index("lev"), lax.axis_index("rows")]).astype(jnp.int32)
     lam, modes, w2h, w2l, w4h, w4l = eigen(couplings)
-    parts = forward_x(at, source, solid, (spread, twiddle, fh, fl, eh, el))
+    parts = forward_x(source, solid, (spread, twiddle, fh, fl, eh, el))
     xs = [parts[0]] + [shift(parts[step], -step) for step in (1, 2, 3)]
-    f, ends = level_ends(at, xs, w2h, w2l, lam, eig)
+    *parts, ends = level_solve(xs, (w2h, w2l, w4h, w4l), lam, eig)
+    specs = [parts[0]] + [shift(parts[step], step) for step in (1, 2, 3)]
     ends = lax.all_to_all(ends, "rows", 0, 0, tiled=True)
-    parts = level_solve(at, f, w4h, w4l, lam, eig)
-    specs = [parts[0]] + [shift(parts[step], step) for step in (1, 2, 3)]
-    ends = carries(at, ends, lam, eig).reshape(128, 4, LANES)
+    ends = carries(ends, lam, eig).reshape(128, 4, LANES)
     ends = lax.all_to_all(ends, ("rows", "lev"), 0, 0, tiled=True).reshape(2, NZ, 4, 4, LANES)
-    return inverse_x(at, specs, ends, modes, lam, eig, (twiddle, fth, ftl, eth, etl))
+    return inverse_x(specs, ends, modes, lam, eig, (twiddle, fth, ftl, eth, etl))
 
 
 def solution(mesh):

time: 98.7 us -> 90.5 us (0.917)
  Pallas kernels: 40.3 us -> 26.7 us
  local copies, waits for them, and re-layouts: 1.96 us -> 7.56 us
    pallas_call x5 -> x4, Pallas kernels: 29.4 us -> 16.7 us  [the longest x1 9.72 us: inverse_x(): pl.pallas_call(inverse_x_kernel, grid=(rows // YB,), in_specs=[VMEM] * 5...]
    unnamed x14 -> x30, local copies, waits for them, and re-layouts: 1.96 us -> 7.56 us
  transfers between devices with their start and end apart: 6 -> 6, of which waited for: 2 -> 2; matrix products, arithmetic and copies ran while one was open for 0% -> 0% of each run, Pallas kernels for 13% -> 11%
where the time goes in v4:
time: 90.5 us; the launch traced here: 90.1 us
  blocking collectives  32.7 us (36%)
  Pallas kernels  26.7 us (30%)
  waiting for transfers between devices  15.6 us (17%)
  local copies, waits for them, and re-layouts  7.56 us (8%)
  starting transfers between devices  7.41 us (8%)
    all_to_all x1, blocking collectives, body(): lax.all_to_all(ends, ('rows', 'lev'), 0, 0, tiled=True)  16.6 us
    all_to_all x1, blocking collectives, body(): ends = lax.all_to_all(ends, 'rows', 0, 0, tiled=True)  16.1 us
    ppermute x6, waiting for transfers between devices, shift(): return lax.ppermute(value, 'lev', [(i, (i + step) % 4) for i in range(4)])  15.6 us
    pallas_call x1, Pallas kernels, eigen(): pl.pallas_call(eigen_kernel, in_specs=[pl.BlockSpec(memory_space=pltpu.SM...  9.99 us
    pallas_call x1, Pallas kernels, inverse_x(): pl.pallas_call(inverse_x_kernel, grid=(rows // YB,), in_specs=[VMEM] * 5...  9.72 us
    unnamed x30, local copies, waits for them, and re-layouts  7.56 us
    ppermute x6, starting transfers between devices, shift(): return lax.ppermute(value, 'lev', [(i, (i + step) % 4) for i in range(4)])  7.41 us
    pallas_call x1, Pallas kernels, forward_x(): pl.pallas_call(forward_x_kernel, grid=(rows // YB,), in_specs=[pl.BlockSp...  4.37 us
  transfers between devices with their start and end apart: 6, of which 2 were waited for; matrix products, arithmetic and copies ran while one was open for 0% of the time, Pallas kernels for 11%

profile of v4, /device:TPU:1, one launch (start us, length us, event | category | flops | bytes accessed | tf_op | source)
XLA Modules:
  0.0 90.1 jit_solution(13799486640250136975)
XLA Ops:
  0.0 1.6 %copy-done = f32[64,4,2048]{2,1,0:T(4,128)S(1)} copy-done((f32[64,4,2048]{2,1,0:T(4,128)S(1)}, f32[64,4,2048]{2,1,0:T(4,128)}, u32[]{:S(2)}) %copy-start) | copy-done | bytes 2097176
  1.6 0.9 %copy-done.5 = bf16[256,256]{1,0:T(8,128)(2,1)S(1)} copy-done((bf16[256,256]{1,0:T(8,128)(2,1)S(1)}, bf16[256,256]{1,0:T(8,128)(2,1)}, u32[]{:S(2)}) %copy-start.5) | copy-done | bytes 131096
  2.5 0.9 %copy-done.6 = bf16[256,256]{1,0:T(8,128)(2,1)S(1)} copy-done((bf16[256,256]{1,0:T(8,128)(2,1)S(1)}, bf16[256,256]{1,0:T(8,128)(2,1)}, u32[]{:S(2)}) %copy-start.6) | copy-done | bytes 131096
  3.4 0.9 %copy-done.7 = bf16[256,256]{1,0:T(8,128)(2,1)S(1)} copy-done((bf16[256,256]{1,0:T(8,128)(2,1)S(1)}, bf16[256,256]{1,0:T(8,128)(2,1)}, u32[]{:S(2)}) %copy-start.7) | copy-done | bytes 131096
  4.3 0.9 %copy-done.8 = bf16[256,256]{1,0:T(8,128)(2,1)S(1)} copy-done((bf16[256,256]{1,0:T(8,128)(2,1)S(1)}, bf16[256,256]{1,0:T(8,128)(2,1)}, u32[]{:S(2)}) %copy-start.8) | copy-done | bytes 131096
  5.2 0.9 %copy-done.9 = bf16[32,2048]{1,0:T(8,128)(2,1)S(1)} copy-done((bf16[32,2048]{1,0:T(8,128)(2,1)S(1)}, bf16[32,2048]{1,0:T(8,128)(2,1)}, u32[]{:S(2)}) %copy-start.9) | copy-done | bytes 131096
  6.1 0.7 copy-done.11
  6.8 0.7 copy-done.13
  7.5 4.4 %forward_x.1 = (f32[4,64,512]{2,1,0:T(8,128)S(1)}, f32[4,64,512]{2,1,0:T(8,128)S(1)}, f32[4,64,512]{2,1,0:T(8,128)S(1)}, f32[4,64,512]{2,1,0:T(8,128)S(1)}) custom-call(f32[64,4,2048]{2,1,0:T(4,128)S(1)} %copy-done, s32[8,4,32]{2,1,0:T(4,128)S(1)} %copy-done.13, bf16[32,2048]{1,0:T(8,128)(2,1)S(1)} %copy-done.9, f32[16,128]{1,0:T(8,128)S(1)} %copy-done.11, ...), custom_call_target="tpu_custom_call" | custom-call | tf_op jit(solution)/shard_map/forward_x/pallas_call | solution.py:193
  11.9 0.0 copy-start.1
  11.9 0.0 copy-start.2
  11.9 0.0 copy-start.3
  12.0 0.0 copy-start.4
  12.0 0.0 copy-start.12
  12.0 3.6 %collective-permute-start = (f32[4,64,512]{2,1,0:T(8,128)S(1)}, f32[4,64,512]{2,1,0:T(8,128)S(1)}, u32[]{:S(2)}, u32[]{:S(2)}) collective-permute-start(f32[4,64,512]{2,1,0:T(8,128)S(1)} %get-tuple-element.21), channel_id=1, source_target_pairs={{0,3},{1,0},{2,1},{3,2},{4,7},{5,4},{6,5},{7,6},{8,11},{9,8},{10,9... | collective-permute-start | bytes 1572872 | tf_op jit(solution)/shard_map/ppermute | solution.py:503
  15.6 0.3 collective-permute-start.1
  16.0 0.7 collective-permute-start.2
  16.6 10.0 %level_modes.1 = (f32[16,128]{1,0:T(8,128)S(1)}, f32[16,128]{1,0:T(8,128)S(1)}, bf16[4,128,128]{2,1,0:T(8,128)(2,1)S(1)}, bf16[4,128,128]{2,1,0:T(8,128)(2,1)S(1...) custom-call(f32[17]{0:T(128)S(1)} %copy-done.14), custom_call_target="tpu_custom_call" | custom-call | tf_op jit(solution)/shard_map/level_modes/pallas_call | solution.py:301
  26.6 10.7 %collective-permute-done.x1 = f32[4,64,512]{2,1,0:T(8,128)S(1)} collective-permute-done((f32[4,64,512]{2,1,0:T(8,128)S(1)}, f32[4,64,512]{2,1,0:T(8,128)S(1)}, u32[]{:S(2)}, u32[]{:S(2)}) %collective-permute-start) | collective-permute-done | bytes 524320 | tf_op jit(solution)/shard_map/ppermute | solution.py:503
  37.3 0.0 collective-permute-done.1.x2
  37.3 4.9 %collective-permute-done.2.x3 = f32[4,64,512]{2,1,0:T(8,128)S(1)} collective-permute-done((f32[4,64,512]{2,1,0:T(8,128)S(1)}, f32[4,64,512]{2,1,0:T(8,128)S(1)}, u32[]{:S(2)}, u32[]{:S(2)}) %collective-permute-start.2) | collective-permute-done | bytes 524320 | tf_op jit(solution)/shard_map/ppermute | solution.py:503
  42.2 2.4 %level_solve.1 = (f32[4,64,512]{2,1,0:T(8,128)S(1)}, f32[4,64,512]{2,1,0:T(8,128)S(1)}, f32[4,64,512]{2,1,0:T(8,128)S(1)}, f32[4,64,512]{2,1,0:T(8,128)S(1)}, f32[32,4,128]{2,1,0:T(4,128)S(1)}) custom-call(f32[4,64,512]{2,1,0:T(8,128)S(1)} %get-tuple-element.20.x0, f32[4,64,512]{2,1,0:T(8,128)S(1)} %collective-permute-done.x1, ...), custom_call_target="tpu_custom_call" | custom-call | tf_op jit(solution)/shard_map/level_solve/pallas_call | solution.py:445
  44.6 0.1 collective-permute-start.3
  44.7 0.4 collective-permute-start.4
  45.1 2.2 %collective-permute-start.5 = (f32[4,64,512]{2,1,0:T(8,128)S(1)}, f32[4,64,512]{2,1,0:T(8,128)S(1)}, u32[]{:S(2)}, u32[]{:S(2)}) collective-permute-start(f32[4,64,512]{2,1,0:T(8,128)S(1)} %get-tuple-element.32), channel_id=1, source_target_pairs={{0,3},{1,0},{2,1},{3,2},{4,7},{5,4},{6,5},{7,6},{8,11},{9,8},{10,9... | collective-permute-start | bytes 1572872 | tf_op jit(solution)/shard_map/ppermute | solution.py:503
  47.4 16.1 %all_to_all.10.ends = f32[32,4,128]{2,1,0:T(4,128)S(1)} all-to-all(f32[32,4,128]{2,1,0:T(4,128)S(1)} %get-tuple-element.33), channel_id=1, replica_groups=mesh['rows'=32,'lev'=4] {'rows'}, dimensions={0} | all-to-all | bytes 131072 | tf_op jit(solution)/shard_map/all_to_all | solution.py:517
  63.5 0.2 section_carries.1
  63.7 16.6 %all_to_all.11 = f32[128,4,128]{2,1,0:T(4,128)S(1)} all-to-all(f32[128,4,128]{2,1,0:T(4,128)S(1)} %bitcast.3), channel_id=1, replica_groups=mesh['rows'=32,'lev'=4] {'rows','lev'}, dimensions={0} | all-to-all | bytes 524288 | tf_op jit(solution)/shard_map/all_to_all | solution.py:519
  80.3 0.0 collective-permute-done.3.spec1
  80.3 0.0 collective-permute-done.4.spec2
  80.3 0.0 collective-permute-done.5.spec3
  80.4 9.7 %inverse_x.1 = f32[64,4,2048]{2,1,0:T(4,128)} custom-call(f32[4,64,512]{2,1,0:T(8,128)S(1)} %get-tuple-element.29.spec0, f32[4,64,512]{2,1,0:T(8,128)S(1)} %collective-permute-done.3.spec1, f32[4,64,512]{2,1,0:T(8,128)S(1)} %collective-permute-done.4.spec2, f32[4,64,512]{2,1,0:T(8,128)S(1)} %collective-permute-done.5.spec3, ...), custom_call_target="tpu_custom_call" | custom-call | tf_op jit(solution)/shard_map/inverse_x/pallas_call | solution.py:393
  (17 shorter events, 0.0 us)
Async XLA Ops:
  0.0 1.6 %copy-start = (f32[64,4,2048]{2,1,0:T(4,128)S(1)}, f32[64,4,2048]{2,1,0:T(4,128)}, u32[]{:S(2)}) copy-start(f32[64,4,2048]{2,1,0:T(4,128)} %src.1) | copy-start | bytes 6291460
  1.6 0.9 %copy-start.5 = (bf16[256,256]{1,0:T(8,128)(2,1)S(1)}, bf16[256,256]{1,0:T(8,128)(2,1)}, u32[]{:S(2)}) copy-start(bf16[256,256]{1,0:T(8,128)(2,1)} %constant.27.clone.el) | copy-start | bytes 393220
  2.5 0.9 %copy-start.6 = (bf16[256,256]{1,0:T(8,128)(2,1)S(1)}, bf16[256,256]{1,0:T(8,128)(2,1)}, u32[]{:S(2)}) copy-start(bf16[256,256]{1,0:T(8,128)(2,1)} %constant.26.clone.eh) | copy-start | bytes 393220
  3.4 0.9 %copy-start.7 = (bf16[256,256]{1,0:T(8,128)(2,1)S(1)}, bf16[256,256]{1,0:T(8,128)(2,1)}, u32[]{:S(2)}) copy-start(bf16[256,256]{1,0:T(8,128)(2,1)} %constant.25.clone.fl) | copy-start | bytes 393220
  4.3 0.9 %copy-start.8 = (bf16[256,256]{1,0:T(8,128)(2,1)S(1)}, bf16[256,256]{1,0:T(8,128)(2,1)}, u32[]{:S(2)}) copy-start(bf16[256,256]{1,0:T(8,128)(2,1)} %constant.24.clone.fh) | copy-start | bytes 393220
  5.2 0.9 %copy-start.9 = (bf16[32,2048]{1,0:T(8,128)(2,1)S(1)}, bf16[32,2048]{1,0:T(8,128)(2,1)}, u32[]{:S(2)}) copy-start(bf16[32,2048]{1,0:T(8,128)(2,1)} %constant.22.clone.spread) | copy-start | bytes 393220
  6.1 0.7 copy-start.11
  6.8 0.7 copy-start.13
  7.5 9.1 %copy-start.14 = (f32[17]{0:T(128)S(1)}, f32[17]{0:T(128)}, u32[]{:S(2)}) copy-start(f32[17]{0:T(128)} %coup.1) | copy-start | bytes 208
  7.5 34.7 %copy-start.10 = (f32[8,256]{1,0:T(8,128)S(1)}, f32[8,256]{1,0:T(8,128)}, u32[]{:S(2)}) copy-start(f32[8,256]{1,0:T(8,128)} %constant.28.clone.eig) | copy-start | bytes 24580
  11.9 68.4 %copy-start.1 = (bf16[256,256]{1,0:T(8,128)(2,1)S(1)}, bf16[256,256]{1,0:T(8,128)(2,1)}, u32[]{:S(2)}) copy-start(bf16[256,256]{1,0:T(8,128)(2,1)} %constant.32.clone.el) | copy-start | bytes 393220
  11.9 68.4 %copy-start.2 = (bf16[256,256]{1,0:T(8,128)(2,1)S(1)}, bf16[256,256]{1,0:T(8,128)(2,1)}, u32[]{:S(2)}) copy-start(bf16[256,256]{1,0:T(8,128)(2,1)} %constant.31.clone.eh) | copy-start | bytes 393220
  11.9 68.4 %copy-start.3 = (bf16[256,256]{1,0:T(8,128)(2,1)S(1)}, bf16[256,256]{1,0:T(8,128)(2,1)}, u32[]{:S(2)}) copy-start(bf16[256,256]{1,0:T(8,128)(2,1)} %constant.30.clone.fl) | copy-start | bytes 393220
  12.0 68.4 %copy-start.4 = (bf16[256,256]{1,0:T(8,128)(2,1)S(1)}, bf16[256,256]{1,0:T(8,128)(2,1)}, u32[]{:S(2)}) copy-start(bf16[256,256]{1,0:T(8,128)(2,1)} %constant.29.clone.fh) | copy-start | bytes 393220
  12.0 68.4 %copy-start.12 = (f32[16,128]{1,0:T(8,128)S(1)}, f32[16,128]{1,0:T(8,128)}, u32[]{:S(2)}) copy-start(f32[16,128]{1,0:T(8,128)} %constant.23.clone.twiddle) | copy-start | bytes 24580
  12.0 25.3 %collective-permute-start = (f32[4,64,512]{2,1,0:T(8,128)S(1)}, f32[4,64,512]{2,1,0:T(8,128)S(1)}, u32[]{:S(2)}, u32[]{:S(2)}) collective-permute-start(f32[4,64,512]{2,1,0:T(8,128)S(1)} %get-tuple-element.21), channel_id=1, source_target_pairs={{0,3},{1,0},{2,1},{3,2},{4,7},{5,4},{6,5},{7,6},{8,11},{9,8},{10,9... | collective-permute-start | bytes 1572872 | tf_op jit(solution)/shard_map/ppermute | solution.py:503
  15.6 21.7 %collective-permute-start.1 = (f32[4,64,512]{2,1,0:T(8,128)S(1)}, f32[4,64,512]{2,1,0:T(8,128)S(1)}, u32[]{:S(2)}, u32[]{:S(2)}) collective-permute-start(f32[4,64,512]{2,1,0:T(8,128)S(1)} %get-tuple-element.22), channel_id=1, source_target_pairs={{0,2},{1,3},{2,0},{3,1},{4,6},{5,7},{6,4},{7,5},{8,10},{9,11},{10,... | collective-permute-start | bytes 1572872 | tf_op jit(solution)/shard_map/ppermute | solution.py:503
  16.0 26.2 %collective-permute-start.2 = (f32[4,64,512]{2,1,0:T(8,128)S(1)}, f32[4,64,512]{2,1,0:T(8,128)S(1)}, u32[]{:S(2)}, u32[]{:S(2)}) collective-permute-start(f32[4,64,512]{2,1,0:T(8,128)S(1)} %get-tuple-element.23), channel_id=1, source_target_pairs={{0,1},{1,2},{2,3},{3,0},{4,5},{5,6},{6,7},{7,4},{8,9},{9,10},{10,1... | collective-permute-start | bytes 1572872 | tf_op jit(solution)/shard_map/ppermute | solution.py:503
  44.6 35.7 %collective-permute-start.3 = (f32[4,64,512]{2,1,0:T(8,128)S(1)}, f32[4,64,512]{2,1,0:T(8,128)S(1)}, u32[]{:S(2)}, u32[]{:S(2)}) collective-permute-start(f32[4,64,512]{2,1,0:T(8,128)S(1)} %get-tuple-element.30), channel_id=1, source_target_pairs={{0,1},{1,2},{2,3},{3,0},{4,5},{5,6},{6,7},{7,4},{8,9},{9,10},{10,1... | collective-permute-start | bytes 1572872 | tf_op jit(solution)/shard_map/ppermute | solution.py:503
  44.7 35.6 %collective-permute-start.4 = (f32[4,64,512]{2,1,0:T(8,128)S(1)}, f32[4,64,512]{2,1,0:T(8,128)S(1)}, u32[]{:S(2)}, u32[]{:S(2)}) collective-permute-start(f32[4,64,512]{2,1,0:T(8,128)S(1)} %get-tuple-element.31), channel_id=1, source_target_pairs={{0,2},{1,3},{2,0},{3,1},{4,6},{5,7},{6,4},{7,5},{8,10},{9,11},{10,... | collective-permute-start | bytes 1572872 | tf_op jit(solution)/shard_map/ppermute | solution.py:503
  45.1 35.2 %collective-permute-start.5 = (f32[4,64,512]{2,1,0:T(8,128)S(1)}, f32[4,64,512]{2,1,0:T(8,128)S(1)}, u32[]{:S(2)}, u32[]{:S(2)}) collective-permute-start(f32[4,64,512]{2,1,0:T(8,128)S(1)} %get-tuple-element.32), channel_id=1, source_target_pairs={{0,3},{1,0},{2,1},{3,2},{4,7},{5,4},{6,5},{7,6},{8,11},{9,8},{10,9... | collective-permute-start | bytes 1572872 | tf_op jit(solution)/shard_map/ppermute | solution.py:503

commit v5 on v4

--- a/solution.py
+++ b/solution.py
@@ -197,14 +197,14 @@
             pl.BlockSpec((YB, levels, cells), lambda i: (i, 0, 0)),
             pl.BlockSpec((YB // BY, levels, cells // BX), lambda i: (i, 0, 0)),
         ]
-        + [VMEM] * 6,
+        + [pl.BlockSpec(value.shape, lambda i: (0, 0)) for value in consts],
         out_specs=[VMEM] * 4,
         out_shape=[jax.ShapeDtypeStruct((levels, rows, 512), F32)] * 4,
         scratch_shapes=[pltpu.VMEM((8 * levels * YB, 256), BF16)] * 2
         + [pltpu.VMEM((levels * YB, 256), BF16)] * 2,
         compiler_params=grant(12),
         name="forward_x",
-    )(source, solid, *consts)
+    )(*[pltpu.with_memory_space_constraint(value, pltpu.HBM) for value in (source, solid, *consts)])
 
 
 def rsqrt(value):
@@ -323,7 +323,7 @@
 
 def inverse_x_kernel(
     spec0, spec1, spec2, spec3, ends, modes, lam, eig, twiddle, fh, fl, eh, el,
-    out, hi, lo, above, below, eighth, steps,
+    out, hi, lo, above, below, eighth, steps, shelf,
 ):
     levels = spec0.shape[0]
     rows = levels * YB
@@ -335,20 +335,27 @@
     @pl.when(i == 0)
     def _():
         b = lax.broadcasted_iota(jnp.int32, (8, LANES), 0)
+        odd, half, upper = [(b & bit) != 0 for bit in (1, 2, 4)]
+
+        def choose(mask, factor, start=1.0):
+            return jnp.where(mask, factor * start, start)
+
         for t in range(16):
             l, h, p = t // 4, (t // 2) % 2, t % 2
             e = eig[t // 2 : t // 2 + 1, p * LANES : (p + 1) * LANES]
             r, gain = decay(lam[:, 0:1], e)
             gain = gain * r
-            up = ends[h, :, l, p, :] * gain
-            down = ends[h, :, l, 2 + p, :] * gain
             r2 = r * r
             r4 = r2 * r2
             eighth[t] = r4 * r4
+            for n, value in enumerate(
+                (r, r2, r4, ends[h, :, l, p, :] * gain, ends[h, :, l, 2 + p, :] * gain)
+            ):
+                shelf[t, n] = value
             for k in range(NZ):
-                base = jnp.broadcast_to(r[k : k + 1], (8, LANES))
-                above[t, k] = powers(base, b) * up[k : k + 1]
-                below[t, k] = powers(base, 7 - b) * down[k : k + 1]
+                r1, r2, r4, up, down = [shelf[t, n, k : k + 1, :] for n in range(5)]
+                above[t, k] = choose(odd, r1, up) * (choose(half, r2) * choose(upper, r4))
+                below[t, k] = choose(~odd, r1, down) * (choose(~half, r2) * choose(~upper, r4))
 
     r8 = eighth[...]
     for o in range(2):
@@ -398,7 +405,8 @@
         out_shape=jax.ShapeDtypeStruct((rows, levels, N), F32),
         scratch_shapes=[pltpu.VMEM((8 * levels * YB, 256), BF16)] * 2
         + [pltpu.VMEM((16, NZ, 8, LANES), F32)] * 2
-        + [pltpu.VMEM((16, NZ, LANES), F32), pltpu.VMEM((4, 16, NZ, LANES), F32)],
+        + [pltpu.VMEM((16, NZ, LANES), F32), pltpu.VMEM((4, 16, NZ, LANES), F32)]
+        + [pltpu.VMEM((16, 5, NZ, LANES), F32)],
         compiler_params=grant(16),
         name="inverse_x",
     )(*specs, ends, modes, lam, eig, *consts)

time: 90.5 us -> 84.1 us (0.929)
  local copies, waits for them, and re-layouts: 7.56 us -> 0.04 us
  Pallas kernels: 26.7 us -> 28 us
    unnamed x30 -> x14, local copies, waits for them, and re-layouts: 7.56 us -> 0.04 us
    pallas_call x1, Pallas kernels: 4.37 us -> 5.64 us  [forward_x(): pl.pallas_call(forward_x_kernel, grid=(rows // YB,), in_specs=[pl.BlockSp...]
  transfers between devices with their start and end apart: 6 -> 6, of which waited for: 2 -> 2; matrix products, arithmetic and copies ran while one was open for 0% -> 0% of each run, Pallas kernels for 11% -> 12%
where the time goes in v5:
time: 84.1 us; the launch traced here: 83.9 us
  blocking collectives  32.7 us (39%)
  Pallas kernels  28 us (33%)
  waiting for transfers between devices  15.6 us (19%)
  starting transfers between devices  7.4 us (9%)
    all_to_all x1, blocking collectives, body(): lax.all_to_all(ends, ('rows', 'lev'), 0, 0, tiled=True)  16.6 us
    all_to_all x1, blocking collectives, body(): ends = lax.all_to_all(ends, 'rows', 0, 0, tiled=True)  16.2 us
    ppermute x6, waiting for transfers between devices, shift(): return lax.ppermute(value, 'lev', [(i, (i + step) % 4) for i in range(4)])  15.6 us
    pallas_call x1, Pallas kernels, eigen(): pl.pallas_call(eigen_kernel, in_specs=[pl.BlockSpec(memory_space=pltpu.SM...  9.99 us
    pallas_call x1, Pallas kernels, inverse_x(): pl.pallas_call(inverse_x_kernel, grid=(rows // YB,), in_specs=[VMEM] * 5...  9.74 us
    ppermute x6, starting transfers between devices, shift(): return lax.ppermute(value, 'lev', [(i, (i + step) % 4) for i in range(4)])  7.4 us
    pallas_call x1, Pallas kernels, forward_x(): pl.pallas_call(forward_x_kernel, grid=(rows // YB,), in_specs=[pl.BlockSp...  5.64 us
    pallas_call x1, Pallas kernels, level_solve(): pl.pallas_call(level_kernel, in_specs=[VMEM] * 10, out_specs=[VMEM] * 5,...  2.4 us
  transfers between devices with their start and end apart: 6, of which 2 were waited for; matrix products, arithmetic and copies ran while one was open for 0% of the time, Pallas kernels for 12%

profile of v5, /device:TPU:1, one launch (start us, length us, event | category | flops | bytes accessed | tf_op | source)
XLA Modules:
  0.0 83.9 jit_solution(4516936458045819955)
XLA Ops:
  0.0 0.0 copy-start.4
  0.0 5.6 %forward_x.1 = (f32[4,64,512]{2,1,0:T(8,128)S(1)}, f32[4,64,512]{2,1,0:T(8,128)S(1)}, f32[4,64,512]{2,1,0:T(8,128)S(1)}, f32[4,64,512]{2,1,0:T(8,128)S(1)}) custom-call(f32[64,4,2048]{2,1,0:T(4,128)} %src.1, s32[8,4,32]{2,1,0:T(4,128)} %solid.1, bf16[32,2048]{1,0:T(8,128)(2,1)} %constant.22.clone.spread, f32[16,128]{1,0:T(8,128)} %constant.23.clone.twiddle, ...), custom_call_target="tpu_custom_call" | custom-call | tf_op jit(solution)/shard_map/forward_x/pallas_call | solution.py:193
  5.7 0.0 copy-start
  5.7 0.0 copy-start.1
  5.7 0.0 copy-start.2
  5.7 0.0 copy-start.3
  5.7 0.0 copy-start.5
  5.7 3.6 %collective-permute-start = (f32[4,64,512]{2,1,0:T(8,128)S(1)}, f32[4,64,512]{2,1,0:T(8,128)S(1)}, u32[]{:S(2)}, u32[]{:S(2)}) collective-permute-start(f32[4,64,512]{2,1,0:T(8,128)S(1)} %get-tuple-element.21), channel_id=1, source_target_pairs={{0,3},{1,0},{2,1},{3,2},{4,7},{5,4},{6,5},{7,6},{8,11},{9,8},{10,9... | collective-permute-start | bytes 1572872 | tf_op jit(solution)/shard_map/ppermute | solution.py:511
  9.3 0.3 collective-permute-start.1
  9.7 0.7 collective-permute-start.2
  10.4 0.0 copy-done.6
  10.4 10.0 %level_modes.1 = (f32[16,128]{1,0:T(8,128)S(1)}, f32[16,128]{1,0:T(8,128)S(1)}, bf16[4,128,128]{2,1,0:T(8,128)(2,1)S(1)}, bf16[4,128,128]{2,1,0:T(8,128)(2,1)S(1...) custom-call(f32[17]{0:T(128)S(1)} %copy-done.6), custom_call_target="tpu_custom_call" | custom-call | tf_op jit(solution)/shard_map/level_modes/pallas_call | solution.py:301
  20.4 10.7 %collective-permute-done.x1 = f32[4,64,512]{2,1,0:T(8,128)S(1)} collective-permute-done((f32[4,64,512]{2,1,0:T(8,128)S(1)}, f32[4,64,512]{2,1,0:T(8,128)S(1)}, u32[]{:S(2)}, u32[]{:S(2)}) %collective-permute-start) | collective-permute-done | bytes 524320 | tf_op jit(solution)/shard_map/ppermute | solution.py:511
  31.0 0.0 collective-permute-done.1.x2
  31.0 4.9 %collective-permute-done.2.x3 = f32[4,64,512]{2,1,0:T(8,128)S(1)} collective-permute-done((f32[4,64,512]{2,1,0:T(8,128)S(1)}, f32[4,64,512]{2,1,0:T(8,128)S(1)}, u32[]{:S(2)}, u32[]{:S(2)}) %collective-permute-start.2) | collective-permute-done | bytes 524320 | tf_op jit(solution)/shard_map/ppermute | solution.py:511
  35.9 0.0 copy-done.4
  35.9 2.4 %level_solve.1 = (f32[4,64,512]{2,1,0:T(8,128)S(1)}, f32[4,64,512]{2,1,0:T(8,128)S(1)}, f32[4,64,512]{2,1,0:T(8,128)S(1)}, f32[4,64,512]{2,1,0:T(8,128)S(1)}, f32[32,4,128]{2,1,0:T(4,128)S(1)}) custom-call(f32[4,64,512]{2,1,0:T(8,128)S(1)} %get-tuple-element.20.x0, f32[4,64,512]{2,1,0:T(8,128)S(1)} %collective-permute-done.x1, ...), custom_call_target="tpu_custom_call" | custom-call | tf_op jit(solution)/shard_map/level_solve/pallas_call | solution.py:453
  38.3 0.1 collective-permute-start.3
  38.4 0.4 collective-permute-start.4
  38.9 2.2 %collective-permute-start.5 = (f32[4,64,512]{2,1,0:T(8,128)S(1)}, f32[4,64,512]{2,1,0:T(8,128)S(1)}, u32[]{:S(2)}, u32[]{:S(2)}) collective-permute-start(f32[4,64,512]{2,1,0:T(8,128)S(1)} %get-tuple-element.32), channel_id=1, source_target_pairs={{0,3},{1,0},{2,1},{3,2},{4,7},{5,4},{6,5},{7,6},{8,11},{9,8},{10,9... | collective-permute-start | bytes 1572872 | tf_op jit(solution)/shard_map/ppermute | solution.py:511
  41.1 16.2 %all_to_all.10.ends = f32[32,4,128]{2,1,0:T(4,128)S(1)} all-to-all(f32[32,4,128]{2,1,0:T(4,128)S(1)} %get-tuple-element.33), channel_id=1, replica_groups=mesh['rows'=32,'lev'=4] {'rows'}, dimensions={0} | all-to-all | bytes 131072 | tf_op jit(solution)/shard_map/all_to_all | solution.py:525
  57.2 0.2 section_carries.1
  57.5 16.6 %all_to_all.11 = f32[128,4,128]{2,1,0:T(4,128)S(1)} all-to-all(f32[128,4,128]{2,1,0:T(4,128)S(1)} %bitcast.3), channel_id=1, replica_groups=mesh['rows'=32,'lev'=4] {'rows','lev'}, dimensions={0} | all-to-all | bytes 524288 | tf_op jit(solution)/shard_map/all_to_all | solution.py:527
  74.1 0.0 collective-permute-done.3.spec1
  74.1 0.0 collective-permute-done.4.spec2
  74.1 0.0 collective-permute-done.5.spec3
  74.1 0.0 copy-done
  74.1 0.0 copy-done.1
  74.1 0.0 copy-done.2
  74.1 0.0 copy-done.3
  74.1 0.0 copy-done.5
  74.1 9.7 %inverse_x.1 = f32[64,4,2048]{2,1,0:T(4,128)} custom-call(f32[4,64,512]{2,1,0:T(8,128)S(1)} %get-tuple-element.29.spec0, f32[4,64,512]{2,1,0:T(8,128)S(1)} %collective-permute-done.3.spec1, f32[4,64,512]{2,1,0:T(8,128)S(1)} %collective-permute-done.4.spec2, f32[4,64,512]{2,1,0:T(8,128)S(1)} %collective-permute-done.5.spec3, ...), custom_call_target="tpu_custom_call" | custom-call | tf_op jit(solution)/shard_map/inverse_x/pallas_call | solution.py:400
  (1 shorter events, 0.0 us)
Async XLA Ops:
  0.0 35.9 %copy-start.4 = (f32[8,256]{1,0:T(8,128)S(1)}, f32[8,256]{1,0:T(8,128)}, u32[]{:S(2)}) copy-start(f32[8,256]{1,0:T(8,128)} %constant.28.clone.eig) | copy-start | bytes 24580
  0.0 10.4 %copy-start.6 = (f32[17]{0:T(128)S(1)}, f32[17]{0:T(128)}, u32[]{:S(2)}) copy-start(f32[17]{0:T(128)} %coup.1) | copy-start | bytes 208
  5.7 68.4 %copy-start = (bf16[256,256]{1,0:T(8,128)(2,1)S(1)}, bf16[256,256]{1,0:T(8,128)(2,1)}, u32[]{:S(2)}) copy-start(bf16[256,256]{1,0:T(8,128)(2,1)} %constant.32.clone.el) | copy-start | bytes 393220
  5.7 68.4 %copy-start.1 = (bf16[256,256]{1,0:T(8,128)(2,1)S(1)}, bf16[256,256]{1,0:T(8,128)(2,1)}, u32[]{:S(2)}) copy-start(bf16[256,256]{1,0:T(8,128)(2,1)} %constant.31.clone.eh) | copy-start | bytes 393220
  5.7 68.4 %copy-start.2 = (bf16[256,256]{1,0:T(8,128)(2,1)S(1)}, bf16[256,256]{1,0:T(8,128)(2,1)}, u32[]{:S(2)}) copy-start(bf16[256,256]{1,0:T(8,128)(2,1)} %constant.30.clone.fl) | copy-start | bytes 393220
  5.7 68.4 %copy-start.3 = (bf16[256,256]{1,0:T(8,128)(2,1)S(1)}, bf16[256,256]{1,0:T(8,128)(2,1)}, u32[]{:S(2)}) copy-start(bf16[256,256]{1,0:T(8,128)(2,1)} %constant.29.clone.fh) | copy-start | bytes 393220
  5.7 68.4 %copy-start.5 = (f32[16,128]{1,0:T(8,128)S(1)}, f32[16,128]{1,0:T(8,128)}, u32[]{:S(2)}) copy-start(f32[16,128]{1,0:T(8,128)} %constant.23.clone.twiddle) | copy-start | bytes 24580
  5.7 25.3 %collective-permute-start = (f32[4,64,512]{2,1,0:T(8,128)S(1)}, f32[4,64,512]{2,1,0:T(8,128)S(1)}, u32[]{:S(2)}, u32[]{:S(2)}) collective-permute-start(f32[4,64,512]{2,1,0:T(8,128)S(1)} %get-tuple-element.21), channel_id=1, source_target_pairs={{0,3},{1,0},{2,1},{3,2},{4,7},{5,4},{6,5},{7,6},{8,11},{9,8},{10,9... | collective-permute-start | bytes 1572872 | tf_op jit(solution)/shard_map/ppermute | solution.py:511
  9.3 21.7 %collective-permute-start.1 = (f32[4,64,512]{2,1,0:T(8,128)S(1)}, f32[4,64,512]{2,1,0:T(8,128)S(1)}, u32[]{:S(2)}, u32[]{:S(2)}) collective-permute-start(f32[4,64,512]{2,1,0:T(8,128)S(1)} %get-tuple-element.22), channel_id=1, source_target_pairs={{0,2},{1,3},{2,0},{3,1},{4,6},{5,7},{6,4},{7,5},{8,10},{9,11},{10,... | collective-permute-start | bytes 1572872 | tf_op jit(solution)/shard_map/ppermute | solution.py:511
  9.7 26.2 %collective-permute-start.2 = (f32[4,64,512]{2,1,0:T(8,128)S(1)}, f32[4,64,512]{2,1,0:T(8,128)S(1)}, u32[]{:S(2)}, u32[]{:S(2)}) collective-permute-start(f32[4,64,512]{2,1,0:T(8,128)S(1)} %get-tuple-element.23), channel_id=1, source_target_pairs={{0,1},{1,2},{2,3},{3,0},{4,5},{5,6},{6,7},{7,4},{8,9},{9,10},{10,1... | collective-permute-start | bytes 1572872 | tf_op jit(solution)/shard_map/ppermute | solution.py:511
  38.3 35.7 %collective-permute-start.3 = (f32[4,64,512]{2,1,0:T(8,128)S(1)}, f32[4,64,512]{2,1,0:T(8,128)S(1)}, u32[]{:S(2)}, u32[]{:S(2)}) collective-permute-start(f32[4,64,512]{2,1,0:T(8,128)S(1)} %get-tuple-element.30), channel_id=1, source_target_pairs={{0,1},{1,2},{2,3},{3,0},{4,5},{5,6},{6,7},{7,4},{8,9},{9,10},{10,1... | collective-permute-start | bytes 1572872 | tf_op jit(solution)/shard_map/ppermute | solution.py:511
  38.4 35.7 %collective-permute-start.4 = (f32[4,64,512]{2,1,0:T(8,128)S(1)}, f32[4,64,512]{2,1,0:T(8,128)S(1)}, u32[]{:S(2)}, u32[]{:S(2)}) collective-permute-start(f32[4,64,512]{2,1,0:T(8,128)S(1)} %get-tuple-element.31), channel_id=1, source_target_pairs={{0,2},{1,3},{2,0},{3,1},{4,6},{5,7},{6,4},{7,5},{8,10},{9,11},{10,... | collective-permute-start | bytes 1572872 | tf_op jit(solution)/shard_map/ppermute | solution.py:511
  38.9 35.2 %collective-permute-start.5 = (f32[4,64,512]{2,1,0:T(8,128)S(1)}, f32[4,64,512]{2,1,0:T(8,128)S(1)}, u32[]{:S(2)}, u32[]{:S(2)}) collective-permute-start(f32[4,64,512]{2,1,0:T(8,128)S(1)} %get-tuple-element.32), channel_id=1, source_target_pairs={{0,3},{1,0},{2,1},{3,2},{4,7},{5,4},{6,5},{7,6},{8,11},{9,8},{10,9... | collective-permute-start | bytes 1572872 | tf_op jit(solution)/shard_map/ppermute | solution.py:511

commit v6 on v5

--- a/solution.py
+++ b/solution.py
@@ -1,3 +1,4 @@
+import functools
 import math
 
 import jax
@@ -8,6 +9,7 @@
 from jax.experimental import pallas as pl
 from jax.experimental.pallas import tpu as pltpu
 from jax.sharding import PartitionSpec as P
+
 
 F32 = jnp.float32
 BF16 = jnp.bfloat16
@@ -143,49 +145,47 @@
 
 
 def forward_x_kernel(
-    src, solid, spread, twiddle, fh, fl, eh, el, out0, out1, out2, out3, hi, lo, hi0, lo0
+    src, solid, spread, twiddle, fh, fl, eh, el,
+    out0, out1, out2, out3, out4, out5, out6, out7, hi, lo, hi0, lo0,
 ):
     lev = lax.axis_index("lev")
-    band = pl.ds(pl.multiple_of(pl.program_id(0) * YB, YB), YB)
     levels = src.shape[1]
     rows = levels * YB
+    band = pl.ds(pl.multiple_of(pl.program_id(0) * rows, rows), rows)
     open_cells = (1 - solid[...]).astype(F32).astype(BF16)
-    masks = mm(open_cells.reshape(solid.shape[0] * levels, solid.shape[2]), spread[...])
-    for z in range(levels):
+    twice = [open_cells[i] for i in range(YB // BY) for _ in range(2)]
+    masks = mm(jnp.concatenate(twice, 0), spread[...])
+    for part in range(levels):
+        near = slice(4 * part, 4 * part + 4)
+        mask_at = 8 * (part // 2)
         cells = []
         for a in range(16):
-            piece = src[:, z, a * LANES : (a + 1) * LANES]
-            mask = masks[:, a * LANES : (a + 1) * LANES]
-            pieces = [
-                piece[8 * i : 8 * i + 8] * mask[i * levels + z : i * levels + z + 1]
-                for i in range(YB // 8)
-            ]
-            cells.append(jnp.concatenate(pieces, 0))
+            cols = slice(a * LANES, (a + 1) * LANES)
+            piece = src[near, :, cols].reshape(2, 8, LANES)
+            cells.append((piece * masks[None, mask_at : mask_at + 8, cols]).reshape(16, LANES))
         real, comps = real16(cells)
-        for part in range(2):
-            high, low = halves(real[part])
-            hi0[z * YB : (z + 1) * YB, part * LANES : (part + 1) * LANES] = high
-            lo0[z * YB : (z + 1) * YB, part * LANES : (part + 1) * LANES] = low
+        for half in range(2):
+            high, low = halves(real[half])
+            hi0[part * 16 : part * 16 + 16, half * LANES : (half + 1) * LANES] = high
+            lo0[part * 16 : part * 16 + 16, half * LANES : (half + 1) * LANES] = low
         for i in range(1, 8):
             block = cmul(comps[i - 1], twiddle[i - 1 : i, :], twiddle[7 + i : 8 + i, :])
             slot = 2 * ((lev - i // 2) & 3) + i % 2
-            place = pl.multiple_of(slot * rows + z * YB, YB)
-            for part in range(2):
-                high, low = halves(block[part])
-                hi[pl.ds(place, YB), part * LANES : (part + 1) * LANES] = high
-                lo[pl.ds(place, YB), part * LANES : (part + 1) * LANES] = low
-    outs = (out0, out1, out2, out3)
+            place = pl.multiple_of(slot * rows + part * 16, 16)
+            for half in range(2):
+                high, low = halves(block[half])
+                hi[pl.ds(place, 16), half * LANES : (half + 1) * LANES] = high
+                lo[pl.ds(place, 16), half * LANES : (half + 1) * LANES] = low
+    outs = (out0, out1, out2, out3, out4, out5, out6, out7)
     rest = mm3((hi[...], lo[...]), (fh[...], fl[...]))
-    for step in range(4):
-        for h in range(2):
-            value = rest[(2 * step + h) * rows : (2 * step + h + 1) * rows]
-            outs[step][:, band, h * 256 : h * 256 + 256] = value.reshape(levels, YB, 256)
-    first = mm3((hi0[...], lo0[...]), (eh[...], el[...])).reshape(levels, YB, 256)
+    for slot in range(8):
+        outs[slot][band, :] = rest[slot * rows : (slot + 1) * rows]
+    first = mm3((hi0[...], lo0[...]), (eh[...], el[...]))
     for step in range(4):
 
         @pl.when(lev == step)
         def _(step=step):
-            outs[step][:, band, 0:256] = first
+            outs[2 * step][band, :] = first
 
 
 def forward_x(source, solid, consts):
@@ -198,8 +198,8 @@
             pl.BlockSpec((YB // BY, levels, cells // BX), lambda i: (i, 0, 0)),
         ]
         + [pl.BlockSpec(value.shape, lambda i: (0, 0)) for value in consts],
-        out_specs=[VMEM] * 4,
-        out_shape=[jax.ShapeDtypeStruct((levels, rows, 512), F32)] * 4,
+        out_specs=[VMEM] * 8,
+        out_shape=[jax.ShapeDtypeStruct((rows * levels, 256), F32)] * 8,
         scratch_shapes=[pltpu.VMEM((8 * levels * YB, 256), BF16)] * 2
         + [pltpu.VMEM((levels * YB, 256), BF16)] * 2,
         compiler_params=grant(12),
@@ -290,9 +290,14 @@
     col = lax.broadcasted_iota(jnp.int32, (LANES, LANES), 1)
     for section in range(4):
         order = [wide[(z + 4 * section) % NZ] for z in range(NZ)]
+        group = []
+        for s in range(4):
+            at = (4 * section + 4 * s) % NZ
+            group += [vectors[at : at + 4]] * 8
         w4 = jnp.where(row % 8 == col // NZ, jnp.concatenate(order, 0), 0.0)
         w4h[section], w4l[section] = halves(w4)
-        w2h[section], w2l[section] = halves(w4.T)
+        w2t = jnp.where(row % 32 // 4 == col // NZ, jnp.concatenate(group, 0), 0.0)
+        w2h[section], w2l[section] = halves(w2t.T)
 
 
 def eigen(couplings):
@@ -322,7 +327,7 @@
 
 
 def inverse_x_kernel(
-    spec0, spec1, spec2, spec3, ends, modes, lam, eig, twiddle, fh, fl, eh, el,
+    spec0, spec1, spec2, spec3, spec4, spec5, spec6, spec7, ends, modes, lam, eig, twiddle, fh, fl, eh, el,
     out, hi, lo, above, below, eighth, steps, shelf,
 ):
     levels = spec0.shape[0]
@@ -362,10 +367,11 @@
         steps[o] = powers(r8, 2 * i + o)
         steps[2 + o] = powers(r8, blocks - 1 - 2 * i - o)
     first_level = lev * levels
-    for step, spec in enumerate((spec0, spec1, spec2, spec3)):
-        l = (lev - step) & 3
-        for part in range(4):
-            t = 4 * l + part
+    specs = (spec0, spec1, spec2, spec3, spec4, spec5, spec6, spec7)
+    for slot, spec in enumerate(specs):
+        block = 2 * ((lev - slot // 2) & 3) + slot % 2
+        for part in range(2):
+            t = 2 * block + part
             acc = [[None, None] for _ in range(levels)]
             for k in range(NZ):
                 u, d = above[t, k], below[t, k]
@@ -377,8 +383,8 @@
             for z in range(levels):
                 value = spec[z, band, part * LANES : (part + 1) * LANES] + jnp.concatenate(acc[z], 0)
                 high, low = halves(value)
-                place = pl.multiple_of((2 * l + part // 2) * rows + z * YB, YB)
-                half = pl.ds((part % 2) * LANES, LANES)
+                place = pl.multiple_of(block * rows + z * YB, YB)
+                half = pl.ds(part * LANES, LANES)
                 hi[pl.ds(place, YB), half] = high
                 lo[pl.ds(place, YB), half] = low
     first = mm3((hi[:rows, :], lo[:rows, :]), (eh[...], el[...]))
@@ -400,7 +406,7 @@
     return pl.pallas_call(
         inverse_x_kernel,
         grid=(rows // YB,),
-        in_specs=[VMEM] * 5 + [pl.BlockSpec(memory_space=pltpu.SMEM)] + [VMEM] * 7,
+        in_specs=[VMEM] * 9 + [pl.BlockSpec(memory_space=pltpu.SMEM)] + [VMEM] * 7,
         out_specs=pl.BlockSpec((YB, levels, N), lambda i: (i, 0, 0)),
         out_shape=jax.ShapeDtypeStruct((rows, levels, N), F32),
         scratch_shapes=[pltpu.VMEM((8 * levels * YB, 256), BF16)] * 2
@@ -412,54 +418,54 @@
     )(*specs, ends, modes, lam, eig, *consts)
 
 
-def level_kernel(
-    x0, x1, x2, x3, w2h, w2l, w4h, w4l, lam, eig, out0, out1, out2, out3, ends, f, work
-):
+def level_kernel(h, x0, x1, x2, x3, w2h, w2l, w4h, w4l, lam, eig, *refs):
+    before = refs[:h]
+    out0, out1, out2, out3, ends, f, work = refs[h:]
     lev = lax.axis_index("lev")
-    rows = x0.shape[1]
+    rows = x0.shape[0] // 4
     w2 = (w2h[lev], w2l[lev])
     w4 = (w4h[lev], w4l[lev])
-    for h in range(x0.shape[2] // 256):
-        cols = pl.ds(h * 256, 256)
-        e = eig[pl.ds(lev * 2 + h, 1), :]
-        r, gain = decay(lam[:, 0:1], e)
-        for o in range(rows // 8):
-            block = [x[:, 8 * o : 8 * o + 8, cols].reshape(32, 256) for x in (x0, x1, x2, x3)]
-            value = mm3(w2, halves(jnp.concatenate(block, 0)))
-            f[8 * o : 8 * o + 8] = value.reshape(8, NZ, 256)
-        up = jnp.zeros((NZ, 256), F32)
-        down = jnp.zeros((NZ, 256), F32)
-        for y in range(rows):
-            up = r * up
-            work[y] = up
-            up = up + f[y]
-        for y in reversed(range(rows)):
-            down = f[y] + r * down
-            work[y] = (work[y] + down) * gain
-        place = pl.ds(h * NZ, NZ)
-        ends[place, 0, :] = up[:, :LANES]
-        ends[place, 1, :] = up[:, LANES:]
-        ends[place, 2, :] = down[:, :LANES]
-        ends[place, 3, :] = down[:, LANES:]
-        for o in range(rows // 8):
-            block = work[8 * o : 8 * o + 8].reshape(LANES, 256)
-            value = mm3(w4, halves(block))
-            for step, out in enumerate((out0, out1, out2, out3)):
-                out[:, 8 * o : 8 * o + 8, cols] = value[32 * step : 32 * step + 32].reshape(4, 8, 256)
-
-
-def level_solve(xs, weights, lam, eig):
-    _, rows, width = xs[0].shape
+    e = eig[pl.ds(lev * 2 + h, 1), :]
+    r, gain = decay(lam[:, 0:1], e)
+    for o in range(rows // 8):
+        block = [x[32 * o : 32 * o + 32, :] for x in (x0, x1, x2, x3)]
+        value = mm3(w2, halves(jnp.concatenate(block, 0)))
+        f[8 * o : 8 * o + 8] = value.reshape(8, NZ, 256)
+    up = jnp.zeros((NZ, 256), F32)
+    down = jnp.zeros((NZ, 256), F32)
+    for y in range(rows):
+        up = r * up
+        work[y] = up
+        up = up + f[y]
+    for y in reversed(range(rows)):
+        down = f[y] + r * down
+        work[y] = (work[y] + down) * gain
+    for value in before:
+        ends[:NZ] = value[...]
+    place = pl.ds(h * NZ, NZ)
+    ends[place, 0, :] = up[:, :LANES]
+    ends[place, 1, :] = up[:, LANES:]
+    ends[place, 2, :] = down[:, :LANES]
+    ends[place, 3, :] = down[:, LANES:]
+    for o in range(rows // 8):
+        block = work[8 * o : 8 * o + 8].reshape(LANES, 256)
+        value = mm3(w4, halves(block))
+        for step, out in enumerate((out0, out1, out2, out3)):
+            out[:, 8 * o : 8 * o + 8, :] = value[32 * step : 32 * step + 32].reshape(4, 8, 256)
+
+
+def level_solve(h, xs, weights, lam, eig, before):
+    pairs, width = xs[0].shape
+    rows = pairs // 4
     return pl.pallas_call(
-        level_kernel,
-        in_specs=[VMEM] * 10,
+        functools.partial(level_kernel, h),
+        in_specs=[VMEM] * (10 + h),
         out_specs=[VMEM] * 5,
         out_shape=[jax.ShapeDtypeStruct((4, rows, width), F32)] * 4
-        + [jax.ShapeDtypeStruct((2 * NZ, 4, LANES), F32)],
-        scratch_shapes=[pltpu.VMEM((rows, NZ, 256), F32)] * 2,
+        + [jax.ShapeDtypeStruct(((h + 1) * NZ, 4, LANES), F32)],
+        scratch_shapes=[pltpu.VMEM((rows, NZ, width), F32)] * 2,
         compiler_params=grant(12),
-        name="level_solve",
-    )(*xs, *weights, lam, eig)
+    )(*xs, *weights, lam, eig, *before)
 
 
 def carry_kernel(ends, lam, eig, out):
@@ -519,9 +525,16 @@
     eth, etl = split_host(edge.T)
     lam, modes, w2h, w2l, w4h, w4l = eigen(couplings)
     parts = forward_x(source, solid, (spread, twiddle, fh, fl, eh, el))
-    xs = [parts[0]] + [shift(parts[step], -step) for step in (1, 2, 3)]
-    *parts, ends = level_solve(xs, (w2h, w2l, w4h, w4l), lam, eig)
-    specs = [parts[0]] + [shift(parts[step], step) for step in (1, 2, 3)]
+    weights = (w2h, w2l, w4h, w4l)
+    xs = [[parts[h]] + [shift(parts[2 * step + h], -step) for step in (1, 2, 3)] for h in range(2)]
+    *parts0, ends0 = level_solve(0, xs[0], weights, lam, eig, ())
+    *parts1, ends = level_solve(1, xs[1], weights, lam, eig, (ends0,))
+    sent = [parts0[0]]
+    for step in (1, 2, 3):
+        sent.append(shift(parts0[step], step))
+    specs = [sent[0], parts1[0]]
+    for step in (1, 2, 3):
+        specs += [sent[step], shift(parts1[step], step)]
     ends = lax.all_to_all(ends, "rows", 0, 0, tiled=True)
     ends = carries(ends, lam, eig).reshape(128, 4, LANES)
     ends = lax.all_to_all(ends, ("rows", "lev"), 0, 0, tiled=True).reshape(2, NZ, 4, 4, LANES)

time: 84.1 us -> 88.9 us (1.057)
  blocking collectives: 32.7 us -> 0 us
  starting transfers between devices: 7.4 us -> 34.5 us
  waiting for transfers between devices: 15.6 us -> 23.3 us
  Pallas kernels: 28 us -> 29.8 us
    all_to_all x2 -> x0, blocking collectives: 32.7 us -> none  [the longest x1 16.6 us: body(): lax.all_to_all(ends, ('rows', 'lev'), 0, 0, tiled=True)]
    all_to_all x0 -> x2, starting transfers between devices: none -> 18.9 us  [the longest x1 10.3 us: body(): lax.all_to_all(ends, ('rows', 'lev'), 0, 0, tiled=True)]
    ppermute x6 -> x12, starting transfers between devices: 7.4 us -> 15.6 us  [shift(): return lax.ppermute(value, 'lev', [(i, (i + step) % 4) for i in range(4)])]
    ppermute x6 -> x12, waiting for transfers between devices: 15.6 us -> 19.8 us  [shift(): return lax.ppermute(value, 'lev', [(i, (i + step) % 4) for i in range(4)])]
    all_to_all x0 -> x2, waiting for transfers between devices: none -> 3.48 us  [the longest x1 3.47 us: body(): lax.all_to_all(ends, ('rows', 'lev'), 0, 0, tiled=True)]
    pallas_call x2 -> x3, Pallas kernels: 12.1 us -> 13.4 us  [the longest x1 9.94 us: inverse_x(): pl.pallas_call(inverse_x_kernel, grid=(rows // YB,), in_specs=[VMEM] * 9...]
  transfers between devices with their start and end apart: 6 -> 14, of which waited for: 2 -> 6; matrix products, arithmetic and copies ran while one was open for 0% -> 0% of each run, Pallas kernels for 12% -> 16%
where the time goes in v6:
time: 88.9 us; the launch traced here: 87.8 us
  starting transfers between devices  34.5 us (39%)
  Pallas kernels  29.8 us (34%)
  waiting for transfers between devices  23.3 us (26%)
    ppermute x12, waiting for transfers between devices, shift(): return lax.ppermute(value, 'lev', [(i, (i + step) % 4) for i in range(4)])  19.8 us
    ppermute x12, starting transfers between devices, shift(): return lax.ppermute(value, 'lev', [(i, (i + step) % 4) for i in range(4)])  15.6 us
    all_to_all x1, starting transfers between devices, body(): lax.all_to_all(ends, ('rows', 'lev'), 0, 0, tiled=True)  10.3 us
    pallas_call x1, Pallas kernels, eigen(): pl.pallas_call(eigen_kernel, in_specs=[pl.BlockSpec(memory_space=pltpu.SM...  9.99 us
    pallas_call x1, Pallas kernels, inverse_x(): pl.pallas_call(inverse_x_kernel, grid=(rows // YB,), in_specs=[VMEM] * 9...  9.94 us
    all_to_all x1, starting transfers between devices, body(): ends = lax.all_to_all(ends, 'rows', 0, 0, tiled=True)  8.61 us
    pallas_call x1, Pallas kernels, forward_x(): pl.pallas_call(forward_x_kernel, grid=(rows // YB,), in_specs=[pl.BlockSp...  5.52 us
    all_to_all x1, waiting for transfers between devices, body(): lax.all_to_all(ends, ('rows', 'lev'), 0, 0, tiled=True)  3.47 us
  transfers between devices with their start and end apart: 14, of which 6 were waited for; matrix products, arithmetic and copies ran while one was open for 0% of the time, Pallas kernels for 16%

profile of v6, /device:TPU:1, one launch (start us, length us, event | category | flops | bytes accessed | tf_op | source)
XLA Modules:
  0.0 87.8 jit_solution(16513482135063355895)
XLA Ops:
  0.0 5.5 %forward_x.1 = (f32[256,256]{1,0:T(8,128)S(1)}, f32[256,256]{1,0:T(8,128)S(1)}, f32[256,256]{1,0:T(8,128)S(1)}, f32[256,256]{1,0:T(8,128)S(1)}, f32[256,256]{1,0...) custom-call(f32[64,4,2048]{2,1,0:T(4,128)} %src.1, s32[8,4,32]{2,1,0:T(4,128)} %solid.1, ...), custom_call_target="tpu_custom_call" | custom-call | tf_op jit(solution)/shard_map/forward_x/pallas_call | solution.py:193
  5.5 3.6 %collective-permute-start = (f32[256,256]{1,0:T(8,128)S(1)}, f32[256,256]{1,0:T(8,128)S(1)}, u32[]{:S(2)}, u32[]{:S(2)}) collective-permute-start(f32[256,256]{1,0:T(8,128)S(1)} %get-tuple-element.30), channel_id=1, source_target_pairs={{0,3},{1,0},{2,1},{3,2},{4,7},{5,4},{6,5},{7,6},{8,11},{9,8},{10,9... | collective-permute-start | bytes 786440 | tf_op jit(solution)/shard_map/ppermute | solution.py:517
  9.1 0.4 collective-permute-start.1
  9.5 0.7 collective-permute-start.2
  10.2 2.0 %collective-permute-start.3 = (f32[256,256]{1,0:T(8,128)S(1)}, f32[256,256]{1,0:T(8,128)S(1)}, u32[]{:S(2)}, u32[]{:S(2)}) collective-permute-start(f32[256,256]{1,0:T(8,128)S(1)} %get-tuple-element.40), channel_id=1, source_target_pairs={{0,3},{1,0},{2,1},{3,2},{4,7},{5,4},{6,5},{7,6},{8,11},{9,8},{10,9... | collective-permute-start | bytes 786440 | tf_op jit(solution)/shard_map/ppermute | solution.py:517
  12.2 1.4 %collective-permute-start.4 = (f32[256,256]{1,0:T(8,128)S(1)}, f32[256,256]{1,0:T(8,128)S(1)}, u32[]{:S(2)}, u32[]{:S(2)}) collective-permute-start(f32[256,256]{1,0:T(8,128)S(1)} %get-tuple-element.41), channel_id=1, source_target_pairs={{0,2},{1,3},{2,0},{3,1},{4,6},{5,7},{6,4},{7,5},{8,10},{9,11},{10,... | collective-permute-start | bytes 786440 | tf_op jit(solution)/shard_map/ppermute | solution.py:517
  13.6 5.0 %collective-permute-done.x1 = f32[256,256]{1,0:T(8,128)S(1)} collective-permute-done((f32[256,256]{1,0:T(8,128)S(1)}, f32[256,256]{1,0:T(8,128)S(1)}, u32[]{:S(2)}, u32[]{:S(2)}) %collective-permute-start) | collective-permute-done | bytes 262176 | tf_op jit(solution)/shard_map/ppermute | solution.py:517
  18.6 0.0 collective-permute-start.5
  18.6 10.0 %level_modes.1 = (f32[16,128]{1,0:T(8,128)S(1)}, f32[16,128]{1,0:T(8,128)S(1)}, bf16[4,128,128]{2,1,0:T(8,128)(2,1)S(1)}, bf16[4,128,128]{2,1,0:T(8,128)(2,1)S(1...) custom-call(f32[17]{0:T(128)S(1)} %copy-done.6), custom_call_target="tpu_custom_call" | custom-call | tf_op jit(solution)/shard_map/level_modes/pallas_call | solution.py:306
  28.6 0.0 collective-permute-done.1.x2
  28.6 0.0 collective-permute-done.2.x3
  28.6 0.0 copy-start.1
  28.6 0.0 copy-start.2
  28.6 0.0 copy-start.3
  28.7 0.0 copy-start.4
  28.7 0.0 copy-start.5
  28.7 1.3 %shard_map.136 = (f32[4,64,256]{2,1,0:T(8,128)S(1)}, f32[4,64,256]{2,1,0:T(8,128)S(1)}, f32[4,64,256]{2,1,0:T(8,128)S(1)}, f32[4,64,256]{2,1,0:T(8,128)S(1)}, f32[16,4,128]{2,1,0:T(4,128)S(1)}) custom-call(f32[256,256]{1,0:T(8,128)S(1)} %get-tuple-element.29.x0, f32[256,256]{1,0:T(8,128)S(1)} %collective-permute-done.x1, ...), custom_call_target="tpu_custom_call" | custom-call | tf_op jit(solution)/shard_map/pallas_call | solution.py:460
  30.0 0.1 collective-permute-start.6
  30.1 0.8 collective-permute-done.3.x1
  30.8 4.8 %collective-permute-done.5.x3 = f32[256,256]{1,0:T(8,128)S(1)} collective-permute-done((f32[256,256]{1,0:T(8,128)S(1)}, f32[256,256]{1,0:T(8,128)S(1)}, u32[]{:S(2)}, u32[]{:S(2)}) %collective-permute-start.5) | collective-permute-done | bytes 262176 | tf_op jit(solution)/shard_map/ppermute | solution.py:517
  35.7 2.1 %shard_map.137 = (f32[4,64,256]{2,1,0:T(8,128)S(1)}, f32[4,64,256]{2,1,0:T(8,128)}, f32[4,64,256]{2,1,0:T(8,128)}, f32[4,64,256]{2,1,0:T(8,128)}, f32[32,4,128]{2,1,0:T(4,128)}) custom-call(f32[256,256]{1,0:T(8,128)S(1)} %get-tuple-element.39.x0, f32[256,256]{1,0:T(8,128)S(1)} %collective-permute-done.3.x1, f32[256,256]{1,0:T(8,128)S(1)} %collective-permute-done.4.x2, ...), custom_call_target="tpu_custom_call" | custom-call | tf_op jit(solution)/shard_map/pallas_call | solution.py:460
  37.8 8.6 %all-to-all-start = ((f32[32,4,128]{2,1,0:T(4,128)}), f32[32,4,128]{2,1,0:T(4,128)S(1)}, u32[]{:S(2)}, u32[]{:S(2)}) async-start(f32[32,4,128]{2,1,0:T(4,128)} %get-tuple-element.51), calls=%async_computation | async-start | bytes 131072 | tf_op jit(solution)/shard_map/all_to_all | solution.py:538
  46.5 2.5 %collective-permute-start.8 = (f32[4,64,256]{2,1,0:T(8,128)S(1)}, f32[4,64,256]{2,1,0:T(8,128)S(1)}, u32[]{:S(2)}, u32[]{:S(2)}) collective-permute-start(f32[4,64,256]{2,1,0:T(8,128)S(1)} %get-tuple-element.47), channel_id=1, source_target_pairs={{0,2},{1,3},{2,0},{3,1},{4,6},{5,7},{6,4},{7,5},{8,10},{9,11},{10,... | collective-permute-start | bytes 786440 | tf_op jit(solution)/shard_map/ppermute | solution.py:517
  49.0 2.3 %collective-permute-start.10 = (f32[4,64,256]{2,1,0:T(8,128)S(1)}, f32[4,64,256]{2,1,0:T(8,128)S(1)}, u32[]{:S(2)}, u32[]{:S(2)}) collective-permute-start(f32[4,64,256]{2,1,0:T(8,128)S(1)} %get-tuple-element.49), channel_id=1, source_target_pairs={{0,3},{1,0},{2,1},{3,2},{4,7},{5,4},{6,5},{7,6},{8,11},{9,8},{10,9... | collective-permute-start | bytes 786440 | tf_op jit(solution)/shard_map/ppermute | solution.py:517
  51.3 1.2 %collective-permute-start.9 = (f32[4,64,256]{2,1,0:T(8,128)}, f32[4,64,256]{2,1,0:T(8,128)S(1)}, u32[]{:S(2)}, u32[]{:S(2)}) collective-permute-start(f32[4,64,256]{2,1,0:T(8,128)} %get-tuple-element.48), channel_id=1, source_target_pairs={{0,2},{1,3},{2,0},{3,1},{4,6},{5,7},{6,4},{7,5},{8,10},{9,11},{10,... | collective-permute-start | bytes 786440 | tf_op jit(solution)/shard_map/ppermute | solution.py:517
  52.5 1.5 %collective-permute-start.11 = (f32[4,64,256]{2,1,0:T(8,128)}, f32[4,64,256]{2,1,0:T(8,128)S(1)}, u32[]{:S(2)}, u32[]{:S(2)}) collective-permute-start(f32[4,64,256]{2,1,0:T(8,128)} %get-tuple-element.50), channel_id=1, source_target_pairs={{0,3},{1,0},{2,1},{3,2},{4,7},{5,4},{6,5},{7,6},{8,11},{9,8},{10,9... | collective-permute-start | bytes 786440 | tf_op jit(solution)/shard_map/ppermute | solution.py:517
  54.0 0.9 %section_carries.1 = f32[32,4,4,128]{3,2,1,0:T(4,128)} custom-call(f32[32,4,128]{2,1,0:T(4,128)S(1)} %all-to-all-done.ends, f32[16,128]{1,0:T(8,128)S(1)} %get-tuple-element.37.lam, f32[8,256]{1,0:T(8,128)S(1)} %copy-done), custom_call_target="tpu_custom_call" | custom-call | tf_op jit(solution)/shard_map/section_carries/pallas_call | solution.py:506
  54.9 10.3 %all-to-all-start.1 = ((f32[128,4,128]{2,1,0:T(4,128)}), f32[128,4,128]{2,1,0:T(4,128)S(1)}, u32[]{:S(2)}, u32[]{:S(2)}) async-start(f32[128,4,128]{2,1,0:T(4,128)} %bitcast), calls=%async_computation.1 | async-start | bytes 524288 | tf_op jit(solution)/shard_map/all_to_all | solution.py:540
  65.2 1.7 %collective-permute-done.9.spec5 = f32[4,64,256]{2,1,0:T(8,128)S(1)} collective-permute-done((f32[4,64,256]{2,1,0:T(8,128)}, f32[4,64,256]{2,1,0:T(8,128)S(1)}, u32[]{:S(2)}, u32[]{:S(2)}) %collective-permute-start.9) | collective-permute-done | bytes 262176 | tf_op jit(solution)/shard_map/ppermute | solution.py:517
  66.9 7.5 %collective-permute-done.11.spec7 = f32[4,64,256]{2,1,0:T(8,128)S(1)} collective-permute-done((f32[4,64,256]{2,1,0:T(8,128)}, f32[4,64,256]{2,1,0:T(8,128)S(1)}, u32[]{:S(2)}, u32[]{:S(2)}) %collective-permute-start.11) | collective-permute-done | bytes 262176 | tf_op jit(solution)/shard_map/ppermute | solution.py:517
  74.4 3.5 %all-to-all-done.1 = f32[128,4,128]{2,1,0:T(4,128)S(1)} async-done(((f32[128,4,128]{2,1,0:T(4,128)}), f32[128,4,128]{2,1,0:T(4,128)S(1)}, u32[]{:S(2)}, u32[]{:S(2)}) %all-to-all-start.1) | async-done | bytes 262176 | tf_op jit(solution)/shard_map/all_to_all | solution.py:540
  77.9 9.9 %inverse_x.1 = f32[64,4,2048]{2,1,0:T(4,128)} custom-call(f32[4,64,256]{2,1,0:T(8,128)S(1)} %get-tuple-element.38.spec0, f32[4,64,256]{2,1,0:T(8,128)S(1)} %get-tuple-element.44.spec1, f32[4,64,256]{2,1,0:T(8,128)S(1)} %collective-permute-done.6.spec2, f32[4,64,256]{2,1,0:T(8,128)S(1)} %collective-permute-done.7.spec3, ...), custom_call_target="tpu_custom_call" | custom-call | tf_op jit(solution)/shard_map/inverse_x/pallas_call | solution.py:406
  (16 shorter events, 0.0 us)
Async XLA Ops:
  0.0 28.6 %copy-start = (f32[8,256]{1,0:T(8,128)S(1)}, f32[8,256]{1,0:T(8,128)}, u32[]{:S(2)}) copy-start(f32[8,256]{1,0:T(8,128)} %constant.28.clone.eig) | copy-start | bytes 24580
  0.0 18.6 %copy-start.6 = (f32[17]{0:T(128)S(1)}, f32[17]{0:T(128)}, u32[]{:S(2)}) copy-start(f32[17]{0:T(128)} %coup.1) | copy-start | bytes 208
  5.5 13.1 %collective-permute-start = (f32[256,256]{1,0:T(8,128)S(1)}, f32[256,256]{1,0:T(8,128)S(1)}, u32[]{:S(2)}, u32[]{:S(2)}) collective-permute-start(f32[256,256]{1,0:T(8,128)S(1)} %get-tuple-element.30), channel_id=1, source_target_pairs={{0,3},{1,0},{2,1},{3,2},{4,7},{5,4},{6,5},{7,6},{8,11},{9,8},{10,9... | collective-permute-start | bytes 786440 | tf_op jit(solution)/shard_map/ppermute | solution.py:517
  9.1 19.4 %collective-permute-start.1 = (f32[256,256]{1,0:T(8,128)S(1)}, f32[256,256]{1,0:T(8,128)S(1)}, u32[]{:S(2)}, u32[]{:S(2)}) collective-permute-start(f32[256,256]{1,0:T(8,128)S(1)} %get-tuple-element.31), channel_id=1, source_target_pairs={{0,2},{1,3},{2,0},{3,1},{4,6},{5,7},{6,4},{7,5},{8,10},{9,11},{10,... | collective-permute-start | bytes 786440 | tf_op jit(solution)/shard_map/ppermute | solution.py:517
  9.5 19.1 %collective-permute-start.2 = (f32[256,256]{1,0:T(8,128)S(1)}, f32[256,256]{1,0:T(8,128)S(1)}, u32[]{:S(2)}, u32[]{:S(2)}) collective-permute-start(f32[256,256]{1,0:T(8,128)S(1)} %get-tuple-element.32), channel_id=1, source_target_pairs={{0,1},{1,2},{2,3},{3,0},{4,5},{5,6},{6,7},{7,4},{8,9},{9,10},{10,1... | collective-permute-start | bytes 786440 | tf_op jit(solution)/shard_map/ppermute | solution.py:517
  10.2 20.6 %collective-permute-start.3 = (f32[256,256]{1,0:T(8,128)S(1)}, f32[256,256]{1,0:T(8,128)S(1)}, u32[]{:S(2)}, u32[]{:S(2)}) collective-permute-start(f32[256,256]{1,0:T(8,128)S(1)} %get-tuple-element.40), channel_id=1, source_target_pairs={{0,3},{1,0},{2,1},{3,2},{4,7},{5,4},{6,5},{7,6},{8,11},{9,8},{10,9... | collective-permute-start | bytes 786440 | tf_op jit(solution)/shard_map/ppermute | solution.py:517
  12.2 18.7 %collective-permute-start.4 = (f32[256,256]{1,0:T(8,128)S(1)}, f32[256,256]{1,0:T(8,128)S(1)}, u32[]{:S(2)}, u32[]{:S(2)}) collective-permute-start(f32[256,256]{1,0:T(8,128)S(1)} %get-tuple-element.41), channel_id=1, source_target_pairs={{0,2},{1,3},{2,0},{3,1},{4,6},{5,7},{6,4},{7,5},{8,10},{9,11},{10,... | collective-permute-start | bytes 786440 | tf_op jit(solution)/shard_map/ppermute | solution.py:517
  18.6 17.1 %collective-permute-start.5 = (f32[256,256]{1,0:T(8,128)S(1)}, f32[256,256]{1,0:T(8,128)S(1)}, u32[]{:S(2)}, u32[]{:S(2)}) collective-permute-start(f32[256,256]{1,0:T(8,128)S(1)} %get-tuple-element.42), channel_id=1, source_target_pairs={{0,1},{1,2},{2,3},{3,0},{4,5},{5,6},{6,7},{7,4},{8,9},{9,10},{10,1... | collective-permute-start | bytes 786440 | tf_op jit(solution)/shard_map/ppermute | solution.py:517
  28.6 49.2 %copy-start.1 = (bf16[256,256]{1,0:T(8,128)(2,1)S(1)}, bf16[256,256]{1,0:T(8,128)(2,1)}, u32[]{:S(2)}) copy-start(bf16[256,256]{1,0:T(8,128)(2,1)} %constant.32.clone.el) | copy-start | bytes 393220
  28.6 49.2 %copy-start.2 = (bf16[256,256]{1,0:T(8,128)(2,1)S(1)}, bf16[256,256]{1,0:T(8,128)(2,1)}, u32[]{:S(2)}) copy-start(bf16[256,256]{1,0:T(8,128)(2,1)} %constant.31.clone.eh) | copy-start | bytes 393220
  28.6 49.2 %copy-start.3 = (bf16[256,256]{1,0:T(8,128)(2,1)S(1)}, bf16[256,256]{1,0:T(8,128)(2,1)}, u32[]{:S(2)}) copy-start(bf16[256,256]{1,0:T(8,128)(2,1)} %constant.30.clone.fl) | copy-start | bytes 393220
  28.7 49.2 %copy-start.4 = (bf16[256,256]{1,0:T(8,128)(2,1)S(1)}, bf16[256,256]{1,0:T(8,128)(2,1)}, u32[]{:S(2)}) copy-start(bf16[256,256]{1,0:T(8,128)(2,1)} %constant.29.clone.fh) | copy-start | bytes 393220
  28.7 49.2 %copy-start.5 = (f32[16,128]{1,0:T(8,128)S(1)}, f32[16,128]{1,0:T(8,128)}, u32[]{:S(2)}) copy-start(f32[16,128]{1,0:T(8,128)} %constant.23.clone.twiddle) | copy-start | bytes 24580
  30.0 22.5 %collective-permute-start.6 = (f32[4,64,256]{2,1,0:T(8,128)S(1)}, f32[4,64,256]{2,1,0:T(8,128)S(1)}, u32[]{:S(2)}, u32[]{:S(2)}) collective-permute-start(f32[4,64,256]{2,1,0:T(8,128)S(1)} %get-tuple-element.45), channel_id=1, source_target_pairs={{0,1},{1,2},{2,3},{3,0},{4,5},{5,6},{6,7},{7,4},{8,9},{9,10},{10,1... | collective-permute-start | bytes 786440 | tf_op jit(solution)/shard_map/ppermute | solution.py:517
  37.8 16.1 %all-to-all-start = ((f32[32,4,128]{2,1,0:T(4,128)}), f32[32,4,128]{2,1,0:T(4,128)S(1)}, u32[]{:S(2)}, u32[]{:S(2)}) async-start(f32[32,4,128]{2,1,0:T(4,128)} %get-tuple-element.51), calls=%async_computation | async-start | bytes 131072 | tf_op jit(solution)/shard_map/all_to_all | solution.py:538
  46.5 18.8 %collective-permute-start.8 = (f32[4,64,256]{2,1,0:T(8,128)S(1)}, f32[4,64,256]{2,1,0:T(8,128)S(1)}, u32[]{:S(2)}, u32[]{:S(2)}) collective-permute-start(f32[4,64,256]{2,1,0:T(8,128)S(1)} %get-tuple-element.47), channel_id=1, source_target_pairs={{0,2},{1,3},{2,0},{3,1},{4,6},{5,7},{6,4},{7,5},{8,10},{9,11},{10,... | collective-permute-start | bytes 786440 | tf_op jit(solution)/shard_map/ppermute | solution.py:517
  49.0 16.3 %collective-permute-start.10 = (f32[4,64,256]{2,1,0:T(8,128)S(1)}, f32[4,64,256]{2,1,0:T(8,128)S(1)}, u32[]{:S(2)}, u32[]{:S(2)}) collective-permute-start(f32[4,64,256]{2,1,0:T(8,128)S(1)} %get-tuple-element.49), channel_id=1, source_target_pairs={{0,3},{1,0},{2,1},{3,2},{4,7},{5,4},{6,5},{7,6},{8,11},{9,8},{10,9... | collective-permute-start | bytes 786440 | tf_op jit(solution)/shard_map/ppermute | solution.py:517
  51.3 13.9 %collective-permute-start.7 = (f32[4,64,256]{2,1,0:T(8,128)}, f32[4,64,256]{2,1,0:T(8,128)S(1)}, u32[]{:S(2)}, u32[]{:S(2)}) collective-permute-start(f32[4,64,256]{2,1,0:T(8,128)} %get-tuple-element.46), channel_id=1, source_target_pairs={{0,1},{1,2},{2,3},{3,0},{4,5},{5,6},{6,7},{7,4},{8,9},{9,10},{10,1... | collective-permute-start | bytes 786440 | tf_op jit(solution)/shard_map/ppermute | solution.py:517
  51.3 15.6 %collective-permute-start.9 = (f32[4,64,256]{2,1,0:T(8,128)}, f32[4,64,256]{2,1,0:T(8,128)S(1)}, u32[]{:S(2)}, u32[]{:S(2)}) collective-permute-start(f32[4,64,256]{2,1,0:T(8,128)} %get-tuple-element.48), channel_id=1, source_target_pairs={{0,2},{1,3},{2,0},{3,1},{4,6},{5,7},{6,4},{7,5},{8,10},{9,11},{10,... | collective-permute-start | bytes 786440 | tf_op jit(solution)/shard_map/ppermute | solution.py:517
  52.5 21.9 %collective-permute-start.11 = (f32[4,64,256]{2,1,0:T(8,128)}, f32[4,64,256]{2,1,0:T(8,128)S(1)}, u32[]{:S(2)}, u32[]{:S(2)}) collective-permute-start(f32[4,64,256]{2,1,0:T(8,128)} %get-tuple-element.50), channel_id=1, source_target_pairs={{0,3},{1,0},{2,1},{3,2},{4,7},{5,4},{6,5},{7,6},{8,11},{9,8},{10,9... | collective-permute-start | bytes 786440 | tf_op jit(solution)/shard_map/ppermute | solution.py:517
  54.9 23.0 %all-to-all-start.1 = ((f32[128,4,128]{2,1,0:T(4,128)}), f32[128,4,128]{2,1,0:T(4,128)S(1)}, u32[]{:S(2)}, u32[]{:S(2)}) async-start(f32[128,4,128]{2,1,0:T(4,128)} %bitcast), calls=%async_computation.1 | async-start | bytes 524288 | tf_op jit(solution)/shard_map/all_to_all | solution.py:540
